TPU v7x, 32 devices: a whole 2x2x4 slice. The times are simulated.
32 devices in a mesh: shard: 4 (over y, x), ctx: 2 (over core), tp: 4 (over z).
Axes of the slice: x: 2, y: 2, z: 4, core: 2. Of those that a mesh axis runs over, the one named last changes fastest.
Arguments:
- tokens: bfloat16 [4, 1024, 1536], P('shard', ('ctx', 'tp')), may hold values from -6 to 6
- cotangent: bfloat16 [4, 1024, 1536], P('shard', ('ctx', 'tp')), may hold values from -6 to 6
- lengths: int32 [4], P('shard'), may hold values from 256 to 1024, as said below
- w_qkv: bfloat16 [1536, 3, 1536], P(('shard', 'ctx'), None, 'tp'), may hold values from -0.15625 to 0.15625
- w_forget: bfloat16 [1536, 24], P(('shard', 'ctx'), 'tp'), may hold values from -0.15625 to 0.15625
- forget_bias: float32 [24], replicated, may hold values from 3 to 8
- w_ogate: bfloat16 [1536, 1536], P(('shard', 'ctx'), 'tp'), may hold values from -0.15625 to 0.15625
- w_out: bfloat16 [1536, 1536], P(('shard', 'ctx'), 'tp'), may hold values from -0.625 to 0.625
- w_gu: bfloat16 [1536, 2, 4096], P(('shard', 'ctx'), None, 'tp'), may hold values from -0.15625 to 0.15625
- w_down: bfloat16 [1536, 4096], P(('shard', 'ctx'), 'tp'), may hold values from -0.09375 to 0.09375
- gain_attn: float32 [1536], replicated, may hold values from 0.5 to 1.5
- gain_mlp: float32 [1536], replicated, may hold values from 0.5 to 1.5
- qk_gain: float32 [2, 64], replicated, may hold values from 1 to 2
Outputs:
- output: bfloat16 [4, 1024, 1536], P('shard', ('ctx', 'tp'))
- input_grad: bfloat16 [4, 1024, 1536], P('shard', ('ctx', 'tp'))
- grad_qkv: float32 [1536, 3, 1536], P(('shard', 'ctx'), None, 'tp')
- grad_forget: float32 [1536, 24], P(('shard', 'ctx'), 'tp')
- grad_forget_bias: float32 [24], replicated
- grad_ogate: float32 [1536, 1536], P(('shard', 'ctx'), 'tp')
- grad_out: float32 [1536, 1536], P(('shard', 'ctx'), 'tp')
- grad_gu: float32 [1536, 2, 4096], P(('shard', 'ctx'), None, 'tp')
- grad_down: float32 [1536, 4096], P(('shard', 'ctx'), 'tp')
- grad_gain_attn: float32 [1536], replicated
- grad_gain_mlp: float32 [1536], replicated
- grad_qk_gain: float32 [2, 64], replicated
Inputs may be any that keep to these rules, and one draw needn't show every extreme that they name: `lengths`: real tokens of a slot; positions at or past it are padding; both the least and the most value occur in every draw.
All inputs are finite; a program needn't handle non-finite values.
Results may differ from a plain program's by a relative error of at most 0.04.
Values may be sent and summed in bfloat16 or wider, within the bound.
No kernel may reach another device: no remote copies, remote signals or barrier semaphores. Data moves between devices by JAX's collectives and lax.ppermute only.
A program may use at most 128 MiB of HBM per device.

v0:
```python
import math

import jax
import jax.numpy as jnp
from jax import lax
from jax.sharding import PartitionSpec as P

epsilon = 1e-06


def shifted(block, axis, distance):
    devices = range(lax.axis_size(axis))
    route = [(i - distance, i) for i in devices if i - distance in devices]
    return lax.ppermute(block, axis, route)


def norm_rows(values, gain):
    return values * lax.rsqrt(jnp.mean(values * values, axis=-1, keepdims=True) + epsilon) * gain


def product(left, right):
    return jnp.dot(left, right, preferred_element_type=jnp.float32)


def product_t(left, right):
    return lax.dot_general(
        left, right, (((1,), (1,)), ((), ())), preferred_element_type=jnp.float32
    )


def outer_rows(left, right):
    return lax.dot_general(
        left, right, (((0,), (0,)), ((), ())), preferred_element_type=jnp.float32
    )


def body(
    tokens,
    cotangent,
    lengths,
    w_qkv,
    w_forget,
    forget_bias,
    w_ogate,
    w_out,
    w_gu,
    w_down,
    gain_attn,
    gain_mlp,
    qk_gain,
):
    slot_count, own_rows, model_width = tokens.shape
    tensor_size = lax.axis_size("tp")
    tensor_place = lax.axis_index("tp")
    span_index = lax.axis_index("ctx")
    half_rows = own_rows * tensor_size
    row_count = slot_count * half_rows
    local_heads = w_forget.shape[1]
    head_size = qk_gain.shape[1]
    head_cols = local_heads * head_size
    hidden_units = w_down.shape[1]
    item_count = slot_count * local_heads
    score_scale = 1.0 / math.sqrt(head_size)
    own_start = tensor_place * own_rows
    full_tokens, full_cot = (
        lax.all_gather(tokens, "tp", axis=1, tiled=True),
        lax.all_gather(cotangent, "tp", axis=1, tiled=True),
    )
    qkv_full, forget_full, ogate_full, out_full, gu_full, down_full = (
        lax.all_gather(w_qkv, ("shard", "ctx"), axis=0, tiled=True),
        lax.all_gather(w_forget, ("shard", "ctx"), axis=0, tiled=True),
        lax.all_gather(w_ogate, ("shard", "ctx"), axis=0, tiled=True),
        lax.all_gather(w_out, ("shard", "ctx"), axis=0, tiled=True),
        lax.all_gather(w_gu, ("shard", "ctx"), axis=0, tiled=True),
        lax.all_gather(w_down, ("shard", "ctx"), axis=0, tiled=True),
    )
    qkv_flat = qkv_full.reshape(model_width, 3 * head_cols)
    gu_flat = gu_full.reshape(model_width, 2 * hidden_units)

    def own_slice(values):
        return lax.dynamic_slice_in_dim(
            values.reshape(slot_count, half_rows, values.shape[-1]), own_start, own_rows, 1
        )

    positions = span_index * half_rows + jnp.arange(half_rows, dtype=jnp.int32)
    valid_rows = (positions[None, :] < lengths[:, None]).astype(jnp.float32).reshape(row_count, 1)
    own_positions = span_index * half_rows + own_start + jnp.arange(own_rows, dtype=jnp.int32)
    valid_own = (own_positions[None, :] < lengths[:, None]).astype(jnp.float32)[:, :, None]
    residual = full_tokens.reshape(row_count, model_width).astype(jnp.float32)
    normed = norm_rows(residual, gain_attn).astype(jnp.bfloat16)
    qkv_rows = product(normed, qkv_flat).reshape(row_count, 3, head_cols)
    query_raw = qkv_rows[:, 0].reshape(row_count, local_heads, head_size)
    key_raw = qkv_rows[:, 1].reshape(row_count, local_heads, head_size)
    queries = (
        norm_rows(query_raw, qk_gain[0])
        .astype(jnp.bfloat16)
        .reshape(slot_count, half_rows, head_cols)
    )
    keys_here = (
        norm_rows(key_raw, qk_gain[1])
        .astype(jnp.bfloat16)
        .reshape(slot_count, half_rows, head_cols)
    )
    values_here = qkv_rows[:, 2].astype(jnp.bfloat16).reshape(slot_count, half_rows, head_cols)
    bias_here = lax.dynamic_slice_in_dim(forget_bias, tensor_place * local_heads, local_heads)
    forget_pre = (product(normed, forget_full) + bias_here).reshape(
        slot_count, half_rows, local_heads
    )
    cum_here = jnp.cumsum(jax.nn.log_sigmoid(forget_pre), axis=1)
    keys_left, values_left = shifted((keys_here, values_here), "ctx", 1)
    cum_left = shifted(cum_here, "ctx", 1)
    cum_query = cum_here + cum_left[:, -1:, :]

    def by_head(values):
        shaped = values.reshape(slot_count, half_rows, local_heads, head_size)
        return jnp.transpose(shaped, (0, 2, 1, 3)).reshape(item_count, half_rows, head_size)

    def by_head_cum(values):
        return jnp.transpose(values, (0, 2, 1)).reshape(item_count, half_rows)

    def to_slots(values):
        shaped = values.reshape(slot_count, local_heads, half_rows, head_size)
        return jnp.transpose(shaped, (0, 2, 1, 3)).reshape(slot_count, half_rows, head_cols)

    def to_slots_cum(values):
        return jnp.transpose(values.reshape(slot_count, local_heads, half_rows), (0, 2, 1))

    q_items = by_head(queries)
    k_items = jnp.concatenate([by_head(keys_left), by_head(keys_here)], axis=1)
    v_items = jnp.concatenate([by_head(values_left), by_head(values_here)], axis=1)
    cq_items = by_head_cum(cum_query)
    ck_items = jnp.concatenate([by_head_cum(cum_left), cq_items], axis=1)
    place_ids = jnp.arange(half_rows, dtype=jnp.int32)
    earlier = jnp.broadcast_to(span_index > 0, (half_rows, half_rows))
    allowed = jnp.concatenate([earlier, place_ids[None, :] <= place_ids[:, None]], axis=1)

    def score_block(query_block, key_block, cum_rows, cum_cols):
        score_raw = (
            product_t(query_block, key_block) * score_scale + cum_rows[:, None] - cum_cols[None, :]
        )
        return jnp.where(allowed, score_raw, -jnp.inf)

    def forward_item(pieces):
        query_block, key_block, value_block, cum_rows, cum_cols = pieces
        score_vals = score_block(query_block, key_block, cum_rows, cum_cols)
        row_max = jnp.max(score_vals, axis=1, keepdims=True)
        expo = jnp.exp(score_vals - row_max)
        row_total = jnp.sum(expo, axis=1, keepdims=True)
        attn_probs = (expo / row_total).astype(jnp.bfloat16)
        return (product(attn_probs, value_block), (row_max + jnp.log(row_total))[:, 0])

    attended_items, lse_items = lax.map(
        forward_item, (q_items, k_items, v_items, cq_items, ck_items)
    )
    attended_rows = to_slots(attended_items).reshape(row_count, head_cols)
    opener = jax.nn.sigmoid(product(normed, ogate_full))
    gated = (attended_rows * opener).astype(jnp.bfloat16)
    branch_part = product_t(gated, out_full)
    branch_full = lax.psum(branch_part, "tp")
    middle = residual + branch_full
    middle_share = own_slice(middle)
    normed_mid = norm_rows(middle, gain_mlp).astype(jnp.bfloat16)
    both = product(normed_mid, gu_flat).reshape(row_count, 2, hidden_units)
    gate_pre = both[:, 0]
    up_pre = both[:, 1]
    gate_sig = jax.nn.sigmoid(gate_pre)
    hidden = (gate_pre * gate_sig * up_pre).astype(jnp.bfloat16)
    down_share = lax.psum_scatter(
        product_t(hidden, down_full)
        .reshape(slot_count, half_rows, model_width)
        .astype(jnp.bfloat16),
        "tp",
        scatter_dimension=1,
        tiled=True,
    ).astype(jnp.float32)
    output = (valid_own * (middle_share + down_share)).astype(jnp.bfloat16)
    cot_rows = full_cot.reshape(row_count, model_width) * valid_rows.astype(jnp.bfloat16)
    d_hidden = product(cot_rows, down_full)
    d_gate = d_hidden * up_pre * gate_sig * (1.0 + gate_pre * (1.0 - gate_sig))
    d_up = d_hidden * gate_pre * gate_sig
    d_both = (
        jnp.stack([d_gate, d_up], axis=1).astype(jnp.bfloat16).reshape(row_count, 2 * hidden_units)
    )
    grad_down = outer_rows(cot_rows, hidden)
    grad_gu = outer_rows(normed_mid, d_both).reshape(model_width, 2, hidden_units)
    d_mid_terms = product_t(d_both, gu_flat)
    d_normed_mid = lax.psum(d_mid_terms, "tp")
    _, pull_mid = jax.vjp(norm_rows, middle, gain_mlp)
    d_middle_norm, d_gain_mlp_all = pull_mid(d_normed_mid)
    d_middle = d_middle_norm + cot_rows.astype(jnp.float32)
    feat_share = model_width // tensor_size
    owner = jnp.arange(model_width, dtype=jnp.int32) // feat_share == tensor_place
    d_gain_mlp_own = jnp.where(owner, d_gain_mlp_all, 0.0)
    d_branch = d_middle.astype(jnp.bfloat16)
    d_middle_share = own_slice(d_middle)
    d_gated = product(d_branch, out_full)
    grad_out = outer_rows(d_branch, gated)
    d_attended = (d_gated * opener).astype(jnp.bfloat16)
    d_open = (d_gated * attended_rows * opener * (1.0 - opener)).astype(jnp.bfloat16)
    grad_ogate = outer_rows(normed, d_open)
    da_items = by_head(d_attended.reshape(slot_count, half_rows, head_cols))

    def backward_item(pieces):
        query_block, key_block, value_block, cum_rows, cum_cols, lse_block, grad_block = pieces
        score_vals = score_block(query_block, key_block, cum_rows, cum_cols)
        attn_probs = jnp.exp(score_vals - lse_block[:, None])
        d_probs = product_t(grad_block, value_block)
        centre = jnp.sum(attn_probs * d_probs, axis=1, keepdims=True)
        d_scores = (attn_probs * (d_probs - centre)).astype(jnp.bfloat16)
        d_query_block = product(d_scores, key_block) * score_scale
        d_key_block = outer_rows(d_scores, query_block) * score_scale
        d_value_block = outer_rows(attn_probs.astype(jnp.bfloat16), grad_block)
        d_cum_rows = jnp.sum(d_scores, axis=1, dtype=jnp.float32)
        d_cum_cols = -jnp.sum(d_scores, axis=0, dtype=jnp.float32)
        return (d_query_block, d_key_block, d_value_block, d_cum_rows, d_cum_cols)

    dq_items, dk_items, dv_items, dcq_items, dck_items = lax.map(
        backward_item, (q_items, k_items, v_items, cq_items, ck_items, lse_items, da_items)
    )
    dc_own = dcq_items + dck_items[:, half_rows:]
    dc_left = dck_items[:, :half_rows]
    dc_left = dc_left.at[:, -1].add(jnp.sum(dc_own, axis=1))
    back_keys, back_values, back_cum = (
        shifted(to_slots(dk_items[:, :half_rows]).astype(jnp.bfloat16), "ctx", -1).astype(
            jnp.float32
        ),
        shifted(to_slots(dv_items[:, :half_rows]).astype(jnp.bfloat16), "ctx", -1).astype(
            jnp.float32
        ),
        shifted(to_slots_cum(dc_left).astype(jnp.bfloat16), "ctx", -1).astype(jnp.float32),
    )
    d_query = to_slots(dq_items).reshape(row_count, local_heads, head_size)
    d_key = (to_slots(dk_items[:, half_rows:]) + back_keys).reshape(
        row_count, local_heads, head_size
    )
    d_value = (to_slots(dv_items[:, half_rows:]) + back_values).reshape(row_count, head_cols)
    d_cum = to_slots_cum(dc_own) + back_cum
    d_log = jnp.flip(jnp.cumsum(jnp.flip(d_cum, 1), axis=1), 1)
    d_forget = d_log * jax.nn.sigmoid(-forget_pre)
    d_bias_own = jnp.sum(d_forget, axis=(0, 1))
    d_forget_low = d_forget.reshape(row_count, local_heads).astype(jnp.bfloat16)
    grad_forget = outer_rows(normed, d_forget_low)
    _, pull_query = jax.vjp(norm_rows, query_raw, qk_gain[0])
    d_query_raw, d_query_gain = pull_query(d_query)
    _, pull_key = jax.vjp(norm_rows, key_raw, qk_gain[1])
    d_key_raw, d_key_gain = pull_key(d_key)
    d_mixed = (
        jnp.stack(
            [
                d_query_raw.reshape(row_count, head_cols),
                d_key_raw.reshape(row_count, head_cols),
                d_value,
            ],
            axis=1,
        )
        .astype(jnp.bfloat16)
        .reshape(row_count, 3 * head_cols)
    )
    grad_qkv = outer_rows(normed, d_mixed).reshape(model_width, 3, head_cols)
    d_normed = (
        product_t(d_mixed, qkv_flat)
        + product_t(d_open, ogate_full)
        + product_t(d_forget_low, forget_full)
    )
    root = lax.rsqrt(jnp.mean(residual * residual, axis=1, keepdims=True) + epsilon)
    unit = residual * root
    d_unit = d_normed * gain_attn
    dot_part = (jnp.sum(d_unit * unit, axis=1) / model_width).reshape(slot_count, half_rows)
    d_unit_share, dot_full = (
        lax.psum_scatter(
            d_unit.reshape(slot_count, half_rows, model_width).astype(jnp.bfloat16),
            "tp",
            scatter_dimension=1,
            tiled=True,
        ).astype(jnp.float32),
        lax.psum_scatter(
            dot_part.astype(jnp.bfloat16), "tp", scatter_dimension=1, tiled=True
        ).astype(jnp.float32),
    )
    unit_share = own_slice(unit)
    root_share = own_slice(root)
    input_grad = (
        d_middle_share + root_share * (d_unit_share - unit_share * dot_full[:, :, None])
    ).astype(jnp.bfloat16)
    grad_parts = (
        lax.psum_scatter(
            grad_qkv.astype(jnp.bfloat16), ("shard", "ctx"), scatter_dimension=0, tiled=True
        ).astype(jnp.float32),
        lax.psum_scatter(
            grad_forget.astype(jnp.bfloat16), ("shard", "ctx"), scatter_dimension=0, tiled=True
        ).astype(jnp.float32),
        lax.psum_scatter(
            grad_ogate.astype(jnp.bfloat16), ("shard", "ctx"), scatter_dimension=0, tiled=True
        ).astype(jnp.float32),
        lax.psum_scatter(
            grad_out.astype(jnp.bfloat16), ("shard", "ctx"), scatter_dimension=0, tiled=True
        ).astype(jnp.float32),
        lax.psum_scatter(
            grad_gu.astype(jnp.bfloat16), ("shard", "ctx"), scatter_dimension=0, tiled=True
        ).astype(jnp.float32),
        lax.psum_scatter(
            grad_down.astype(jnp.bfloat16), ("shard", "ctx"), scatter_dimension=0, tiled=True
        ).astype(jnp.float32),
    )
    bias_full = lax.dynamic_update_slice_in_dim(
        jnp.zeros(forget_bias.shape, jnp.float32), d_bias_own, tensor_place * local_heads, 0
    )
    gain_attn_part = jnp.sum(d_normed * unit, axis=0)
    small_parts = lax.psum(
        (gain_attn_part, d_gain_mlp_own, jnp.stack([d_query_gain, d_key_gain]), bias_full),
        ("shard", "ctx", "tp"),
    )
    return (
        output,
        input_grad,
        grad_parts[0],
        grad_parts[1],
        small_parts[3],
        grad_parts[2],
        grad_parts[3],
        grad_parts[4],
        grad_parts[5],
        small_parts[0],
        small_parts[1],
        small_parts[2],
    )


def solution(mesh):
    return jax.shard_map(
        body,
        mesh=mesh,
        in_specs=(
            P("shard", ("ctx", "tp"), None),
            P("shard", ("ctx", "tp"), None),
            P("shard"),
            P(("shard", "ctx"), None, "tp"),
            P(("shard", "ctx"), "tp"),
            P(),
            P(("shard", "ctx"), "tp"),
            P(("shard", "ctx"), "tp"),
            P(("shard", "ctx"), None, "tp"),
            P(("shard", "ctx"), "tp"),
            P(),
            P(),
            P(),
        ),
        out_specs=(
            P("shard", ("ctx", "tp"), None),
            P("shard", ("ctx", "tp"), None),
            P(("shard", "ctx"), None, "tp"),
            P(("shard", "ctx"), "tp"),
            P(),
            P(("shard", "ctx"), "tp"),
            P(("shard", "ctx"), "tp"),
            P(("shard", "ctx"), None, "tp"),
            P(("shard", "ctx"), "tp"),
            P(),
            P(),
            P(),
        ),
        check_vma=False,
    )
```

profile of v0, /device:TPU:0, one launch (start us, length us, event | category | flops | bytes accessed | tf_op | source)
XLA Modules:
  0.0 1049.5 jit_solution(11627350117377922482)
XLA Ops:
  11.9 10.6 %all-gather = bf16[8,192,6]{1,2,0:T(8,128)(2,1)S(1)} all-gather(bf16[1,192,6]{1,2,0:T(8,128)(2,1)} %bitcast.510), channel_id=1, replica_groups=mesh['shard'=4,'ctx'=2,'tp'=4] {'shard','ctx'}, dimensions={0}, use_global_device_ids=true | all-gather | bytes 20736 | tf_op jit(solution)/shard_map/all_gather | solution.py:71
  24.6 24.8 %all-gather.9.cloned.1.call-done = bf16[1,512,1536]{2,1,0:T(8,128)(2,1)} async-done(((bf16[1,128,1536]{2,1,0:T(8,128)(2,1)}), bf16[1,512,1536]{2,1,0:T(8,128)(2,1)}) %all-gather.9.cloned.1.call-update) | async-done | bytes 1572880 | tf_op jit(solution)/shard_map/all_gather | solution.py:66
  59.5 24.7 %all-gather.11.cloned.1.call-done = bf16[1536,3,384]{2,0,1:T(8,128)(2,1)} async-done(((bf16[192,3,384]{2,0,1:T(8,128)(2,1)}), bf16[1536,3,384]{2,0,1:T(8,128)(2,1)}) %all-gather.11.cloned.1.call-update) | async-done | bytes 3538960 | tf_op jit(solution)/shard_map/all_gather | solution.py:70
  84.2 6.1 copy.92
  90.3 4.1 fusion.41
  118.7 37.0 %while.31 = (s32[]{:T(128)}, f32[6,512,64]{1,2,0:T(8,128)}, f32[6,512]{1,0:T(8,128)S(1)}, bf16[6,512,64]{2,1,0:T(8,128)(2,1)}, bf16[6,1024,64]{2,1,0:T(8,128)(2,...) while((s32[]{:T(128)}, f32[6,512,64]{1,2,0:T(8,128)}, ...), condition=%wide.region_8.9_spmd, body=%wide.region_5.8_spmd.sunk | while | flops 139460096 | bytes 7643265 | solution.py:152
  159.7 4.0 fusion.126
  168.9 116.0 %all-reduce.5.cloned.1.call-done = f32[512,1536]{1,0:T(8,128)} async-done(((f32[512,1536]{1,0:T(8,128)}), f32[512,1536]{1,0:T(8,128)}) %all-reduce.5.cloned.1.call-update) | async-done | bytes 3145744 | tf_op jit(solution)/shard_map/psum | solution.py:159
  289.3 42.5 %all-gather.17.cloned.1.call-done = bf16[1536,2,1024]{2,0,1:T(8,128)(2,1)} async-done(((bf16[192,2,1024]{2,0,1:T(8,128)(2,1)}), bf16[1536,2,1024]{2,0,1:T(8,128)(2,1)}) %all-gather.17.cloned.1.call-update) | async-done | bytes 6291472 | tf_op jit(solution)/shard_map/all_gather | solution.py:74
  331.8 8.7 copy.104
  340.5 8.1 fusion.36
  348.6 21.9 %all-gather.21.cloned.1.call-done = bf16[1,512,1536]{2,1,0:T(8,128)(2,1)} async-done(((bf16[1,128,1536]{2,1,0:T(8,128)(2,1)}), bf16[1,512,1536]{2,1,0:T(8,128)(2,1)}) %all-gather.21.cloned.1.call-update) | async-done | bytes 1572880 | tf_op jit(solution)/shard_map/all_gather | solution.py:67
  370.5 33.1 %all-gather.19.cloned.1.call-done = bf16[1536,1024]{1,0:T(8,128)(2,1)} async-done(((bf16[192,1024]{1,0:T(8,128)(2,1)}), bf16[1536,1024]{1,0:T(8,128)(2,1)}) %all-gather.19.cloned.1.call-update) | async-done | bytes 3145744 | tf_op jit(solution)/shard_map/all_gather | solution.py:75
  403.6 6.0 fusion.52
  410.9 8.0 convolution_bitcast_fusion.2
  423.5 6.7 fusion.47
  430.7 109.5 %all-reduce.7.cloned.1.call-done = f32[512,1536]{1,0:T(8,128)} async-done(((f32[512,1536]{1,0:T(8,128)}), f32[512,1536]{1,0:T(8,128)}) %all-reduce.7.cloned.1.call-update) | async-done | bytes 3145744 | tf_op jit(solution)/shard_map/psum | solution.py:187
  552.2 97.2 %while.32 = (s32[]{:T(128)}, f32[6,512,64]{1,2,0:T(8,128)}, f32[6,1024,64]{1,2,0:T(8,128)}, f32[6,1024,64]{1,2,0:T(8,128)}, f32[6,512]{1,0:T(8,128)}, /*index=5*...) while((s32[]{:T(128)}, f32[6,512,64]{1,2,0:T(8,128)}, ...), condition=%wide.region_18.19_spmd, body=%wide.region_14.18_spmd.sunk | while | flops 342981632 | bytes 20376776 | solution.py:217
  676.4 4.1 reduce-window.16
  711.3 3.4 multiply_reduce_fusion.2
  715.6 6.4 convolution_convert_fusion.2
  722.1 3.7 convolution_convert_fusion.5
  728.9 5.8 convolution_convert_fusion.1
  738.0 4.0 copy.114
  741.9 8.9 convolution_convert_fusion
  755.5 41.1 %all-reduce.1 = (f32[24]{0:T(128)}, f32[1536]{0:T(1024)}, f32[1536]{0:T(1024)}, f32[2,64]{1,0:T(2,128)}) all-reduce(f32[24]{0:T(128)S(1)} %dynamic_update_slice.28, f32[1536]{0:T(1024)S(1)} %get-tuple-element.207, f32[1536]{0:T(1024)S(1)} %fusion.108, ...), channel_id=1, replica_groups=mesh['shard'=4,'ctx'=2,'tp'=4] {'shard','ctx','tp'}, use_global_device_ids=true, to_apply=%region_30.31 | all-reduce | flops 3224 | bytes 25792 | tf_op jit(solution)/shard_map/psum | solution.py:309
  797.4 8.3 reduce-scatter.26.cloned.1.call-done
  807.7 37.9 %reduce-scatter.20.cloned.1.call-done = bf16[192,384]{1,0:T(8,128)(2,1)} async-done(((bf16[1536,384]{1,0:T(8,128)(2,1)}), bf16[192,384]{1,0:T(8,128)(2,1)}) %reduce-scatter.20.cloned.1.call-update) | async-done | bytes 147472 | tf_op jit(solution)/shard_map/reduce_scatter | solution.py:292
  847.2 38.6 %reduce-scatter.22.cloned.1.call-done = bf16[192,384]{1,0:T(8,128)(2,1)} async-done(((bf16[1536,384]{1,0:T(8,128)(2,1)}), bf16[192,384]{1,0:T(8,128)(2,1)}) %reduce-scatter.22.cloned.1.call-update) | async-done | bytes 147472 | tf_op jit(solution)/shard_map/reduce_scatter | solution.py:295
  887.5 36.4 %reduce-scatter.16.cloned.1.call-done = bf16[1,128,1536]{2,1,0:T(8,128)(2,1)} async-done(((bf16[1,512,1536]{2,1,0:T(8,128)(2,1)}), bf16[1,128,1536]{2,1,0:T(8,128)(2,1)}) %reduce-scatter.16.cloned.1.call-update) | async-done | bytes 393232 | tf_op jit(solution)/shard_map/reduce_scatter | solution.py:270
  926.1 48.2 %reduce-scatter.18.cloned.1.call-done = bf16[192,3,384]{2,0,1:T(8,128)(2,1)} async-done(((bf16[1536,3,384]{2,0,1:T(8,128)(2,1)}), bf16[192,3,384]{2,0,1:T(8,128)(2,1)}) %reduce-scatter.18.cloned.1.call-update) | async-done | bytes 442384 | tf_op jit(solution)/shard_map/reduce_scatter | solution.py:286
  976.3 63.0 %reduce-scatter.24.cloned.1.call-done = bf16[192,2,1024]{2,0,1:T(8,128)(2,1)} async-done(((bf16[1536,2,1024]{2,0,1:T(8,128)(2,1)}), bf16[192,2,1024]{2,0,1:T(8,128)(2,1)}) %reduce-scatter.24.cloned.1.call-update) | async-done | bytes 786448 | tf_op jit(solution)/shard_map/reduce_scatter | solution.py:298
  (435 shorter events, 288.5 us)
Async XLA Ops:
  7.2 17.4 %copy-start.69 = (f32[24]{0:T(128)S(1)}, f32[24]{0:T(128)}, u32[]{:S(2)}) copy-start(f32[24]{0:T(128)} %param.24) | copy-start | bytes 292
  7.2 42.2 %all-gather.9.cloned.1.call-start = ((), (), s32[]{:S(2)}) async-start(), calls=%async_computation.9 | async-start | bytes 1966080 | tf_op jit(solution)/shard_map/all_gather | solution.py:66
  7.9 76.3 %all-gather.11.cloned.1.call-start = ((), (), s32[]{:S(2)}) async-start(), calls=%async_computation.10 | async-start | bytes 3981312 | tf_op jit(solution)/shard_map/all_gather | solution.py:70
  8.7 42.5 %copy-start.59 = (f32[1536]{0:T(1024)S(1)}, f32[1536]{0:T(1024)}, u32[]{:S(2)}) copy-start(f32[1536]{0:T(1024)} %param.29) | copy-start | bytes 18436
  8.7 147.0 %all-gather.13.cloned.1.call-start = ((), (), s32[]{:S(2)}) async-start(), calls=%async_computation.11 | async-start | bytes 1327104 | tf_op jit(solution)/shard_map/all_gather | solution.py:72
  9.4 150.3 %all-gather.15.cloned.1.call-start = ((), (), s32[]{:S(2)}) async-start(), calls=%async_computation.12 | async-start | bytes 1327104 | tf_op jit(solution)/shard_map/all_gather | solution.py:73
  10.0 274.9 %all-reduce.5.cloned.1.call-start = ((), (), s32[]{:S(2)}) async-start(), calls=%async_computation.13 | async-start | bytes 6291456 | tf_op jit(solution)/shard_map/psum | solution.py:159
  11.5 84.3 %copy-start.49 = (f32[384]{0:T(512)}, f32[384]{0:T(512)S(1)}, u32[]{:S(2)}) copy-start(f32[384]{0:T(512)S(1)} %mul.513) | copy-start | bytes 4612
  22.7 30.5 %copy-start.39 = (bf16[1536,6]{0,1:T(8,128)(2,1)}, bf16[1536,6]{0,1:T(8,128)(2,1)S(1)}, u32[]{:S(2)}) copy-start(bf16[1536,6]{0,1:T(8,128)(2,1)S(1)} %reshape.771) | copy-start | bytes 55300
  51.2 39.1 %copy-start.57 = (f32[512]{0:T(512)}, f32[512]{0:T(512)S(1)}, u32[]{:S(2)}) copy-start(f32[512]{0:T(512)S(1)} %add_rsqrt_fusion) | copy-start | bytes 6148
  55.5 2.4 collective-permute-start.1
  59.5 30.8 %copy-start.2 = (bf16[1,512,1536]{2,1,0:T(8,128)(2,1)S(1)}, bf16[1,512,1536]{2,1,0:T(8,128)(2,1)}, u32[]{:S(2)}) copy-start(bf16[1,512,1536]{2,1,0:T(8,128)(2,1)} %all-gather.9.cloned.1.call-done) | copy-start | bytes 4718596
  94.6 9.4 copy-start.6
  96.7 13.4 %collective-permute-start = (bf16[1,512,384]{1,2,0:T(8,128)(2,1)}, bf16[1,512,384]{1,2,0:T(8,128)(2,1)}, u32[]{:S(2)}, u32[]{:S(2)}) collective-permute-start(bf16[1,512,384]{1,2,0:T(8,128)(2,1)} %multiply_convert_fusion.9), channel_id=1, source_target_pairs={{0,4},{1,5},{2,6},{3,7},{8,12},{9,13},{10,14},{11,15},{16,20},{17,... | collective-permute-start | bytes 1179656 | tf_op jit(solution)/shard_map/ppermute | solution.py:14
  99.6 12.7 %collective-permute-start.2 = (bf16[1,512,384]{1,2,0:T(8,128)(2,1)}, bf16[1,512,384]{1,2,0:T(8,128)(2,1)}, u32[]{:S(2)}, u32[]{:S(2)}) collective-permute-start(bf16[1,512,384]{1,2,0:T(8,128)(2,1)} %slice_bitcast_fusion.5), channel_id=1, source_target_pairs={{0,4},{1,5},{2,6},{3,7},{8,12},{9,13},{10,14},{11,15},{16,20},{17,... | collective-permute-start | bytes 1179656 | tf_op jit(solution)/shard_map/ppermute | solution.py:14
  163.7 168.1 %all-gather.17.cloned.1.call-start = ((), (), s32[]{:S(2)}) async-start(), calls=%async_computation.14 | async-start | bytes 7077888 | tf_op jit(solution)/shard_map/all_gather | solution.py:74
  165.9 204.6 %all-gather.21.cloned.1.call-start = ((), (), s32[]{:S(2)}) async-start(), calls=%async_computation.17 | async-start | bytes 1966080 | tf_op jit(solution)/shard_map/all_gather | solution.py:67
  166.7 236.9 %all-gather.19.cloned.1.call-start = ((), (), s32[]{:S(2)}) async-start(), calls=%async_computation.15 | async-start | bytes 3538944 | tf_op jit(solution)/shard_map/all_gather | solution.py:75
  167.4 372.7 %all-reduce.7.cloned.1.call-start = ((), (), s32[]{:S(2)}) async-start(), calls=%async_computation.18 | async-start | bytes 6291456 | tf_op jit(solution)/shard_map/psum | solution.py:187
  287.8 252.4 %copy-start = (f32[512,1536]{1,0:T(8,128)}, f32[512,1536]{1,0:T(8,128)S(1)}, u32[]{:S(2)}) copy-start(f32[512,1536]{1,0:T(8,128)S(1)} %get-tuple-element.267) | copy-start | bytes 9437188
  418.9 332.6 %reduce-scatter.14.cloned.1.call-start = ((), (), s32[]{:S(2)}) async-start(), calls=%async_computation.16 | async-start | bytes 1966080 | tf_op jit(solution)/shard_map/reduce_scatter | solution.py:168
  430.2 323.6 %reduce-scatter.30.cloned.1.call-start = ((), (), s32[]{:S(2)}) async-start(), calls=%async_computation.26 | async-start | bytes 442368
  653.4 51.7 %collective-permute-start.4 = (bf16[1,512,384]{1,2,0:T(8,128)(2,1)}, bf16[1,512,384]{1,2,0:T(8,128)(2,1)}, u32[]{:S(2)}, u32[]{:S(2)}) collective-permute-start(bf16[1,512,384]{1,2,0:T(8,128)(2,1)} %bitcast.100), channel_id=1, source_target_pairs={{4,0},{5,1},{6,2},{7,3},{12,8},{13,9},{14,10},{15,11},{20,16},{21,... | collective-permute-start | bytes 1179656 | tf_op jit(solution)/shard_map/ppermute | solution.py:14
  656.6 43.9 %collective-permute-start.3 = (bf16[1,512,384]{1,2,0:T(8,128)(2,1)}, bf16[1,512,384]{1,2,0:T(8,128)(2,1)}, u32[]{:S(2)}, u32[]{:S(2)}) collective-permute-start(bf16[1,512,384]{1,2,0:T(8,128)(2,1)} %bitcast.90), channel_id=1, source_target_pairs={{4,0},{5,1},{6,2},{7,3},{12,8},{13,9},{14,10},{15,11},{20,16},{21,... | collective-permute-start | bytes 1179656 | tf_op jit(solution)/shard_map/ppermute | solution.py:14
  665.8 6.0 collective-permute-start.5
  700.3 96.3 %reduce-scatter.28.cloned.1.call-start = ((), (), s32[]{:S(2)}) async-start(), calls=%async_computation.25 | async-start | bytes 163840
  715.6 90.1 %reduce-scatter.26.cloned.1.call-start = ((), (), s32[]{:S(2)}) async-start(), calls=%async_computation.24 | async-start | bytes 3538944 | tf_op jit(solution)/shard_map/reduce_scatter | solution.py:301
  722.1 123.5 %reduce-scatter.20.cloned.1.call-start = ((), (), s32[]{:S(2)}) async-start(), calls=%async_computation.21 | async-start | bytes 1327104 | tf_op jit(solution)/shard_map/reduce_scatter | solution.py:292
  725.8 160.0 %reduce-scatter.22.cloned.1.call-start = ((), (), s32[]{:S(2)}) async-start(), calls=%async_computation.22 | async-start | bytes 1327104 | tf_op jit(solution)/shard_map/reduce_scatter | solution.py:295
  728.0 195.9 %reduce-scatter.16.cloned.1.call-start = ((), (), s32[]{:S(2)}) async-start(), calls=%async_computation.19 | async-start | bytes 1966080 | tf_op jit(solution)/shard_map/reduce_scatter | solution.py:270
  728.5 245.8 %reduce-scatter.18.cloned.1.call-start = ((), (), s32[]{:S(2)}) async-start(), calls=%async_computation.20 | async-start | bytes 3981312 | tf_op jit(solution)/shard_map/reduce_scatter | solution.py:286
  734.8 304.5 %reduce-scatter.24.cloned.1.call-start = ((), (), s32[]{:S(2)}) async-start(), calls=%async_computation.23 | async-start | bytes 7077888 | tf_op jit(solution)/shard_map/reduce_scatter | solution.py:298
  (67 other events, 194.6 us)
Sparse Core Ops, SparseCore 0:
  9.6 39.7 all-gather.8
  51.3 32.8 all-gather.10
  86.1 24.0 all-gather.12
  112.0 24.0 all-gather.14
  163.8 121.0 all-reduce.4
  287.2 44.5 all-gather.16
  333.4 37.0 all-gather.20
  372.4 31.1 all-gather.18
  419.0 121.0 all-reduce.6
  542.3 34.2 reduce-scatter.13
  700.4 35.1 reduce-scatter.29
  738.2 19.1 reduce-scatter.27
  761.2 44.4 reduce-scatter.25
  808.8 36.7 reduce-scatter.19
  849.0 36.7 reduce-scatter.21
  888.6 35.2 reduce-scatter.15
  927.2 47.0 reduce-scatter.17
  977.6 61.7 reduce-scatter.23
where the time goes:
time: 1060 us; the launch traced here: 1050 us
  waiting for transfers between devices  611 us (58%)
  matrix products  162 us (15%)
  local copies, waits for them, and re-layouts  121 us (11%)
  other arithmetic  75.4 us (7%)
  blocking collectives  51.7 us (5%)
  between operations  16.1 us (2%)
  starting transfers between devices  12.3 us (1%)
    psum x1, waiting for transfers between devices, body(): branch_full = lax.psum(branch_part, 'tp')  116 us
    psum x1, waiting for transfers between devices, body(): d_normed_mid = lax.psum(d_mid_terms, 'tp')  109 us
    reduce_scatter x1, waiting for transfers between devices, body(): lax.psum_scatter(grad_gu.astype(jnp.bfloat16), ('shard', 'ctx'), scatter_...  63 us
    dot_general x24, matrix products, product_t(): lax.dot_general(left, right, (((1,), (1,)), ((), ())), preferred_element_...  58 us
    dot_general x18, matrix products, outer_rows(): lax.dot_general(left, right, (((0,), (0,)), ((), ())), preferred_element_...  52.8 us
    dot_general x18, matrix products, product(): return jnp.dot(left, right, preferred_element_type=jnp.float32)  51.2 us
    reduce_scatter x1, waiting for transfers between devices, body(): lax.psum_scatter(grad_qkv.astype(jnp.bfloat16), ('shard', 'ctx'), scatter...  48.2 us
    all_gather x1, waiting for transfers between devices, body(): lax.all_gather(w_gu, ('shard', 'ctx'), axis=0, tiled=True)  42.5 us
  transfers between devices with their start and end apart: 24, of which 14 were waited for; matrix products, arithmetic and copies ran while one was open for 31% of the time, Pallas kernels for 0%

commit v1 on v0

v1 whole, which is shorter than its diff:
```python
import functools
import math

import jax
import jax.numpy as jnp
from jax import lax
from jax.experimental import pallas as pl
from jax.experimental.pallas import tpu as pltpu
from jax.sharding import PartitionSpec as P

epsilon = 1e-06
f32 = jnp.float32
bf16 = jnp.bfloat16
BIG = 1e30
VMEM_LIMIT = 60 * 1024 * 1024


def mm(left, right):
    return jnp.dot(left, right, preferred_element_type=f32)


def mm_nt(left, right):
    return lax.dot_general(left, right, (((1,), (1,)), ((), ())), preferred_element_type=f32)


def mm_tn(left, right):
    return lax.dot_general(left, right, (((0,), (0,)), ((), ())), preferred_element_type=f32)


def whole(shape):
    return pl.BlockSpec(shape, lambda *_: (0,) * len(shape))


def call(kernel, outs, *operands, grid=None, in_specs=None, out_specs=None, scratch=(), flops=0):
    size = sum(math.prod(o.shape) * o.dtype.itemsize for o in list(operands) + list(outs))
    extra = {}
    if grid is not None:
        extra = dict(grid=grid, in_specs=in_specs, out_specs=out_specs)
    return pl.pallas_call(
        kernel,
        out_shape=outs,
        scratch_shapes=list(scratch),
        compiler_params=pltpu.CompilerParams(vmem_limit_bytes=VMEM_LIMIT),
        cost_estimate=pl.CostEstimate(flops=int(flops), bytes_accessed=int(size), transcendentals=0),
        **extra,
    )(*operands)


def sds(shape, dtype):
    return jax.ShapeDtypeStruct(shape, dtype)


def swap(value, axis, bit):
    n = lax.axis_size(axis)
    return lax.ppermute(value, axis, [(j, j ^ bit) for j in range(n)])


def gather_rows(own):
    n = lax.axis_size("tp")
    return [own] + [swap(own, "tp", k) for k in range(1, n)]


def scatter_rows(parts):
    n = lax.axis_size("tp")
    got = [swap(parts[k], "tp", k) for k in range(1, n)]
    total = parts[0].astype(f32)
    for g in got:
        total = total + g.astype(f32)
    return total


def sum_all(value):
    for axis in ("ctx", "tp", "shard"):
        n = lax.axis_size(axis)
        total = value
        for k in range(1, n):
            total = total + swap(value, axis, k)
        value = total
    return value


def project_kernel(heads, size, chunks, *refs):
    x_refs = refs[:chunks]
    w_ref, gain_ref, qk_ref, bias_ref, rank_ref, rank_t_ref = refs[chunks : chunks + 6]
    (normed_ref, q_ref, kv_ref, qraw_ref, kraw_ref, open_ref, pre_ref, cum_ref, cumt_ref) = refs[
        chunks + 6 :
    ]
    rows = x_refs[0].shape[0]
    cols = heads * size
    gain = gain_ref[...]
    for c in range(chunks):
        x = x_refs[c][...].astype(f32)
        r = lax.rsqrt(jnp.mean(x * x, axis=1, keepdims=True) + epsilon)
        normed_ref[c * rows : (c + 1) * rows, :] = (x * r * gain).astype(bf16)
    normed = normed_ref[...]
    for which, raw_ref, out_ref in ((0, qraw_ref, q_ref), (1, kraw_ref, kv_ref)):
        raw = mm(normed, w_ref[:, which * cols : (which + 1) * cols])
        raw_ref[...] = raw
        g = qk_ref[which : which + 1, :]
        for h in range(heads):
            piece = raw[:, h * size : (h + 1) * size]
            r = lax.rsqrt(jnp.mean(piece * piece, axis=1, keepdims=True) + epsilon)
            out_ref[:, h * size : (h + 1) * size] = (piece * r * g).astype(bf16)
    kv_ref[:, cols : 2 * cols] = mm(normed, w_ref[:, 2 * cols : 3 * cols]).astype(bf16)
    open_ref[...] = jax.nn.sigmoid(mm(normed, w_ref[:, 3 * cols : 4 * cols]))
    pre = mm(normed, w_ref[:, 4 * cols :]) + bias_ref[...]
    pre_ref[...] = pre
    logs = jnp.minimum(pre, 0.0) - jnp.log(1.0 + jnp.exp(-jnp.abs(pre)))
    earlier = (rank_t_ref[...] <= rank_ref[...]).astype(f32)
    cum = lax.dot_general(
        earlier, logs, (((1,), (0,)), ((), ())), precision=lax.Precision.HIGHEST, preferred_element_type=f32
    )
    total = jnp.sum(logs, axis=0, keepdims=True)
    cum_ref[...] = cum
    cumt_ref[0:8, :] = jnp.transpose(cum)[0:8, :]
    cumt_ref[8:16, :] = jnp.transpose(cum - total)[0:8, :]


def attend_kernel(heads, size, q_ref, kv_ref, kvl_ref, cum_ref, cumt_ref, left_ref, open_ref, rank_ref, rank_t_ref,
                  wout_ref, gated_ref, att_ref, lse_ref, *branch_refs):
    cols = heads * size
    rows = q_ref.shape[0]
    scale = 1.0 / math.sqrt(size)
    chunks = len(branch_refs)
    step = rows // chunks
    block = min(256, rows)
    keep = rank_t_ref[...] <= rank_ref[...]
    for b in range(rows // block):
        at = slice(b * block, (b + 1) * block)
        mask = keep[at, :]
        lses = []
        for h in range(heads):
            hs = slice(h * size, (h + 1) * size)
            vs = slice(cols + h * size, cols + (h + 1) * size)
            q = q_ref[at, hs]
            cq = cum_ref[at, h : h + 1]
            left = mm_nt(q, kvl_ref[:, hs]) * scale + (cq - left_ref[h : h + 1, :])
            right = mm_nt(q, kv_ref[:, hs]) * scale + (cq - cumt_ref[h : h + 1, :])
            el = jnp.exp(left)
            er = jnp.exp(jnp.where(mask, right, -BIG))
            total = jnp.sum(el, axis=1, keepdims=True) + jnp.sum(er, axis=1, keepdims=True)
            o = mm(el.astype(bf16), kvl_ref[:, vs]) + mm(er.astype(bf16), kv_ref[:, vs])
            att = o / total
            att_ref[at, hs] = att
            gated_ref[at, hs] = (att * open_ref[at, hs]).astype(bf16)
            lses.append(jnp.log(total))
        lse_ref[at, :] = jnp.concatenate(lses + [jnp.zeros((block, 128 - heads), f32)], axis=1)
    w = wout_ref[...]
    for c in range(chunks):
        at = slice(c * step, (c + 1) * step)
        branch_refs[c][...] = mm_nt(gated_ref[at, :], w).astype(bf16)


def ffn_kernel(steps, chunks, nm_ref, cot_ref, wg_ref, wu_ref, wd_ref, hid_ref, dg_ref, du_ref, *rest):
    p_refs = rest[:chunks]
    acc_ref = rest[chunks]
    j = pl.program_id(0)
    gate = mm(nm_ref[...], wg_ref[...])
    up = mm(nm_ref[...], wu_ref[...])
    dh = mm(cot_ref[...], wd_ref[...])
    sig = jax.nn.sigmoid(gate)
    act = gate * sig
    hid_ref[...] = (act * up).astype(bf16)
    dg = (dh * up * sig * (1.0 + gate * (1.0 - sig))).astype(bf16)
    du = (dh * act).astype(bf16)
    dg_ref[...] = dg
    du_ref[...] = du
    part = mm_nt(dg, wg_ref[...]) + mm_nt(du, wu_ref[...])

    @pl.when(j == 0)
    def _():
        acc_ref[...] = part

    @pl.when(j > 0)
    def _():
        acc_ref[...] += part

    @pl.when(j == steps - 1)
    def _():
        rows = acc_ref.shape[0] // chunks
        for c in range(chunks):
            p_refs[c][...] = acc_ref[c * rows : (c + 1) * rows, :].astype(bf16)


def attend_back_kernel(heads, size, q_ref, kv_ref, kvl_ref, cum_ref, cumt_ref, left_ref, open_ref, att_ref, lse_ref,
                       rank_ref, rank_t_ref, db_ref, wout_ref,
                       dq_ref, dkv_ref, back_ref, dopen_ref, dcum_ref, dleft_ref):
    cols = heads * size
    rows = q_ref.shape[0]
    scale = 1.0 / math.sqrt(size)
    block = min(256, rows)
    keep = rank_t_ref[...] <= rank_ref[...]
    ones = jnp.ones((block, 64), bf16)
    dcs, dls = [], []
    dg_all = mm(db_ref[...], wout_ref[...])
    op = open_ref[...]
    att_all = att_ref[...]
    dopen_ref[...] = (dg_all * att_all * op * (1.0 - op)).astype(bf16)
    da_all = (dg_all * op).astype(bf16)
    prod = da_all.astype(f32) * att_all
    for h in range(heads):
        hs = slice(h * size, (h + 1) * size)
        vs = slice(cols + h * size, cols + (h + 1) * size)
        kl, kr = kvl_ref[:, hs], kv_ref[:, hs]
        vl, vr = kvl_ref[:, vs], kv_ref[:, vs]
        sums = [None] * 6
        row_sums = []
        for b in range(rows // block):
            at = slice(b * block, (b + 1) * block)
            q = q_ref[at, hs]
            da = da_all[at, hs]
            delta = jnp.sum(prod[at, hs], axis=1, keepdims=True)
            cq = cum_ref[at, h : h + 1] - lse_ref[at, h : h + 1]
            pl_ = jnp.exp(mm_nt(q, kl) * scale + (cq - left_ref[h : h + 1, :]))
            right = mm_nt(q, kr) * scale + (cq - cumt_ref[h : h + 1, :])
            pr = jnp.exp(jnp.where(keep[at, :], right, -BIG))
            dsl = (pl_ * (mm_nt(da, vl) - delta)).astype(bf16)
            dsr = (pr * (mm_nt(da, vr) - delta)).astype(bf16)
            dq_ref[at, hs] = (mm(dsl, kl) + mm(dsr, kr)) * scale
            fl, fr = dsl.astype(f32), dsr.astype(f32)
            row_sums.append(jnp.sum(fl, axis=1, keepdims=True) + jnp.sum(fr, axis=1, keepdims=True))
            new = [
                mm_tn(dsl, q),
                mm_tn(dsr, q),
                mm_tn(pl_.astype(bf16), da),
                mm_tn(pr.astype(bf16), da),
                jnp.sum(fl, axis=0, keepdims=True),
                jnp.sum(fr, axis=0, keepdims=True),
            ]
            sums = [n if s is None else s + n for s, n in zip(sums, new)]
        back_ref[:, hs] = (sums[0] * scale).astype(bf16)
        dkv_ref[:, hs] = sums[1] * scale
        back_ref[:, vs] = sums[2].astype(bf16)
        dkv_ref[:, vs] = sums[3]
        rs = jnp.concatenate(row_sums, axis=0)
        dls.append(-sums[4])
        dcs.append((rs, -sums[5]))
    pad = 128 - heads
    rs_all = jnp.concatenate([d[0] for d in dcs] + [jnp.zeros((rows, pad), f32)], axis=1)
    rs_t = jnp.transpose(rs_all)
    for h in range(heads):
        dcum_ref[h : h + 1, :] = rs_t[h : h + 1, :] + dcs[h][1]
        dleft_ref[h : h + 1, :] = dls[h]
    for h in range(heads, 8):
        dcum_ref[h : h + 1, :] = jnp.zeros((1, rows), f32)
        dleft_ref[h : h + 1, :] = jnp.zeros((1, rows), f32)


def project_back_kernel(heads, size, chunks, *refs):
    x_refs = refs[:chunks]
    (w_ref, qk_ref, qraw_ref, kraw_ref, dq_ref, dkv_ref, back_ref, dopen_ref, dcum_ref, dleft_ref, extra_ref, pre_ref,
     rank_ref, rank_t_ref) = refs[chunks : chunks + 14]
    mixed_ref, bias_ref, gain_ref, qkg_ref = refs[chunks + 14 : chunks + 18]
    out_refs = refs[chunks + 18 :]
    cols = heads * size
    rows = x_refs[0].shape[0]
    for which, raw_ref in ((0, qraw_ref), (1, kraw_ref)):
        g = qk_ref[which : which + 1, :]
        total = jnp.zeros((1, size), f32)
        for h in range(heads):
            hs = slice(h * size, (h + 1) * size)
            d = dq_ref[:, hs] if which == 0 else dkv_ref[:, hs] + back_ref[:, hs].astype(f32)
            raw = raw_ref[:, hs]
            r = lax.rsqrt(jnp.mean(raw * raw, axis=1, keepdims=True) + epsilon)
            u = raw * r
            total = total + jnp.sum(d * u, axis=0, keepdims=True)
            e = d * g
            mixed_ref[:, which * cols + h * size : which * cols + (h + 1) * size] = (
                r * (e - u * jnp.mean(e * u, axis=1, keepdims=True))
            ).astype(bf16)
        qkg_ref[which : which + 1, :] = total
    mixed_ref[:, 2 * cols : 3 * cols] = (dkv_ref[:, cols:] + back_ref[:, cols:].astype(f32)).astype(bf16)
    mixed_ref[:, 3 * cols : 4 * cols] = dopen_ref[...]
    later = (rank_t_ref[...] <= rank_ref[...]).astype(f32)
    dcum = dcum_ref[...] + dleft_ref[...]
    dlog = lax.dot_general(
        dcum, later, (((1,), (0,)), ((), ())), precision=lax.Precision.HIGHEST, preferred_element_type=f32
    ) + extra_ref[:, 0:1]
    dlog = jnp.concatenate([dlog, jnp.zeros((120, dlog.shape[1]), f32)], axis=0)
    df = jnp.transpose(dlog) * jax.nn.sigmoid(-pre_ref[...])
    bias_ref[...] = jnp.sum(df, axis=0, keepdims=True)
    mixed_ref[:, 4 * cols :] = df.astype(bf16)
    gain = jnp.zeros((1, x_refs[0].shape[1]), f32)
    for c in range(chunks):
        at = slice(c * rows, (c + 1) * rows)
        dn = mm_nt(mixed_ref[at, :], w_ref[...])
        out_refs[c][...] = dn.astype(bf16)
        x = x_refs[c][...].astype(f32)
        r = lax.rsqrt(jnp.mean(x * x, axis=1, keepdims=True) + epsilon)
        gain = gain + jnp.sum(dn * (x * r), axis=0, keepdims=True)
    gain_ref[...] = gain


def body(tokens, cotangent, lengths, w_qkv, w_forget, forget_bias, w_ogate, w_out, w_gu, w_down, gain_attn, gain_mlp,
         qk_gain):
    slots, rows, width = tokens.shape
    assert slots == 1
    n = lax.axis_size("tp")
    me = lax.axis_index("tp")
    half = lax.axis_index("ctx")
    both = ("shard", "ctx")
    span = rows * n
    heads = w_forget.shape[1]
    size = qk_gain.shape[1]
    cols = heads * size
    units = w_down.shape[1]
    slab = w_qkv.shape[0]

    x_own = tokens[0]
    x_parts = gather_rows(x_own)

    own_pos = half * span + me * rows + jnp.arange(rows, dtype=jnp.int32)
    valid = (own_pos < lengths[0]).astype(f32)[:, None]
    cot_own = (cotangent[0].astype(f32) * valid).astype(bf16)
    cot_own, _ = lax.optimization_barrier((cot_own, x_parts))
    cot_parts = gather_rows(cot_own)

    order = jnp.concatenate([(me ^ k) * rows + jnp.arange(rows, dtype=jnp.int32) for k in range(n)])
    rank, rank_t = order[:, None], order[None, :]

    first = jnp.concatenate(
        [w_qkv.reshape(slab, 3 * cols), w_ogate, w_forget, jnp.zeros((slab, 128 - heads), bf16)], axis=1
    )
    w_first = lax.all_gather(first, both, axis=0, tiled=True)
    w_out_full = lax.all_gather(w_out, both, axis=0, tiled=True)
    w_gu_full = lax.all_gather(w_gu.reshape(slab, 2 * units), both, axis=0, tiled=True)
    w_down_full = lax.all_gather(w_down, both, axis=0, tiled=True)

    bias = lax.dynamic_slice_in_dim(forget_bias, me * heads, heads)
    bias = jnp.concatenate([bias, jnp.zeros((128 - heads,), f32)])[None, :]
    gain_a, gain_m = gain_attn[None, :], gain_mlp[None, :]

    wide = w_first.shape[1]
    normed, q, kv, qraw, kraw, opener, pre, cum, cumt = call(
        functools.partial(project_kernel, heads, size, n),
        [
            sds((span, width), bf16),
            sds((span, cols), bf16),
            sds((span, 2 * cols), bf16),
            sds((span, cols), f32),
            sds((span, cols), f32),
            sds((span, cols), f32),
            sds((span, 128), f32),
            sds((span, 128), f32),
            sds((16, span), f32),
        ],
        *x_parts, w_first, gain_a, qk_gain, bias, rank, rank_t,
        flops=2 * span * width * wide,
    )
    left_to_right = [(0, 1)]
    kv_left = lax.ppermute(kv, "ctx", left_to_right)
    cum_left = lax.ppermute(cumt[8:16], "ctx", left_to_right)
    cum_left = jnp.where(half == 0, BIG, cum_left)
    cum_rows = cumt[0:8]

    gated, attended, lse, *branch = call(
        functools.partial(attend_kernel, heads, size),
        [sds((span, cols), bf16), sds((span, cols), f32), sds((span, 128), f32)] + [sds((rows, width), bf16)] * n,
        q, kv, kv_left, cum, cum_rows, cum_left, opener, rank, rank_t, w_out_full,
        flops=2 * span * 2 * span * cols * 2 + 2 * span * cols * width,
    )
    x_f = x_own.astype(f32)
    middle = x_f + scatter_rows(branch)
    r2 = lax.rsqrt(jnp.mean(middle * middle, axis=1, keepdims=True) + epsilon)
    u2 = middle * r2
    nm_own = (u2 * gain_m).astype(bf16)
    nm = jnp.concatenate(gather_rows(nm_own), axis=0)
    cot = jnp.concatenate(cot_parts, axis=0)

    tile = min(256, units)
    steps = units // tile
    hidden, d_gate, d_up, *p_parts = call(
        functools.partial(ffn_kernel, steps, n),
        [sds((span, units), bf16)] * 3 + [sds((rows, width), bf16)] * n,
        nm, cot, w_gu_full, w_gu_full, w_down_full,
        grid=(steps,),
        in_specs=[
            whole((span, width)),
            whole((span, width)),
            pl.BlockSpec((width, tile), lambda j: (0, j)),
            pl.BlockSpec((width, tile), lambda j: (0, j + steps)),
            pl.BlockSpec((width, tile), lambda j: (0, j)),
        ],
        out_specs=[pl.BlockSpec((span, tile), lambda j: (0, j))] * 3 + [whole((rows, width))] * n,
        scratch=[pltpu.VMEM((span, width), f32)],
        flops=2 * span * width * units * 5,
    )
    d_nm = scatter_rows(p_parts)

    def reduce_weight(grad):
        return lax.psum_scatter(grad.astype(bf16), both, scatter_dimension=0, tiled=True).astype(f32)

    d_units = jnp.concatenate([d_gate, d_up], axis=1)
    grad_gu = reduce_weight(mm_tn(nm, d_units)).reshape(slab, 2, units)
    grad_down = reduce_weight(mm_tn(cot, hidden))

    e2 = d_nm * gain_m
    d_middle = valid * cotangent[0].astype(f32) + r2 * (e2 - u2 * jnp.mean(e2 * u2, axis=1, keepdims=True))
    gain_m_part = jnp.sum(d_nm * u2, axis=0)
    db_parts = gather_rows(d_middle.astype(bf16))
    d_branch = jnp.concatenate(db_parts, axis=0)

    hidden_late, _ = lax.optimization_barrier((hidden, d_branch))
    down = mm_nt(hidden_late, w_down_full).astype(bf16)
    down_parts = [down[k * rows : (k + 1) * rows] for k in range(n)]
    output = (valid * (middle + scatter_rows(down_parts))).astype(bf16)

    grad_out = reduce_weight(mm_tn(d_branch, gated))
    dq, dkv, back, d_open, d_cum, d_left = call(
        functools.partial(attend_back_kernel, heads, size),
        [
            sds((span, cols), f32),
            sds((span, 2 * cols), f32),
            sds((span, 2 * cols), bf16),
            sds((span, cols), bf16),
            sds((8, span), f32),
            sds((8, span), f32),
        ],
        q, kv, kv_left, cum, cum_rows, cum_left, opener, attended, lse, rank, rank_t, d_branch, w_out_full,
        flops=2 * span * 2 * span * cols * 5 + 2 * span * cols * width,
    )
    right_to_left = [(1, 0)]
    back = lax.ppermute(back, "ctx", right_to_left)
    sent = jnp.concatenate([d_left, jnp.broadcast_to(jnp.sum(d_cum, axis=1, keepdims=True), (8, 128))], axis=1)
    sent = lax.ppermute(sent, "ctx", right_to_left)
    d_left, extra = sent[:, :span], sent[:, span:]

    mixed, bias_part, gain_part, qkg_part, *dn_parts = call(
        functools.partial(project_back_kernel, heads, size, n),
        [sds((span, wide), bf16), sds((1, 128), f32), sds((1, width), f32), sds((2, size), f32)]
        + [sds((rows, width), bf16)] * n,
        *x_parts, w_first, qk_gain, qraw, kraw, dq, dkv, back, d_open, d_cum, d_left, extra, pre, rank, rank_t,
        flops=2 * span * width * wide,
    )
    d_normed = scatter_rows(dn_parts)
    grad_first = reduce_weight(mm_tn(normed, mixed))
    grad_qkv = grad_first[:, : 3 * cols].reshape(slab, 3, cols)
    grad_ogate = grad_first[:, 3 * cols : 4 * cols]
    grad_forget = grad_first[:, 4 * cols : 4 * cols + heads]

    r1 = lax.rsqrt(jnp.mean(x_f * x_f, axis=1, keepdims=True) + epsilon)
    u1 = x_f * r1
    e1 = d_normed * gain_a
    input_grad = (d_middle + r1 * (e1 - u1 * jnp.mean(e1 * u1, axis=1, keepdims=True))).astype(bf16)

    bias_full = lax.dynamic_update_slice_in_dim(
        jnp.zeros(forget_bias.shape, f32), bias_part[0, :heads], me * heads, 0
    )
    small = sum_all(jnp.concatenate([gain_part[0], gain_m_part, qkg_part.reshape(-1), bias_full]))
    edges = [0, width, 2 * width, 2 * width + 2 * size]
    return (
        output[None],
        input_grad[None],
        grad_qkv,
        grad_forget,
        small[edges[3] :],
        grad_ogate,
        grad_out,
        grad_gu,
        grad_down,
        small[edges[0] : edges[1]],
        small[edges[1] : edges[2]],
        small[edges[2] : edges[3]].reshape(2, size),
    )


def solution(mesh):
    rows = P("shard", ("ctx", "tp"), None)
    flat = P(("shard", "ctx"), "tp")
    deep = P(("shard", "ctx"), None, "tp")
    return jax.shard_map(
        body,
        mesh=mesh,
        in_specs=(rows, rows, P("shard"), deep, flat, P(), flat, flat, deep, flat, P(), P(), P()),
        out_specs=(rows, rows, deep, flat, P(), flat, flat, deep, flat, P(), P(), P()),
        check_vma=False,
    )
```

time: 1060 us -> 509 us (0.48)
  waiting for transfers between devices: 611 us -> 267 us
  matrix products: 162 us -> 25.4 us
  local copies, waits for them, and re-layouts: 121 us -> 23.1 us
  Pallas kernels: 0 us -> 77.9 us
  starting transfers between devices: 12.3 us -> 78.4 us
  other arithmetic: 75.4 us -> 15.8 us
  blocking collectives: 51.7 us -> 0 us
    psum x2 -> x0, waiting for transfers between devices: 225 us -> none  [the longest x1 116 us: body(): branch_full = lax.psum(branch_part, 'tp')]
    ppermute x6 -> x35, waiting for transfers between devices: 0.76 us -> 197 us  [the longest x31 195 us: swap(): return lax.ppermute(value, axis, [(j, j ^ bit) for j in range(n)])]
    reduce_scatter x7 -> x4, waiting for transfers between devices: 233 us -> 54.5 us  [reduce_weight(): lax.psum_scatter(grad.astype(bf16), both, scatter_dimension=0, tiled=True)]
    dot_general x60 -> x5, matrix products: 162 us -> 25.4 us  [the longest x4 21.6 us: mm_tn(): lax.dot_general(left, right, (((0,), (0,)), ((), ())), preferred_element_...]
    all_gather x7 -> x4, waiting for transfers between devices: 147 us -> 13.7 us  [the longest x1 7.78 us: body(): w_first = lax.all_gather(first, both, axis=0, tiled=True)]
    pallas_call x0 -> x5, Pallas kernels: none -> 77.9 us  [call(): pl.pallas_call(kernel, out_shape=outs, scratch_shapes=list(scratch), comp...]
    ppermute x6 -> x35, starting transfers between devices: 10.6 us -> 77.7 us  [the longest x31 71.5 us: swap(): return lax.ppermute(value, axis, [(j, j ^ bit) for j in range(n)])]
    psum x1 -> x0, blocking collectives: 41.1 us -> none  [body(): lax.psum((gain_attn_part, d_gain_mlp_own, jnp.stack([d_query_gain, d_key_...]
  transfers between devices with their start and end apart: 24 -> 43, of which waited for: 14 -> 17; matrix products, arithmetic and copies ran while one was open for 31% -> 10% of each run, Pallas kernels for 0% -> 11%
where the time goes in v1:
time: 509 us; the launch traced here: 503 us
  waiting for transfers between devices  267 us (52%)
  starting transfers between devices  78.4 us (15%)
  Pallas kernels  77.9 us (15%)
  matrix products  25.4 us (5%)
  local copies, waits for them, and re-layouts  23.1 us (5%)
  other arithmetic  15.8 us (3%)
  between operations  15.5 us (3%)
    ppermute x31, waiting for transfers between devices, swap(): return lax.ppermute(value, axis, [(j, j ^ bit) for j in range(n)])  195 us
    pallas_call x5, Pallas kernels, call(): pl.pallas_call(kernel, out_shape=outs, scratch_shapes=list(scratch), comp...  77.9 us
    ppermute x31, starting transfers between devices, swap(): return lax.ppermute(value, axis, [(j, j ^ bit) for j in range(n)])  71.5 us
    reduce_scatter x4, waiting for transfers between devices, reduce_weight(): lax.psum_scatter(grad.astype(bf16), both, scatter_dimension=0, tiled=True)  54.5 us
    dot_general x4, matrix products, mm_tn(): lax.dot_general(left, right, (((0,), (0,)), ((), ())), preferred_element_...  21.6 us
  transfers between devices with their start and end apart: 43, of which 17 were waited for; matrix products, arithmetic and copies ran while one was open for 10% of the time, Pallas kernels for 11%

profile of v1, /device:TPU:0, one launch (start us, length us, event | category | flops | bytes accessed | tf_op | source)
XLA Modules:
  0.0 502.9 jit_solution(6147996110816987647)
XLA Ops:
  13.8 3.1 collective-permute-start
  22.3 11.4 %collective-permute-done.refs_1_ = bf16[128,1536]{1,0:T(8,128)(2,1)S(1)} collective-permute-done((bf16[128,1536]{1,0:T(8,128)(2,1)S(1)}, bf16[128,1536]{1,0:T(8,128)(2,1)S(1)}, u32[]{:S(2)}, u32[]{:S(2)}) %collective-permute-start) | collective-permute-done | bytes 393248 | tf_op jit(solution)/shard_map/ppermute | solution.py:55
  33.7 13.0 %collective-permute-done.1.refs_2_ = bf16[128,1536]{1,0:T(8,128)(2,1)S(1)} collective-permute-done((bf16[128,1536]{1,0:T(8,128)(2,1)S(1)}, bf16[128,1536]{1,0:T(8,128)(2,1)S(1)}, u32[]{:S(2)}, u32[]{:S(2)}) %collective-permute-start.1) | collective-permute-done | bytes 393248 | tf_op jit(solution)/shard_map/ppermute | solution.py:55
  46.7 7.8 %all-gather.5.cloned.1.call-done.refs_4_ = bf16[1536,1664]{1,0:T(8,128)(2,1)} async-done(((bf16[192,1664]{1,0:T(8,128)(2,1)}), bf16[1536,1664]{1,0:T(8,128)(2,1)}) %all-gather.5.cloned.1.call-update) | async-done | bytes 5111824 | tf_op jit(solution)/shard_map/all_gather | solution.py:324
  54.5 10.4 %shard_map.220 = (bf16[512,1536]{1,0:T(8,128)(2,1)}, bf16[512,384]{1,0:T(8,128)(2,1)}, bf16[512,768]{1,0:T(8,128)(2,1)}, f32[512,384]{1,0:T(8,128)}, f32[512,384...) custom-call(bf16[128,1536]{1,0:T(8,128)(2,1)} %bitcast.38, ...), custom_call_target="tpu_custom_call" | custom-call | flops 2617245696 | bytes 12364800 | tf_op jit(solution)/shard_map/pallas_call | solution.py:39
  74.6 5.9 %all-gather.7.cloned.1.call-done.wout_ref = bf16[1536,384]{1,0:T(8,128)(2,1)} async-done(((bf16[192,384]{1,0:T(8,128)(2,1)}), bf16[1536,384]{1,0:T(8,128)(2,1)}) %all-gather.7.cloned.1.call-update) | async-done | bytes 1179664 | tf_op jit(solution)/shard_map/all_gather | solution.py:325
  81.4 10.9 %shard_map.221 = (bf16[512,384]{1,0:T(8,128)(2,1)}, f32[512,384]{1,0:T(8,128)}, f32[512,128]{1,0:T(8,128)}, bf16[128,1536]{1,0:T(8,128)(2,1)}, bf16[128,1536]{1,...) custom-call(bf16[512,384]{1,0:T(8,128)(2,1)} %get-tuple-element.51.q_ref, ...), custom_call_target="tpu_custom_call" | custom-call | flops 1409286144 | bytes 7245824 | tf_op jit(solution)/shard_map/pallas_call | solution.py:39
  96.8 3.4 collective-permute-start.13
  100.2 11.5 %collective-permute-done.5 = bf16[128,1536]{1,0:T(8,128)(2,1)S(1)} collective-permute-done((bf16[128,1536]{1,0:T(8,128)(2,1)}, bf16[128,1536]{1,0:T(8,128)(2,1)S(1)}, u32[]{:S(2)}, u32[]{:S(2)}) %collective-permute-start.5) | collective-permute-done | bytes 393248 | tf_op jit(solution)/shard_map/ppermute | solution.py:55
  111.7 20.5 %collective-permute-done.6 = bf16[128,1536]{1,0:T(8,128)(2,1)S(1)} collective-permute-done((bf16[128,1536]{1,0:T(8,128)(2,1)}, bf16[128,1536]{1,0:T(8,128)(2,1)S(1)}, u32[]{:S(2)}, u32[]{:S(2)}) %collective-permute-start.6) | collective-permute-done | bytes 393248 | tf_op jit(solution)/shard_map/ppermute | solution.py:55
  135.7 16.5 %collective-permute-start.8 = (bf16[128,1536]{1,0:T(8,128)(2,1)S(1)}, bf16[128,1536]{1,0:T(8,128)(2,1)S(1)}, u32[]{:S(2)}, u32[]{:S(2)}) collective-permute-start(bf16[128,1536]{1,0:T(8,128)(2,1)S(1)} %multiply_convert_fusion.1), channel_id=1, source_target_pairs={{0,1},{1,0},{2,3},{3,2},{4,5},{5,4},{6,7},{7,6},{8,9},{9,8},{10,11... | collective-permute-start | bytes 1179656 | tf_op jit(solution)/shard_map/ppermute | solution.py:55
  152.3 9.5 %collective-permute-done.8 = bf16[128,1536]{1,0:T(8,128)(2,1)S(1)} collective-permute-done((bf16[128,1536]{1,0:T(8,128)(2,1)S(1)}, bf16[128,1536]{1,0:T(8,128)(2,1)S(1)}, u32[]{:S(2)}, u32[]{:S(2)}) %collective-permute-start.8) | collective-permute-done | bytes 393248 | tf_op jit(solution)/shard_map/ppermute | solution.py:55
  161.8 20.0 %collective-permute-done.9 = bf16[128,1536]{1,0:T(8,128)(2,1)S(1)} collective-permute-done((bf16[128,1536]{1,0:T(8,128)(2,1)S(1)}, bf16[128,1536]{1,0:T(8,128)(2,1)S(1)}, u32[]{:S(2)}, u32[]{:S(2)}) %collective-permute-start.9) | collective-permute-done | bytes 393248 | tf_op jit(solution)/shard_map/ppermute | solution.py:55
  183.1 21.4 %shard_map.222 = (bf16[512,1024]{1,0:T(8,128)(2,1)}, bf16[512,1024]{1,0:T(8,128)(2,1)}, bf16[512,1024]{1,0:T(8,128)(2,1)}, bf16[128,1536]{1,0:T(8,128)(2,1)}, bf...) custom-call(bf16[512,1536]{1,0:T(8,128)(2,1)} %pad_maximum_fusion.nm_ref, ...), custom_call_target="tpu_custom_call" | custom-call | flops 8053063680 | bytes 23592960 | tf_op jit(solution)/shard_map/pallas_call | solution.py:39
  204.6 2.9 collective-permute-start.15
  209.0 13.4 %collective-permute-done.14 = bf16[128,1536]{1,0:T(8,128)(2,1)S(1)} collective-permute-done((bf16[128,1536]{1,0:T(8,128)(2,1)}, bf16[128,1536]{1,0:T(8,128)(2,1)S(1)}, u32[]{:S(2)}, u32[]{:S(2)}) %collective-permute-start.14) | collective-permute-done | bytes 393248 | tf_op jit(solution)/shard_map/ppermute | solution.py:55
  222.3 12.3 %collective-permute-done.15 = bf16[128,1536]{1,0:T(8,128)(2,1)S(1)} collective-permute-done((bf16[128,1536]{1,0:T(8,128)(2,1)}, bf16[128,1536]{1,0:T(8,128)(2,1)S(1)}, u32[]{:S(2)}, u32[]{:S(2)}) %collective-permute-start.15) | collective-permute-done | bytes 393248 | tf_op jit(solution)/shard_map/ppermute | solution.py:55
  237.2 7.2 %collective-permute-start.17 = (bf16[128,1536]{1,0:T(8,128)(2,1)S(1)}, bf16[128,1536]{1,0:T(8,128)(2,1)S(1)}, u32[]{:S(2)}, u32[]{:S(2)}) collective-permute-start(bf16[128,1536]{1,0:T(8,128)(2,1)S(1)} %get-tuple-element.116), channel_id=1, source_target_pairs={{0,1},{1,0},{2,3},{3,2},{4,5},{5,4},{6,7},{7,6},{8,9},{9,8},{10,11... | collective-permute-start | bytes 1179656 | tf_op jit(solution)/shard_map/ppermute | solution.py:55
  246.9 11.9 %collective-permute-done.17 = bf16[128,1536]{1,0:T(8,128)(2,1)S(1)} collective-permute-done((bf16[128,1536]{1,0:T(8,128)(2,1)S(1)}, bf16[128,1536]{1,0:T(8,128)(2,1)S(1)}, u32[]{:S(2)}, u32[]{:S(2)}) %collective-permute-start.17) | collective-permute-done | bytes 393248 | tf_op jit(solution)/shard_map/ppermute | solution.py:55
  258.8 15.4 %collective-permute-done.18 = bf16[128,1536]{1,0:T(8,128)(2,1)S(1)} collective-permute-done((bf16[128,1536]{1,0:T(8,128)(2,1)S(1)}, bf16[128,1536]{1,0:T(8,128)(2,1)S(1)}, u32[]{:S(2)}, u32[]{:S(2)}) %collective-permute-start.18) | collective-permute-done | bytes 393248 | tf_op jit(solution)/shard_map/ppermute | solution.py:55
  277.3 5.2 %convolution_convert_fusion.2 = bf16[1536,1024]{1,0:T(8,128)(2,1)} fusion(bf16[512,1536]{1,0:T(8,128)(2,1)} %copy-done.17, bf16[512,1024]{1,0:T(8,128)(2,1)} %get-tuple-element.66), kind=kOutput, calls=%fused_computation.2 | convolution fusion | flops 1612185600 | bytes 5767168 | tf_op jit(solution)/shard_map/dot_general | solution.py:27
  285.3 21.0 %shard_map.223 = (f32[512,384]{1,0:T(8,128)}, f32[512,768]{1,0:T(8,128)}, bf16[512,768]{1,0:T(8,128)(2,1)}, bf16[512,384]{1,0:T(8,128)(2,1)}, f32[8,512]{1,0:T(8,128)}, /*index=5*/f32[8,512]{1,0:T(8,128)}) custom-call(bf16[512,384]{1,0:T(8,128)(2,1)} %get-tuple-element.51.q_ref, bf16[512,768]{1,0:T(8,128)(2,1)} %get-tuple-element.52.kv_ref, ...), custom_call_target="tpu_custom_call" | custom-call | flops 2617245696 | bytes 10424320 | tf_op jit(solution)/shard_map/pallas_call | solution.py:39
  314.5 14.4 %shard_map.224 = (bf16[512,1664]{1,0:T(8,128)(2,1)}, f32[1,128]{1,0:T(1,128)}, f32[1,1536]{1,0:T(1,128)}, f32[2,64]{1,0:T(2,128)}, bf16[128,1536]{1,0:T(8,128)(2...) custom-call(bf16[128,1536]{1,0:T(8,128)(2,1)} %bitcast.39, ...), custom_call_target="tpu_custom_call" | custom-call | flops 2617245696 | bytes 15384064 | tf_op jit(solution)/shard_map/pallas_call | solution.py:39
  328.8 7.5 %convolution_convert_fusion = bf16[1536,1664]{1,0:T(8,128)(2,1)} fusion(bf16[512,1536]{1,0:T(8,128)(2,1)} %get-tuple-element.82, bf16[512,1664]{1,0:T(8,128)(2,1)} %get-tuple-element.83), kind=kOutput, calls=%fused_computation | convolution fusion | flops 2619801600 | bytes 8388608 | tf_op jit(solution)/shard_map/dot_general | solution.py:27
  337.3 6.9 %convolution_convert_fusion.1 = bf16[1536,2048]{1,0:T(8,128)(2,1)} fusion(bf16[512,1024]{1,0:T(8,128)(2,1)} %get-tuple-element.89, bf16[512,1024]{1,0:T(8,128)(2,1)} %get-tuple-element.88, bf16[128,1536]{1,0:T(8,128)(2,1)S(1)} %collective-permute-done.10, bf16[128,1536]{1,0:T(8,128)(2,1)S(1)} %copy-done.13, ...), kind=kOutput, calls=%fused_computation.1 | convolution fusion | flops 3234856960 | bytes 9961472 | tf_op jit(solution)/shard_map/dot_general | solution.py:27
  345.5 3.7 convolution_convert_fusion.3
  349.3 5.9 %collective-permute-start.29 = (f32[3224]{0:T(1024)S(1)}, f32[3224]{0:T(1024)S(1)}, u32[]{:S(2)}, u32[]{:S(2)}) collective-permute-start(f32[3224]{0:T(1024)S(1)} %fusion.28), channel_id=1, source_target_pairs={{0,1},{1,0},{2,3},{3,2},{4,5},{5,4},{6,7},{7,6},{8,9},{9,8},{10,11... | collective-permute-start | bytes 38696 | tf_op jit(solution)/shard_map/ppermute | solution.py:55
  362.2 31.8 %collective-permute-done.30 = f32[3224]{0:T(1024)S(1)} collective-permute-done((f32[3224]{0:T(1024)S(1)}, f32[3224]{0:T(1024)S(1)}, u32[]{:S(2)}, u32[]{:S(2)}) %collective-permute-start.30) | collective-permute-done | bytes 12928 | tf_op jit(solution)/shard_map/ppermute | solution.py:55
  404.8 9.7 %collective-permute-done.25 = bf16[128,1536]{1,0:T(8,128)(2,1)S(1)} collective-permute-done((bf16[128,1536]{1,0:T(8,128)(2,1)}, bf16[128,1536]{1,0:T(8,128)(2,1)S(1)}, u32[]{:S(2)}, u32[]{:S(2)}) %collective-permute-start.25) | collective-permute-done | bytes 393248 | tf_op jit(solution)/shard_map/ppermute | solution.py:55
  414.5 14.8 %collective-permute-done.26 = bf16[128,1536]{1,0:T(8,128)(2,1)S(1)} collective-permute-done((bf16[128,1536]{1,0:T(8,128)(2,1)}, bf16[128,1536]{1,0:T(8,128)(2,1)S(1)}, u32[]{:S(2)}, u32[]{:S(2)}) %collective-permute-start.26) | collective-permute-done | bytes 393248 | tf_op jit(solution)/shard_map/ppermute | solution.py:55
  438.0 54.5 %reduce-scatter.9.cloned.1.call-done = bf16[192,2048]{1,0:T(8,128)(2,1)} async-done(((bf16[1536,2048]{1,0:T(8,128)(2,1)}), bf16[192,2048]{1,0:T(8,128)(2,1)}) %reduce-scatter.9.cloned.1.call-update) | async-done | bytes 786448 | tf_op jit(solution)/shard_map/reduce_scatter | solution.py:391
  492.5 3.3 reshape.89
  (205 shorter events, 80.3 us)
Async XLA Ops:
  7.2 47.3 %all-gather.5.cloned.1.call-start = ((), (), s32[]{:S(2)}) async-start(), calls=%async_computation.4 | async-start | bytes 5750784 | tf_op jit(solution)/shard_map/all_gather | solution.py:324
  11.1 69.4 %all-gather.7.cloned.1.call-start = ((), (), s32[]{:S(2)}) async-start(), calls=%async_computation.5 | async-start | bytes 1327104 | tf_op jit(solution)/shard_map/all_gather | solution.py:325
  11.8 171.3 %all-gather.11.cloned.1.call-start = ((), (), s32[]{:S(2)}) async-start(), calls=%async_computation.7 | async-start | bytes 3538944 | tf_op jit(solution)/shard_map/all_gather | solution.py:327
  12.6 170.5 %all-gather.9.cloned.1.call-start = ((), (), s32[]{:S(2)}) async-start(), calls=%async_computation.6 | async-start | bytes 7077888 | tf_op jit(solution)/shard_map/all_gather | solution.py:326
  13.8 417.1 %reduce-scatter.7.cloned.1.call-start = ((), (), s32[]{:S(2)}) async-start(), calls=%async_computation.9 | async-start | bytes 1327104 | tf_op jit(solution)/shard_map/reduce_scatter | solution.py:391
  13.8 19.9 %collective-permute-start = (bf16[128,1536]{1,0:T(8,128)(2,1)S(1)}, bf16[128,1536]{1,0:T(8,128)(2,1)S(1)}, u32[]{:S(2)}, u32[]{:S(2)}) collective-permute-start(bf16[128,1536]{1,0:T(8,128)(2,1)S(1)} %bitcast.40), channel_id=1, source_target_pairs={{0,1},{1,0},{2,3},{3,2},{4,5},{5,4},{6,7},{7,6},{8,9},{9,8},{10,11... | collective-permute-start | bytes 1179656 | tf_op jit(solution)/shard_map/ppermute | solution.py:55
  16.9 29.8 %collective-permute-start.1 = (bf16[128,1536]{1,0:T(8,128)(2,1)S(1)}, bf16[128,1536]{1,0:T(8,128)(2,1)S(1)}, u32[]{:S(2)}, u32[]{:S(2)}) collective-permute-start(bf16[128,1536]{1,0:T(8,128)(2,1)S(1)} %bitcast.41), channel_id=1, source_target_pairs={{0,2},{1,3},{2,0},{3,1},{4,6},{5,7},{6,4},{7,5},{8,10},{9,11},{10,... | collective-permute-start | bytes 1179656 | tf_op jit(solution)/shard_map/ppermute | solution.py:55
  19.5 27.2 %collective-permute-start.2 = (bf16[128,1536]{1,0:T(8,128)(2,1)S(1)}, bf16[128,1536]{1,0:T(8,128)(2,1)S(1)}, u32[]{:S(2)}, u32[]{:S(2)}) collective-permute-start(bf16[128,1536]{1,0:T(8,128)(2,1)S(1)} %bitcast.42), channel_id=1, source_target_pairs={{0,3},{1,2},{2,1},{3,0},{4,7},{5,6},{6,5},{7,4},{8,11},{9,10},{10,... | collective-permute-start | bytes 1179656 | tf_op jit(solution)/shard_map/ppermute | solution.py:55
  70.0 26.7 %collective-permute-start.11 = (bf16[128,1536]{1,0:T(8,128)(2,1)S(1)}, bf16[128,1536]{1,0:T(8,128)(2,1)S(1)}, u32[]{:S(2)}, u32[]{:S(2)}) collective-permute-start(bf16[128,1536]{1,0:T(8,128)(2,1)S(1)} %fusion.12), channel_id=1, source_target_pairs={{0,1},{1,0},{2,3},{3,2},{4,5},{5,4},{6,7},{7,6},{8,9},{9,8},{10,11... | collective-permute-start | bytes 1179656 | tf_op jit(solution)/shard_map/ppermute | solution.py:55
  71.6 80.6 %collective-permute-start.12 = (bf16[128,1536]{1,0:T(8,128)(2,1)S(1)}, bf16[128,1536]{1,0:T(8,128)(2,1)S(1)}, u32[]{:S(2)}, u32[]{:S(2)}) collective-permute-start(bf16[128,1536]{1,0:T(8,128)(2,1)S(1)} %fusion.12), channel_id=1, source_target_pairs={{0,2},{1,3},{2,0},{3,1},{4,6},{5,7},{6,4},{7,5},{8,10},{9,11},{10,... | collective-permute-start | bytes 1179656 | tf_op jit(solution)/shard_map/ppermute | solution.py:55
  92.2 19.4 %collective-permute-start.5 = (bf16[128,1536]{1,0:T(8,128)(2,1)}, bf16[128,1536]{1,0:T(8,128)(2,1)S(1)}, u32[]{:S(2)}, u32[]{:S(2)}) collective-permute-start(bf16[128,1536]{1,0:T(8,128)(2,1)} %get-tuple-element.57), channel_id=1, source_target_pairs={{0,1},{1,0},{2,3},{3,2},{4,5},{5,4},{6,7},{7,6},{8,9},{9,8},{10,11... | collective-permute-start | bytes 1179656 | tf_op jit(solution)/shard_map/ppermute | solution.py:55
  93.8 38.4 %collective-permute-start.6 = (bf16[128,1536]{1,0:T(8,128)(2,1)}, bf16[128,1536]{1,0:T(8,128)(2,1)S(1)}, u32[]{:S(2)}, u32[]{:S(2)}) collective-permute-start(bf16[128,1536]{1,0:T(8,128)(2,1)} %get-tuple-element.58), channel_id=1, source_target_pairs={{0,2},{1,3},{2,0},{3,1},{4,6},{5,7},{6,4},{7,5},{8,10},{9,11},{10,... | collective-permute-start | bytes 1179656 | tf_op jit(solution)/shard_map/ppermute | solution.py:55
  96.2 36.0 %collective-permute-start.7 = (bf16[128,1536]{1,0:T(8,128)(2,1)}, bf16[128,1536]{1,0:T(8,128)(2,1)S(1)}, u32[]{:S(2)}, u32[]{:S(2)}) collective-permute-start(bf16[128,1536]{1,0:T(8,128)(2,1)} %get-tuple-element.59), channel_id=1, source_target_pairs={{0,3},{1,2},{2,1},{3,0},{4,7},{5,6},{6,5},{7,4},{8,11},{9,10},{10,... | collective-permute-start | bytes 1179656 | tf_op jit(solution)/shard_map/ppermute | solution.py:55
  96.8 55.5 %collective-permute-start.13 = (bf16[128,1536]{1,0:T(8,128)(2,1)S(1)}, bf16[128,1536]{1,0:T(8,128)(2,1)S(1)}, u32[]{:S(2)}, u32[]{:S(2)}) collective-permute-start(bf16[128,1536]{1,0:T(8,128)(2,1)S(1)} %fusion.12), channel_id=1, source_target_pairs={{0,3},{1,2},{2,1},{3,0},{4,7},{5,6},{6,5},{7,4},{8,11},{9,10},{10,... | collective-permute-start | bytes 1179656 | tf_op jit(solution)/shard_map/ppermute | solution.py:55
  133.2 19.1 %collective-permute-start.10 = (bf16[128,1536]{1,0:T(8,128)(2,1)S(1)}, bf16[128,1536]{1,0:T(8,128)(2,1)S(1)}, u32[]{:S(2)}, u32[]{:S(2)}) collective-permute-start(bf16[128,1536]{1,0:T(8,128)(2,1)S(1)} %multiply_convert_fusion.1), channel_id=1, source_target_pairs={{0,3},{1,2},{2,1},{3,0},{4,7},{5,6},{6,5},{7,4},{8,11},{9,10},{10,... | collective-permute-start | bytes 1179656 | tf_op jit(solution)/shard_map/ppermute | solution.py:55
  135.7 26.1 %collective-permute-start.8 = (bf16[128,1536]{1,0:T(8,128)(2,1)S(1)}, bf16[128,1536]{1,0:T(8,128)(2,1)S(1)}, u32[]{:S(2)}, u32[]{:S(2)}) collective-permute-start(bf16[128,1536]{1,0:T(8,128)(2,1)S(1)} %multiply_convert_fusion.1), channel_id=1, source_target_pairs={{0,1},{1,0},{2,3},{3,2},{4,5},{5,4},{6,7},{7,6},{8,9},{9,8},{10,11... | collective-permute-start | bytes 1179656 | tf_op jit(solution)/shard_map/ppermute | solution.py:55
  152.2 29.6 %collective-permute-start.9 = (bf16[128,1536]{1,0:T(8,128)(2,1)S(1)}, bf16[128,1536]{1,0:T(8,128)(2,1)S(1)}, u32[]{:S(2)}, u32[]{:S(2)}) collective-permute-start(bf16[128,1536]{1,0:T(8,128)(2,1)S(1)} %multiply_convert_fusion.1), channel_id=1, source_target_pairs={{0,2},{1,3},{2,0},{3,1},{4,6},{5,7},{6,4},{7,5},{8,10},{9,11},{10,... | collective-permute-start | bytes 1179656 | tf_op jit(solution)/shard_map/ppermute | solution.py:55
  204.6 30.1 %collective-permute-start.15 = (bf16[128,1536]{1,0:T(8,128)(2,1)}, bf16[128,1536]{1,0:T(8,128)(2,1)S(1)}, u32[]{:S(2)}, u32[]{:S(2)}) collective-permute-start(bf16[128,1536]{1,0:T(8,128)(2,1)} %get-tuple-element.64), channel_id=1, source_target_pairs={{0,2},{1,3},{2,0},{3,1},{4,6},{5,7},{6,4},{7,5},{8,10},{9,11},{10,... | collective-permute-start | bytes 1179656 | tf_op jit(solution)/shard_map/ppermute | solution.py:55
  207.5 27.1 %collective-permute-start.16 = (bf16[128,1536]{1,0:T(8,128)(2,1)}, bf16[128,1536]{1,0:T(8,128)(2,1)S(1)}, u32[]{:S(2)}, u32[]{:S(2)}) collective-permute-start(bf16[128,1536]{1,0:T(8,128)(2,1)} %get-tuple-element.65), channel_id=1, source_target_pairs={{0,3},{1,2},{2,1},{3,0},{4,7},{5,6},{6,5},{7,4},{8,11},{9,10},{10,... | collective-permute-start | bytes 1179656 | tf_op jit(solution)/shard_map/ppermute | solution.py:55
  237.2 21.6 %collective-permute-start.17 = (bf16[128,1536]{1,0:T(8,128)(2,1)S(1)}, bf16[128,1536]{1,0:T(8,128)(2,1)S(1)}, u32[]{:S(2)}, u32[]{:S(2)}) collective-permute-start(bf16[128,1536]{1,0:T(8,128)(2,1)S(1)} %get-tuple-element.116), channel_id=1, source_target_pairs={{0,1},{1,0},{2,3},{3,2},{4,5},{5,4},{6,7},{7,6},{8,9},{9,8},{10,11... | collective-permute-start | bytes 1179656 | tf_op jit(solution)/shard_map/ppermute | solution.py:55
  244.4 29.8 %collective-permute-start.18 = (bf16[128,1536]{1,0:T(8,128)(2,1)S(1)}, bf16[128,1536]{1,0:T(8,128)(2,1)S(1)}, u32[]{:S(2)}, u32[]{:S(2)}) collective-permute-start(bf16[128,1536]{1,0:T(8,128)(2,1)S(1)} %get-tuple-element.116), channel_id=1, source_target_pairs={{0,2},{1,3},{2,0},{3,1},{4,6},{5,7},{6,4},{7,5},{8,10},{9,11},{10,... | collective-permute-start | bytes 1179656 | tf_op jit(solution)/shard_map/ppermute | solution.py:55
  245.4 28.8 %collective-permute-start.19 = (bf16[128,1536]{1,0:T(8,128)(2,1)S(1)}, bf16[128,1536]{1,0:T(8,128)(2,1)S(1)}, u32[]{:S(2)}, u32[]{:S(2)}) collective-permute-start(bf16[128,1536]{1,0:T(8,128)(2,1)S(1)} %get-tuple-element.116), channel_id=1, source_target_pairs={{0,3},{1,2},{2,1},{3,0},{4,7},{5,6},{6,5},{7,4},{8,11},{9,10},{10,... | collective-permute-start | bytes 1179656 | tf_op jit(solution)/shard_map/ppermute | solution.py:55
  277.2 155.3 %reduce-scatter.11.cloned.1.call-start = ((), (), s32[]{:S(2)}) async-start(), calls=%async_computation.11 | async-start | bytes 3538944 | tf_op jit(solution)/shard_map/reduce_scatter | solution.py:391
  282.5 152.0 %reduce-scatter.5.cloned.1.call-start = ((), (), s32[]{:S(2)}) async-start(), calls=%async_computation.8 | async-start | bytes 5750784 | tf_op jit(solution)/shard_map/reduce_scatter | solution.py:391
  336.3 156.2 %reduce-scatter.9.cloned.1.call-start = ((), (), s32[]{:S(2)}) async-start(), calls=%async_computation.10 | async-start | bytes 7077888 | tf_op jit(solution)/shard_map/reduce_scatter | solution.py:391
  355.4 40.8 %collective-permute-start.20 = (bf16[128,1536]{1,0:T(8,128)(2,1)S(1)}, bf16[128,1536]{1,0:T(8,128)(2,1)S(1)}, u32[]{:S(2)}, u32[]{:S(2)}) collective-permute-start(bf16[128,1536]{1,0:T(8,128)(2,1)S(1)} %get-tuple-element.120), channel_id=1, source_target_pairs={{0,1},{1,0},{2,3},{3,2},{4,5},{5,4},{6,7},{7,6},{8,9},{9,8},{10,11... | collective-permute-start | bytes 1179656 | tf_op jit(solution)/shard_map/ppermute | solution.py:55
  355.4 42.1 %collective-permute-start.21 = (bf16[128,1536]{1,0:T(8,128)(2,1)S(1)}, bf16[128,1536]{1,0:T(8,128)(2,1)S(1)}, u32[]{:S(2)}, u32[]{:S(2)}) collective-permute-start(bf16[128,1536]{1,0:T(8,128)(2,1)S(1)} %get-tuple-element.122), channel_id=1, source_target_pairs={{0,2},{1,3},{2,0},{3,1},{4,6},{5,7},{6,4},{7,5},{8,10},{9,11},{10,... | collective-permute-start | bytes 1179656 | tf_op jit(solution)/shard_map/ppermute | solution.py:55
  358.4 39.2 %collective-permute-start.22 = (bf16[128,1536]{1,0:T(8,128)(2,1)S(1)}, bf16[128,1536]{1,0:T(8,128)(2,1)S(1)}, u32[]{:S(2)}, u32[]{:S(2)}) collective-permute-start(bf16[128,1536]{1,0:T(8,128)(2,1)S(1)} %get-tuple-element.121), channel_id=1, source_target_pairs={{0,3},{1,2},{2,1},{3,0},{4,7},{5,6},{6,5},{7,4},{8,11},{9,10},{10,... | collective-permute-start | bytes 1179656 | tf_op jit(solution)/shard_map/ppermute | solution.py:55
  359.8 34.2 %collective-permute-start.30 = (f32[3224]{0:T(1024)S(1)}, f32[3224]{0:T(1024)S(1)}, u32[]{:S(2)}, u32[]{:S(2)}) collective-permute-start(f32[3224]{0:T(1024)S(1)} %fusion.28), channel_id=1, source_target_pairs={{0,2},{1,3},{2,0},{3,1},{4,6},{5,7},{6,4},{7,5},{8,10},{9,11},{10,... | collective-permute-start | bytes 38696 | tf_op jit(solution)/shard_map/ppermute | solution.py:55
  359.9 34.1 %collective-permute-start.31 = (f32[3224]{0:T(1024)S(1)}, f32[3224]{0:T(1024)S(1)}, u32[]{:S(2)}, u32[]{:S(2)}) collective-permute-start(f32[3224]{0:T(1024)S(1)} %fusion.28), channel_id=1, source_target_pairs={{0,3},{1,2},{2,1},{3,0},{4,7},{5,6},{6,5},{7,4},{8,11},{9,10},{10,... | collective-permute-start | bytes 38696 | tf_op jit(solution)/shard_map/ppermute | solution.py:55
  399.3 30.0 %collective-permute-start.26 = (bf16[128,1536]{1,0:T(8,128)(2,1)}, bf16[128,1536]{1,0:T(8,128)(2,1)S(1)}, u32[]{:S(2)}, u32[]{:S(2)}) collective-permute-start(bf16[128,1536]{1,0:T(8,128)(2,1)} %get-tuple-element.80), channel_id=1, source_target_pairs={{0,2},{1,3},{2,0},{3,1},{4,6},{5,7},{6,4},{7,5},{8,10},{9,11},{10,... | collective-permute-start | bytes 1179656 | tf_op jit(solution)/shard_map/ppermute | solution.py:55
  401.6 27.7 %collective-permute-start.27 = (bf16[128,1536]{1,0:T(8,128)(2,1)S(1)}, bf16[128,1536]{1,0:T(8,128)(2,1)S(1)}, u32[]{:S(2)}, u32[]{:S(2)}) collective-permute-start(bf16[128,1536]{1,0:T(8,128)(2,1)S(1)} %copy-done.31), channel_id=1, source_target_pairs={{0,3},{1,2},{2,1},{3,0},{4,7},{5,6},{6,5},{7,4},{8,11},{9,10},{10,... | collective-permute-start | bytes 1179656 | tf_op jit(solution)/shard_map/ppermute | solution.py:55
  (48 other events, 868.6 us)
Sparse Core Ops, SparseCore 0:
  11.2 43.2 all-gather.4
  56.4 24.0 all-gather.6
  82.4 32.3 all-gather.10
  116.4 45.5 all-gather.8
  277.4 40.2 reduce-scatter.6
  321.3 46.2 reduce-scatter.10
  371.1 56.2 reduce-scatter.4
  430.8 61.7 reduce-scatter.8

commit v2 on v1

v2 whole, which is shorter than its diff:
```python
import functools
import math

import jax
import jax.numpy as jnp
from jax import lax
from jax.experimental import pallas as pl
from jax.experimental.pallas import tpu as pltpu
from jax.sharding import PartitionSpec as P

epsilon = 1e-06
f32 = jnp.float32
bf16 = jnp.bfloat16
BIG = 1e30
VMEM_LIMIT = 60 * 1024 * 1024


def mm(left, right):
    return jnp.dot(left, right, preferred_element_type=f32)


def mm_nt(left, right):
    return lax.dot_general(left, right, (((1,), (1,)), ((), ())), preferred_element_type=f32)


def mm_tn(left, right):
    return lax.dot_general(left, right, (((0,), (0,)), ((), ())), preferred_element_type=f32)


def whole(shape):
    return pl.BlockSpec(shape, lambda *_: (0,) * len(shape))


def call(kernel, outs, *operands, grid=None, in_specs=None, out_specs=None, scratch=(), blocks=None, places=None,
         weight=0.1):
    extra = {}
    if grid is None and blocks:
        grid = (1,)
        places = places or {}
        in_specs = [
            pl.BlockSpec(blocks.get(i, o.shape), functools.partial(lambda at, *_: at, places.get(i, (0,) * o.ndim)))
            for i, o in enumerate(operands)
        ]
        out_specs = [whole(o.shape) for o in outs]
    if grid is not None:
        extra = dict(grid=grid, in_specs=in_specs, out_specs=out_specs)
    return pl.pallas_call(
        kernel,
        out_shape=outs,
        scratch_shapes=list(scratch),
        compiler_params=pltpu.CompilerParams(vmem_limit_bytes=VMEM_LIMIT),
        cost_estimate=pl.CostEstimate(flops=int(weight * 1e9), bytes_accessed=int(weight * 1e6), transcendentals=0),
        **extra,
    )(*operands)


def sds(shape, dtype):
    return jax.ShapeDtypeStruct(shape, dtype)


def swap(value, axis, bit):
    n = lax.axis_size(axis)
    return lax.ppermute(value, axis, [(j, j ^ bit) for j in range(n)])


def gather_rows(own):
    n = lax.axis_size("tp")
    return [own] + [swap(own, "tp", k) for k in range(1, n)]


def send_rows(parts):
    n = lax.axis_size("tp")
    return [parts[0]] + [swap(parts[k], "tp", k) for k in range(1, n)]


def gather_all(own):
    n = lax.axis_size("tp")
    return lax.all_to_all(jnp.broadcast_to(own[None], (n,) + own.shape), "tp", 0, 0, tiled=True)


def after(value, *others):
    return lax.optimization_barrier((value, others))[0]


def pick(value, index, axis=0):
    return lax.dynamic_index_in_dim(value, index, axis, keepdims=False)


def scatter_weight(part):
    shards, halves = lax.axis_size("shard"), lax.axis_size("ctx")
    me, half = lax.axis_index("shard"), lax.axis_index("ctx")
    width, cols = part.shape
    blocks = part.reshape(shards, halves, width // (shards * halves), cols)
    got = swap(pick(blocks, 1 - half, 1), "ctx", 1)
    keep = pick(blocks, half, 1)

    def pair(k):
        return pick(keep, me ^ k).astype(f32) + pick(got, me ^ k).astype(f32)

    arrived = [swap(pair(k).astype(bf16), "shard", k) for k in range(1, shards)]
    return pair(0), arrived


def finish_weight(state):
    own, arrived = state
    for g in arrived:
        own = own + g.astype(f32)
    return own


def sum_over(value, axes):
    for axis in axes:
        n = lax.axis_size(axis)
        total = value
        for k in range(1, n):
            total = total + swap(value, axis, k)
        value = total
    return value


def thirds(value):
    high = value.astype(bf16)
    rest = value - high.astype(f32)
    middle = rest.astype(bf16)
    return high, middle, (rest - middle.astype(f32)).astype(bf16)


def head_sums(value, size):
    cols = value.shape[1]
    shape = (cols, cols)
    row = lax.broadcasted_iota(jnp.int32, shape, 0) // size
    col = lax.broadcasted_iota(jnp.int32, shape, 1) // size
    same = (row == col).astype(bf16)
    high = value.astype(bf16)
    low = (value - high.astype(f32)).astype(bf16)
    return mm(high, same) + mm(low, same)


def spread(pieces, rows):
    used = sum(p.shape[1] for p in pieces)
    return jnp.concatenate(list(pieces) + [jnp.zeros((rows, 128 - used), bf16)], axis=1)


def running(mask, value, heads):
    rows = value.shape[0]
    parts = thirds(value[:, :heads])
    total = mm(mask, spread(parts, rows))
    return total[:, :heads] + total[:, heads : 2 * heads] + total[:, 2 * heads : 3 * heads]


def project_kernel(heads, size, chunks, *refs):
    x_refs, refs = refs[:chunks], refs[chunks:]
    w_ref, gain_ref, qk_ref, bias_ref, rank_ref, rank_t_ref = refs[:6]
    (normed_ref, qa_ref, ka_ref, va_ref, send_ref, qraw_ref, kraw_ref, open_ref, pre_ref, cum_ref) = refs[6:]
    rows = x_refs[0].shape[0]
    span = rows * chunks
    cols = heads * size
    gain = gain_ref[...]
    for c in range(chunks):
        x = x_refs[c][...].astype(f32)
        r = lax.rsqrt(jnp.mean(x * x, axis=1, keepdims=True) + epsilon)
        normed_ref[c * rows : (c + 1) * rows, :] = (x * r * gain).astype(bf16)
    normed = normed_ref[...]
    pre = mm(normed, w_ref[:, 4 * cols : 4 * cols + 128]) + bias_ref[...]
    pre_ref[...] = pre
    logs = jnp.minimum(pre, 0.0) - jnp.log(1.0 + jnp.exp(-jnp.abs(pre)))
    earlier = (rank_t_ref[...] <= rank_ref[...]).astype(bf16)
    cum = running(earlier, logs, heads)
    cum_ref[...] = jnp.concatenate([cum, jnp.zeros((span, 128 - heads), f32)], axis=1)
    ones = jnp.ones((span, 3), bf16)
    fill = jnp.zeros((span, 128 - size - 6), bf16)
    cums = thirds(cum)
    outs = thirds(-cum)
    fars = thirds(jnp.sum(logs[:, :heads], axis=0, keepdims=True) - cum)

    def at(parts, h):
        return [p[:, h : h + 1] for p in parts]

    for which, raw_ref in ((0, qraw_ref), (1, kraw_ref)):
        raw = mm(normed, w_ref[:, (which + 1) * cols : (which + 2) * cols])
        raw_ref[...] = raw
        r = lax.rsqrt(head_sums(raw * raw, size) * (1.0 / size) + epsilon)
        value = (raw * r * qk_ref[which : which + 1, :]).astype(bf16)
        if which == 0:
            value = value * jnp.asarray(1.0 / math.sqrt(size), bf16)
            for h in range(heads):
                piece = value[:, h * size : (h + 1) * size]
                qa_ref[:, h * 128 : (h + 1) * 128] = jnp.concatenate([piece] + at(cums, h) + [ones, fill], axis=1)
        else:
            send_ref[:, 0:cols] = value
            for h in range(heads):
                piece = value[:, h * size : (h + 1) * size]
                ka_ref[:, h * 128 : (h + 1) * 128] = jnp.concatenate([piece, ones] + at(outs, h) + [fill], axis=1)
    value = mm(normed, w_ref[:, 3 * cols : 4 * cols]).astype(bf16)
    send_ref[:, cols : 2 * cols] = value
    tail = jnp.concatenate([ones, jnp.zeros((span, 128 - size - 3), bf16)], axis=1)
    for h in range(heads):
        va_ref[:, h * 128 : (h + 1) * 128] = jnp.concatenate([value[:, h * size : (h + 1) * size], tail], axis=1)
    send_ref[:, 2 * cols :] = spread(fars, span)
    open_ref[...] = jax.nn.sigmoid(mm(normed, w_ref[:, 4 * cols + 128 :]))


def attend_kernel(heads, size, qa_ref, ka_ref, va_ref, left_ref, open_ref, rank_ref, rank_t_ref, wout_ref,
                  gated_ref, att_ref, lse_ref, kl_ref, vl_ref, *branch_refs):
    cols = heads * size
    rows = qa_ref.shape[0]
    chunks = len(branch_refs)
    step = rows // chunks
    keep = rank_t_ref[...] <= rank_ref[...]
    shut = jnp.where(lax.axis_index("ctx") == 0, -BIG, 0.0).astype(bf16)
    ones = jnp.ones((rows, 3), bf16)
    fill = jnp.zeros((rows, 128 - size - 6), bf16)
    tail = jnp.zeros((rows, 128 - size - 3), bf16)
    lses = []
    for h in range(heads):
        wide = slice(h * 128, (h + 1) * 128)
        hs = slice(h * size, (h + 1) * size)
        far = [left_ref[:, 2 * cols + i * heads + h : 2 * cols + i * heads + h + 1] for i in range(3)]
        kl = jnp.concatenate([left_ref[:, hs], ones, far[0] + shut, far[1], far[2], fill], axis=1)
        vl = jnp.concatenate([left_ref[:, cols + h * size : cols + (h + 1) * size], ones, tail], axis=1)
        kl_ref[:, wide] = kl
        vl_ref[:, wide] = vl
        q = qa_ref[:, wide]
        el = jnp.exp(mm_nt(q, kl)).astype(bf16)
        er = jnp.exp(jnp.where(keep, mm_nt(q, ka_ref[:, wide]), -BIG)).astype(bf16)
        o = mm(el, vl) + mm(er, va_ref[:, wide])
        total = o[:, size : size + 1]
        att = o[:, :size] / total
        att_ref[:, hs] = att
        gated_ref[:, hs] = (att * open_ref[:, hs]).astype(bf16)
        lses.append(jnp.log(total))
    lse_ref[...] = jnp.concatenate(lses + [jnp.zeros((rows, 128 - heads), f32)], axis=1)
    branch = mm_nt(gated_ref[...], wout_ref[...]).astype(bf16)
    for c in range(chunks):
        branch_refs[c][...] = branch[c * step : (c + 1) * step, :]


def hidden_back_kernel(chunks, cot_ref, wd_ref, dh_ref, order_ref):
    me = lax.axis_index("tp")
    rows = cot_ref.shape[1]

    @pl.when(pl.program_id(0) == 0)
    def _():
        for c in range(chunks):
            order_ref[c * rows : (c + 1) * rows, :] = cot_ref[pl.ds(me ^ c, 1)][0]

    dh_ref[...] = mm(order_ref[...], wd_ref[...])


def ffn_kernel(steps, chunks, *refs):
    nm_refs, refs = refs[:chunks], refs[chunks:]
    dh_ref, wg_ref, wu_ref, nm_ref, hid_ref, dgu_ref = refs[:6]
    p_refs, refs = refs[6 : 6 + chunks], refs[6 + chunks :]
    w_all = refs[0]
    rows = nm_refs[0].shape[0]
    tile = wg_ref.shape[1]
    units = tile * steps
    j = pl.program_id(0)

    @pl.when(j == 0)
    def _():
        for c in range(chunks):
            nm_ref[c * rows : (c + 1) * rows, :] = nm_refs[c][...]

    gate = mm(nm_ref[...], wg_ref[...])
    up = mm(nm_ref[...], wu_ref[...])
    dh = dh_ref[...]
    sig = jax.nn.sigmoid(gate)
    act = gate * sig
    hid_ref[...] = (act * up).astype(bf16)
    dg = (dh * up * sig * (1.0 + gate * (1.0 - sig))).astype(bf16)
    du = (dh * act).astype(bf16)
    for s in range(steps):

        @pl.when(j == s)
        def _():
            at, up_at = slice(s * tile, (s + 1) * tile), slice(units + s * tile, units + (s + 1) * tile)
            dgu_ref[:, at] = dg
            dgu_ref[:, up_at] = du
            w_all[:, at] = wg_ref[...]
            w_all[:, up_at] = wu_ref[...]

    @pl.when(j == steps - 1)
    def _():
        width = w_all.shape[0]
        for b in range(0, width, 256):
            part = mm_nt(dgu_ref[...], w_all[b : b + 256, :]).astype(bf16)
            for c in range(chunks):
                p_refs[c][:, b : b + 256] = part[c * rows : (c + 1) * rows, :]


def down_kernel(chunks, hid_ref, wd_ref, out_ref):
    me = lax.axis_index("tp")
    down = mm_nt(hid_ref[...], wd_ref[...]).astype(bf16)
    rows = out_ref.shape[1]
    for c in range(chunks):
        out_ref[pl.ds(me ^ c, 1)] = down[c * rows : (c + 1) * rows, :][None]


def attend_back_kernel(heads, size, chunks, *refs):
    db_refs, refs = refs[:chunks], refs[chunks:]
    (qa_ref, ka_ref, va_ref, kl_ref, vl_ref, cum_ref, lse_ref, open_ref, att_ref, rank_ref, rank_t_ref,
     wout_ref) = refs[:12]
    branch_ref, dq_ref, dk_ref, dv_ref, back_ref, dopen_ref, dcum_ref = refs[12:]
    cols = heads * size
    part = db_refs[0].shape[0]
    rows = part * chunks
    for c in range(chunks):
        branch_ref[c * part : (c + 1) * part, :] = db_refs[c][...]
    keep = rank_t_ref[...] >= rank_ref[...]
    dg = mm(branch_ref[...], wout_ref[...])
    op = open_ref[...]
    att = att_ref[...]
    dopen_ref[...] = (dg * att * op * (1.0 - op)).astype(bf16)
    da_all = (dg * op).astype(bf16)
    prod = da_all.astype(f32) * att
    place = thirds(cum_ref[:, :heads] - lse_ref[:, :heads])
    ones = jnp.ones((rows, 3), bf16)
    fill = jnp.zeros((rows, 128 - size - 6), bf16)
    tail = jnp.zeros((rows, 128 - size - 3), bf16)
    owns, lefts = [], []
    for h in range(heads):
        wide = slice(h * 128, (h + 1) * 128)
        hs = slice(h * size, (h + 1) * size)
        vs = slice(cols + h * size, cols + (h + 1) * size)
        q = jnp.concatenate([qa_ref[:, h * 128 : h * 128 + size]] + [p[:, h : h + 1] for p in place] + [ones, fill], axis=1)
        delta = thirds(-jnp.sum(prod[:, hs], axis=1, keepdims=True))
        da = jnp.concatenate([da_all[:, hs], delta[0], delta[1], delta[2], tail], axis=1)
        dq = jnp.zeros((rows, 128), f32)
        found = []
        for k_ref, v_ref, right in ((kl_ref, vl_ref, False), (ka_ref, va_ref, True)):
            k, v = k_ref[:, wide], v_ref[:, wide]
            score = mm_nt(k, q)
            if right:
                score = jnp.where(keep, score, -BIG)
            p = jnp.exp(score)
            ds = (p * mm_nt(v, da)).astype(bf16)
            found += [mm(p.astype(bf16), da)[:, :size], mm(ds, q)]
            dq = dq + mm_tn(ds, k)
        dq_ref[:, hs] = dq[:, :size] * (1.0 / math.sqrt(size))
        back_ref[:, vs] = found[0].astype(bf16)
        back_ref[:, hs] = found[1][:, :size].astype(bf16)
        dv_ref[:, hs] = found[2]
        dk_ref[:, hs] = found[3][:, :size]
        lefts.append(-found[1][:, size + 3 : size + 4])
        owns.append(dq[:, size : size + 1] - found[3][:, size + 3 : size + 4])
    own = jnp.concatenate(owns, axis=1)
    dcum_ref[...] = jnp.concatenate([own, jnp.zeros((rows, 128 - heads), f32)], axis=1)
    total = jnp.broadcast_to(jnp.sum(own, axis=0, keepdims=True), (rows, heads))
    sent = thirds(jnp.concatenate(lefts, axis=1)) + thirds(total)
    back_ref[:, 2 * cols :] = spread(sent, rows)


def project_back_kernel(heads, size, chunks, *refs):
    x_refs, refs = refs[:chunks], refs[chunks:]
    (w_ref, qk_ref, qraw_ref, kraw_ref, dq_ref, dk_ref, dv_ref, back_ref, dopen_ref, dcum_ref, pre_ref, rank_ref,
     rank_t_ref, gm_ref) = refs[:14]
    mixed_ref, out_refs = refs[14], refs[15:]
    cols = heads * size
    width = x_refs[0].shape[1]
    rows = x_refs[0].shape[0]
    span = rows * chunks
    sums = []
    for which, raw_ref in ((0, qraw_ref), (1, kraw_ref)):
        d = dq_ref[...] if which == 0 else dk_ref[...] + back_ref[:, :cols].astype(f32)
        raw = raw_ref[...]
        r = lax.rsqrt(head_sums(raw * raw, size) * (1.0 / size) + epsilon)
        u = raw * r
        total = jnp.sum(d * u, axis=0, keepdims=True)
        sums.append(sum(total[:, h * size : (h + 1) * size] for h in range(heads)))
        e = d * qk_ref[which : which + 1, :]
        mixed_ref[:, which * cols : (which + 1) * cols] = (
            r * (e - u * (head_sums(e * u, size) * (1.0 / size)))
        ).astype(bf16)
    mixed_ref[:, 2 * cols : 3 * cols] = (dv_ref[...] + back_ref[:, cols : 2 * cols].astype(f32)).astype(bf16)
    mixed_ref[:, 3 * cols + 128 :] = dopen_ref[...]
    extra = back_ref[:, 2 * cols :].astype(f32)
    got = extra[:, :heads] + extra[:, heads : 2 * heads] + extra[:, 2 * heads : 3 * heads]
    after_sum = extra[:, 3 * heads : 4 * heads] + extra[:, 4 * heads : 5 * heads] + extra[:, 5 * heads : 6 * heads]
    later = (rank_t_ref[...] >= rank_ref[...]).astype(bf16)
    dlog = running(later, dcum_ref[:, :heads] + got, heads) + after_sum
    df = jnp.concatenate([dlog, jnp.zeros((span, 128 - heads), f32)], axis=1) * jax.nn.sigmoid(-pre_ref[...])
    bias = jnp.sum(df, axis=0, keepdims=True)
    mixed_ref[:, 3 * cols : 3 * cols + 128] = df.astype(bf16)
    gain = jnp.zeros((1, width), f32)
    lows = []
    for c in range(chunks):
        at = slice(c * rows, (c + 1) * rows)
        dn = mm_nt(mixed_ref[at, :], w_ref[:, cols:])
        out_refs[c][0:rows, :] = dn.astype(bf16)
        x = x_refs[c][...].astype(f32)
        r = lax.rsqrt(jnp.mean(x * x, axis=1, keepdims=True) + epsilon)
        gain = gain + jnp.sum(dn * (x * r), axis=0, keepdims=True)
    lanes = jnp.concatenate([sums[0], sums[1], bias, jnp.zeros((1, width - 2 * size - 128), f32)], axis=1)
    low = jnp.concatenate([gain, lanes, gm_ref[...], jnp.zeros((13, width), f32)], axis=0).astype(bf16)
    for c in range(chunks):
        out_refs[c][rows : rows + 16, :] = low


def middle_kernel(chunks, x_ref, gain_ref, *refs):
    middle = x_ref[...].astype(f32)
    for c in range(chunks):
        middle = middle + refs[c][...].astype(f32)
    mid_ref, nm_ref = refs[chunks:]
    mid_ref[...] = middle
    r = lax.rsqrt(jnp.mean(middle * middle, axis=1, keepdims=True) + epsilon)
    nm_ref[...] = (middle * r * gain_ref[...]).astype(bf16)


def norm_back(d, v, gain):
    r = lax.rsqrt(jnp.mean(v * v, axis=1, keepdims=True) + epsilon)
    u = v * r
    e = d * gain
    return r * (e - u * jnp.mean(e * u, axis=1, keepdims=True)), jnp.sum(d * u, axis=0, keepdims=True)


def middle_back_kernel(chunks, mid_ref, cot_ref, gain_ref, *refs):
    d = refs[0][...].astype(f32)
    for c in range(1, chunks):
        d = d + refs[c][...].astype(f32)
    dmid_ref, branch_ref, part_ref = refs[chunks:]
    back, part = norm_back(d, mid_ref[...], gain_ref[...])
    back = back + cot_ref[...].astype(f32)
    dmid_ref[...] = back
    branch_ref[...] = back.astype(bf16)
    part_ref[...] = part


def input_back_kernel(chunks, x_ref, dmid_ref, gain_ref, *refs):
    rows = x_ref.shape[0]
    d = refs[0][...].astype(f32)
    for c in range(1, chunks):
        d = d + refs[c][...].astype(f32)
    back, _ = norm_back(d[0:rows, :], x_ref[...].astype(f32), gain_ref[...])
    refs[chunks][...] = (back + dmid_ref[...]).astype(bf16)
    refs[chunks + 1][...] = d[rows:, :]


def body(tokens, cotangent, lengths, w_qkv, w_forget, forget_bias, w_ogate, w_out, w_gu, w_down, gain_attn, gain_mlp,
         qk_gain):
    slots, rows, width = tokens.shape
    assert slots == 1
    n = lax.axis_size("tp")
    me = lax.axis_index("tp")
    half = lax.axis_index("ctx")
    both = ("shard", "ctx")
    span = rows * n
    heads = w_forget.shape[1]
    size = qk_gain.shape[1]
    cols = heads * size
    units = w_down.shape[1]
    slab = w_qkv.shape[0]

    x_own = tokens[0]
    x_parts = gather_rows(x_own)

    own_pos = half * span + me * rows + jnp.arange(rows, dtype=jnp.int32)
    valid = (own_pos < lengths[0]).astype(f32)[:, None]
    cot_own = (cotangent[0].astype(f32) * valid).astype(bf16)
    cot = gather_all(after(cot_own, *x_parts))

    order = jnp.concatenate([(me ^ k) * rows + jnp.arange(rows, dtype=jnp.int32) for k in range(n)])
    rank, rank_t = order[:, None], order[None, :]

    first = jnp.concatenate(
        [w_out, w_qkv.reshape(slab, 3 * cols), w_forget, jnp.zeros((slab, 128 - heads), bf16), w_ogate], axis=1
    )
    first = lax.all_gather(first, both, axis=0, tiled=True)
    rest = jnp.concatenate([w_gu.reshape(slab, 2 * units), w_down], axis=1)
    rest = lax.all_gather(rest, both, axis=0, tiled=True)
    wide = 4 * cols + 128
    w_out_full, out_block = first, (width, cols)
    if cols % 128:
        w_out_full = first[:, :cols]

    bias = lax.dynamic_slice_in_dim(forget_bias, me * heads, heads)
    bias = jnp.concatenate([bias, jnp.zeros((128 - heads,), f32)])[None, :]
    gain_a, gain_m = gain_attn[None, :], gain_mlp[None, :]
    qk_wide = jnp.tile(qk_gain, (1, heads))

    normed, qa, ka, va, sent, qraw, kraw, opener, pre, cum = call(
        functools.partial(project_kernel, heads, size, n),
        [
            sds((span, width), bf16),
            sds((span, heads * 128), bf16),
            sds((span, heads * 128), bf16),
            sds((span, heads * 128), bf16),
            sds((span, 2 * cols + 128), bf16),
            sds((span, cols), f32),
            sds((span, cols), f32),
            sds((span, cols), f32),
            sds((span, 128), f32),
            sds((span, 128), f32),
        ],
        *x_parts, first, gain_a, qk_wide, bias, rank, rank_t,
    )
    left = lax.ppermute(sent, "ctx", [(0, 1)])
    gated, attended, lse, kl, vl, *branch = call(
        functools.partial(attend_kernel, heads, size),
        [sds((span, cols), bf16), sds((span, cols), f32), sds((span, 128), f32)]
        + [sds((span, heads * 128), bf16)] * 2
        + [sds((rows, width), bf16)] * n,
        qa, ka, va, left, opener, rank, rank_t, w_out_full,
        blocks={7: out_block},
    )
    tile = min(512, units)
    steps = units // tile
    d_hidden, cot = call(
        functools.partial(hidden_back_kernel, n),
        [sds((span, units), f32), sds((span, width), bf16)],
        after(cot, branch), rest,
        grid=(steps,),
        in_specs=[whole((n, rows, width)), pl.BlockSpec((width, tile), lambda j: (0, j + 2 * steps))],
        out_specs=[pl.BlockSpec((span, tile), lambda j: (0, j)), whole((span, width))],
    )
    middle, nm_own = call(
        functools.partial(middle_kernel, n),
        [sds((rows, width), f32), sds((rows, width), bf16)],
        x_own, gain_m, *send_rows(branch),
    )
    nm_parts = after(gather_rows(nm_own), d_hidden)
    nm, hidden, d_units, *p_parts = call(
        functools.partial(ffn_kernel, steps, n),
        [sds((span, width), bf16), sds((span, units), bf16), sds((span, 2 * units), bf16)]
        + [sds((rows, width), bf16)] * n,
        *nm_parts, d_hidden, rest, rest,
        grid=(steps,),
        in_specs=[whole((rows, width))] * n
        + [
            pl.BlockSpec((span, tile), lambda j: (0, j)),
            pl.BlockSpec((width, tile), lambda j: (0, j)),
            pl.BlockSpec((width, tile), lambda j: (0, j + steps)),
        ],
        out_specs=[whole((span, width)), pl.BlockSpec((span, tile), lambda j: (0, j)), whole((span, 2 * units))]
        + [whole((rows, width))] * n,
        scratch=[pltpu.VMEM((width, 2 * units), bf16)],
    )
    p_got = send_rows(p_parts)
    part_ffn = jnp.concatenate([mm_tn(nm, d_units).astype(bf16), mm_tn(cot, hidden).astype(bf16)], axis=1)
    grad_ffn = lax.psum_scatter(after(part_ffn, *p_got), both, scatter_dimension=0, tiled=True)
    d_middle, db_own, gain_m_part = call(
        functools.partial(middle_back_kernel, n),
        [sds((rows, width), f32), sds((rows, width), bf16), sds((1, width), f32)],
        middle, cot_own, gain_m, *after(p_got, part_ffn),
    )
    db_parts = gather_rows(db_own)
    (down,) = call(
        functools.partial(down_kernel, n),
        [sds((n, rows, width), bf16)],
        after(hidden, db_own), rest,
        blocks={1: (width, units)}, places={1: (0, 2)},
    )
    down = lax.all_to_all(after(down, db_parts), "tp", 0, 0, tiled=True)
    down_sum = jnp.sum(down.astype(f32), axis=0)
    output = (valid * (middle + down_sum)).astype(bf16)

    d_branch, dq, dk, dv, back, d_open, d_cum = call(
        functools.partial(attend_back_kernel, heads, size, n),
        [
            sds((span, width), bf16),
            sds((span, cols), f32),
            sds((span, cols), f32),
            sds((span, cols), f32),
            sds((span, 2 * cols + 128), bf16),
            sds((span, cols), bf16),
            sds((span, 128), f32),
        ],
        *db_parts, qa, ka, va, kl, vl, cum, lse, opener, attended, rank, rank_t, w_out_full,
        blocks={n + 11: out_block}, weight=100,
    )
    part_gates = jnp.concatenate([mm_tn(d_branch, gated), mm_tn(normed, d_open)], axis=1).astype(bf16)
    grad_gates = lax.psum_scatter(after(part_gates, grad_ffn), both, scatter_dimension=0, tiled=True)
    back = lax.ppermute(back, "ctx", [(1, 0)])
    mixed, *dn = call(
        functools.partial(project_back_kernel, heads, size, n),
        [sds((span, wide), bf16)] + [sds((rows + 16, width), bf16)] * n,
        *x_parts, first, qk_wide, qraw, kraw, dq, dk, dv, back, d_open, d_cum, pre, rank, rank_t, gain_m_part,
    )
    deep = 3 * cols + 128
    dn = send_rows(dn)
    state_qkv = scatter_weight(mm_tn(normed, mixed[:, :deep]).astype(bf16))
    input_grad, own_sums = call(
        functools.partial(input_back_kernel, n),
        [sds((rows, width), bf16), sds((16, width), f32)],
        x_own, d_middle, gain_a, *after(dn, grad_gates, output, state_qkv[1]),
    )
    grad_ffn, grad_gates = grad_ffn.astype(f32), grad_gates.astype(f32)
    grad_gu, grad_down = grad_ffn[:, : 2 * units].reshape(slab, 2, units), grad_ffn[:, 2 * units :]
    grad_out, grad_ogate = grad_gates[:, :cols], grad_gates[:, cols:]
    grad_first = finish_weight(state_qkv)
    grad_qkv = grad_first[:, : 3 * cols].reshape(slab, 3, cols)
    grad_forget = grad_first[:, 3 * cols : 3 * cols + heads]

    me_bits = [(me ^ k) * heads for k in range(n)]
    bias_sum = jnp.zeros((n * heads,), f32)
    for k in range(n):
        bias_sum = lax.dynamic_update_slice_in_dim(
            bias_sum, dn[k][rows + 1, 2 * size : 2 * size + heads].astype(f32), me_bits[k], 0
        )
    small = jnp.concatenate([own_sums[0], own_sums[1, : 2 * size], bias_sum, own_sums[2]])
    small = sum_over(small, ("ctx", "shard"))
    edges = [0, width, width + 2 * size, width + 2 * size + n * heads]
    return (
        output[None],
        input_grad[None],
        grad_qkv,
        grad_forget,
        small[edges[2] : edges[3]],
        grad_ogate,
        grad_out,
        grad_gu,
        grad_down,
        small[edges[0] : edges[1]],
        small[edges[2] + n * heads :],
        small[edges[1] : edges[2]].reshape(2, size),
    )


def solution(mesh):
    rows = P("shard", ("ctx", "tp"), None)
    flat = P(("shard", "ctx"), "tp")
    deep = P(("shard", "ctx"), None, "tp")
    return jax.shard_map(
        body,
        mesh=mesh,
        in_specs=(rows, rows, P("shard"), deep, flat, P(), flat, flat, deep, flat, P(), P(), P()),
        out_specs=(rows, rows, deep, flat, P(), flat, flat, deep, flat, P(), P(), P()),
        check_vma=False,
    )
```

time: 509 us -> 420 us (0.83)
  the two profiles are of different devices: /device:TPU:0 before, /device:TPU:8 now
where the time goes in v2:
time: 420 us; the launch traced here: 414 us
  waiting for transfers between devices  212 us (50%)
  Pallas kernels  85.3 us (20%)
  starting transfers between devices  40.5 us (10%)
  local copies, waits for them, and re-layouts  33.8 us (8%)
  between operations  15.4 us (4%)
  other arithmetic  14.5 us (3%)
  matrix products  12.6 us (3%)
    ppermute x26, waiting for transfers between devices, swap(): return lax.ppermute(value, axis, [(j, j ^ bit) for j in range(n)])  203 us
    pallas_call x10, Pallas kernels, call(): pl.pallas_call(kernel, out_shape=outs, scratch_shapes=list(scratch), comp...  85.3 us
    ppermute x26, starting transfers between devices, swap(): return lax.ppermute(value, axis, [(j, j ^ bit) for j in range(n)])  28.1 us
    unnamed x97, local copies, waits for them, and re-layouts  16.5 us
    dot_general x5, matrix products, mm_tn(): lax.dot_general(left, right, (((0,), (0,)), ((), ())), preferred_element_...  12.6 us
  transfers between devices with their start and end apart: 34, of which 22 were waited for; matrix products, arithmetic and copies ran while one was open for 11% of the time, Pallas kernels for 17%

profile of v2, /device:TPU:8, one launch (start us, length us, event | category | flops | bytes accessed | tf_op | source)
XLA Modules:
  0.0 413.9 jit_solution(11223345836896223884)
XLA Ops:
  17.1 12.0 %collective-permute-done.refs_1_ = bf16[128,1536]{1,0:T(8,128)(2,1)S(1)} collective-permute-done((bf16[128,1536]{1,0:T(8,128)(2,1)S(1)}, bf16[128,1536]{1,0:T(8,128)(2,1)S(1)}, u32[]{:S(2)}, u32[]{:S(2)}) %collective-permute-start) | collective-permute-done | bytes 393248 | tf_op jit(solution)/shard_map/ppermute | solution.py:63
  29.0 13.1 %collective-permute-done.1.refs_2_ = bf16[128,1536]{1,0:T(8,128)(2,1)S(1)} collective-permute-done((bf16[128,1536]{1,0:T(8,128)(2,1)S(1)}, bf16[128,1536]{1,0:T(8,128)(2,1)S(1)}, u32[]{:S(2)}, u32[]{:S(2)}) %collective-permute-start.1) | collective-permute-done | bytes 393248 | tf_op jit(solution)/shard_map/ppermute | solution.py:63
  42.2 7.9 %collective-permute-done.2.refs_3_ = bf16[128,1536]{1,0:T(8,128)(2,1)S(1)} collective-permute-done((bf16[128,1536]{1,0:T(8,128)(2,1)S(1)}, bf16[128,1536]{1,0:T(8,128)(2,1)S(1)}, u32[]{:S(2)}, u32[]{:S(2)}) %collective-permute-start.2) | collective-permute-done | bytes 393248 | tf_op jit(solution)/shard_map/ppermute | solution.py:63
  51.4 4.3 %all-to-all-start = ((bf16[4,128,1536]{2,1,0:T(8,128)(2,1)}), bf16[4,128,1536]{2,1,0:T(8,128)(2,1)S(1)}, u32[]{:S(2)}, u32[]{:S(2)}) async-start(bf16[4,128,1536]{2,1,0:T(8,128)(2,1)} %broadcast_in_dim.38), calls=%async_computation | async-start | bytes 3145728 | tf_op jit(solution)/shard_map/all_to_all | solution.py:78
  58.5 11.2 %shard_map.220 = (bf16[512,1536]{1,0:T(8,128)(2,1)}, bf16[512,768]{1,0:T(8,128)(2,1)}, bf16[512,768]{1,0:T(8,128)(2,1)}, bf16[512,768]{1,0:T(8,128)(2,1)}, bf16[...) custom-call(bf16[128,1536]{1,0:T(8,128)(2,1)} %bitcast.83, ...), custom_call_target="tpu_custom_call" | custom-call | flops 100000000 | bytes 100000 | tf_op jit(solution)/shard_map/pallas_call | solution.py:47
  74.6 9.3 %shard_map.221 = (bf16[512,384]{1,0:T(8,128)(2,1)}, f32[512,384]{1,0:T(8,128)}, f32[512,128]{1,0:T(8,128)}, bf16[512,768]{1,0:T(8,128)(2,1)}, bf16[512,768]{1,0:...) custom-call(bf16[512,768]{1,0:T(8,128)(2,1)} %get-tuple-element.77.q, ...), custom_call_target="tpu_custom_call" | custom-call | flops 100000000 | bytes 100000 | tf_op jit(solution)/shard_map/pallas_call | solution.py:47
  88.0 16.4 %collective-permute-done.4.refs_1_ = bf16[128,1536]{1,0:T(8,128)(2,1)S(1)} collective-permute-done((bf16[128,1536]{1,0:T(8,128)(2,1)}, bf16[128,1536]{1,0:T(8,128)(2,1)S(1)}, u32[]{:S(2)}, u32[]{:S(2)}) %collective-permute-start.4) | collective-permute-done | bytes 393248 | tf_op jit(solution)/shard_map/ppermute | solution.py:63
  104.4 10.3 %collective-permute-done.5.refs_2_ = bf16[128,1536]{1,0:T(8,128)(2,1)S(1)} collective-permute-done((bf16[128,1536]{1,0:T(8,128)(2,1)}, bf16[128,1536]{1,0:T(8,128)(2,1)S(1)}, u32[]{:S(2)}, u32[]{:S(2)}) %collective-permute-start.5) | collective-permute-done | bytes 393248 | tf_op jit(solution)/shard_map/ppermute | solution.py:63
  114.6 9.3 %collective-permute-done.6.refs_3_ = bf16[128,1536]{1,0:T(8,128)(2,1)S(1)} collective-permute-done((bf16[128,1536]{1,0:T(8,128)(2,1)}, bf16[128,1536]{1,0:T(8,128)(2,1)S(1)}, u32[]{:S(2)}, u32[]{:S(2)}) %collective-permute-start.6) | collective-permute-done | bytes 393248 | tf_op jit(solution)/shard_map/ppermute | solution.py:63
  132.1 5.7 %shard_map.223 = (f32[512,1024]{1,0:T(8,128)}, bf16[512,1536]{1,0:T(8,128)(2,1)}) custom-call(bf16[4,128,1536]{2,1,0:T(8,128)(2,1)} %copy-done.1, bf16[1536,3072]{1,0:T(8,128)(2,1)} %all-gather.5.cloned.1.call-done.wd_ref.refs_5_.refs_6_), custom_call_target="tpu_custom_call" | custom-call | flops 100000000 | bytes 100000 | tf_op jit(solution)/shard_map/pallas_call | solution.py:47
  137.8 4.7 %collective-permute-done.7.refs_1_ = bf16[128,1536]{1,0:T(8,128)(2,1)S(1)} collective-permute-done((bf16[128,1536]{1,0:T(8,128)(2,1)}, bf16[128,1536]{1,0:T(8,128)(2,1)S(1)}, u32[]{:S(2)}, u32[]{:S(2)}) %collective-permute-start.7) | collective-permute-done | bytes 393248 | tf_op jit(solution)/shard_map/ppermute | solution.py:63
  142.5 13.8 %collective-permute-done.8.refs_2_ = bf16[128,1536]{1,0:T(8,128)(2,1)S(1)} collective-permute-done((bf16[128,1536]{1,0:T(8,128)(2,1)}, bf16[128,1536]{1,0:T(8,128)(2,1)S(1)}, u32[]{:S(2)}, u32[]{:S(2)}) %collective-permute-start.8) | collective-permute-done | bytes 393248 | tf_op jit(solution)/shard_map/ppermute | solution.py:63
  156.3 8.0 %collective-permute-done.9.refs_3_ = bf16[128,1536]{1,0:T(8,128)(2,1)S(1)} collective-permute-done((bf16[128,1536]{1,0:T(8,128)(2,1)}, bf16[128,1536]{1,0:T(8,128)(2,1)S(1)}, u32[]{:S(2)}, u32[]{:S(2)}) %collective-permute-start.9) | collective-permute-done | bytes 393248 | tf_op jit(solution)/shard_map/ppermute | solution.py:63
  165.1 13.7 %shard_map.224 = (bf16[512,1536]{1,0:T(8,128)(2,1)}, bf16[512,1024]{1,0:T(8,128)(2,1)}, bf16[512,2048]{1,0:T(8,128)(2,1)}, bf16[128,1536]{1,0:T(8,128)(2,1)}, bf...) custom-call(bf16[128,1536]{1,0:T(8,128)(2,1)} %get-tuple-element.91.refs_0_, ...), custom_call_target="tpu_custom_call" | custom-call | flops 100000000 | bytes 100000 | tf_op jit(solution)/shard_map/pallas_call | solution.py:47
  182.4 3.7 convolution_convert_fusion.2
  186.1 3.7 convolution_convert_fusion.1
  189.8 4.9 %pad_maximum_fusion = bf16[1536,3072]{1,0:T(8,128)(2,1)} fusion(bf16[1536,1024]{1,0:T(8,128)(2,1)S(1)} %convolution_convert_fusion.2, bf16[1536,2048]{1,0:T(8,128)(2,1)S(1)} %convolution_convert_fusion.1), kind=kLoop, calls=%fused_computation | loop fusion | flops 18874368 | bytes 18874368 | tf_op jit(solution)/shard_map/concatenate | solution.py:539
  194.7 13.1 %collective-permute-done.11.refs_2_ = bf16[128,1536]{1,0:T(8,128)(2,1)S(1)} collective-permute-done((bf16[128,1536]{1,0:T(8,128)(2,1)}, bf16[128,1536]{1,0:T(8,128)(2,1)S(1)}, u32[]{:S(2)}, u32[]{:S(2)}) %collective-permute-start.11) | collective-permute-done | bytes 393248 | tf_op jit(solution)/shard_map/ppermute | solution.py:63
  207.8 6.8 %collective-permute-done.12.refs_3_ = bf16[128,1536]{1,0:T(8,128)(2,1)S(1)} collective-permute-done((bf16[128,1536]{1,0:T(8,128)(2,1)}, bf16[128,1536]{1,0:T(8,128)(2,1)S(1)}, u32[]{:S(2)}, u32[]{:S(2)}) %collective-permute-start.12) | collective-permute-done | bytes 393248 | tf_op jit(solution)/shard_map/ppermute | solution.py:63
  222.1 8.8 %collective-permute-done.13.refs_1_ = bf16[128,1536]{1,0:T(8,128)(2,1)S(1)} collective-permute-done((bf16[128,1536]{1,0:T(8,128)(2,1)}, bf16[128,1536]{1,0:T(8,128)(2,1)S(1)}, u32[]{:S(2)}, u32[]{:S(2)}) %collective-permute-start.13) | collective-permute-done | bytes 393248 | tf_op jit(solution)/shard_map/ppermute | solution.py:63
  230.9 16.3 %collective-permute-done.14.refs_2_ = bf16[128,1536]{1,0:T(8,128)(2,1)S(1)} collective-permute-done((bf16[128,1536]{1,0:T(8,128)(2,1)}, bf16[128,1536]{1,0:T(8,128)(2,1)S(1)}, u32[]{:S(2)}, u32[]{:S(2)}) %collective-permute-start.14) | collective-permute-done | bytes 393248 | tf_op jit(solution)/shard_map/ppermute | solution.py:63
  247.2 5.9 %collective-permute-done.15.refs_3_ = bf16[128,1536]{1,0:T(8,128)(2,1)S(1)} collective-permute-done((bf16[128,1536]{1,0:T(8,128)(2,1)}, bf16[128,1536]{1,0:T(8,128)(2,1)S(1)}, u32[]{:S(2)}, u32[]{:S(2)}) %collective-permute-start.15) | collective-permute-done | bytes 393248 | tf_op jit(solution)/shard_map/ppermute | solution.py:63
  253.8 15.9 %shard_map.227 = (bf16[512,1536]{1,0:T(8,128)(2,1)}, f32[512,384]{1,0:T(8,128)}, f32[512,384]{1,0:T(8,128)}, f32[512,384]{1,0:T(8,128)}, bf16[512,896]{1,0:T(8,1...) custom-call(bf16[128,1536]{1,0:T(8,128)(2,1)} %get-tuple-element.107.refs_0_, bf16[128,1536]{1,0:T(8,128)(2,1)} %copy-done.40, ...), custom_call_target="tpu_custom_call" | custom-call | flops 99999997952 | bytes 100000000 | tf_op jit(solution)/shard_map/pallas_call | solution.py:47
  271.0 5.2 %shard_map.226 = bf16[4,128,1536]{2,1,0:T(8,128)(2,1)} custom-call(bf16[512,1024]{1,0:T(8,128)(2,1)} %get-tuple-element.108.hid_ref, bf16[1536,3072]{1,0:T(8,128)(2,1)} %all-gather.5.cloned.1.call-done.wd_ref.refs_5_.refs_6_), custom_call_target="tpu_custom_call" | custom-call | flops 100000000 | bytes 100000 | tf_op jit(solution)/shard_map/pallas_call | solution.py:47
  276.3 4.5 %all-to-all-start.1 = ((bf16[4,128,1536]{2,1,0:T(8,128)(2,1)}), bf16[4,128,1536]{2,1,0:T(8,128)(2,1)}, u32[]{:S(2)}, u32[]{:S(2)}) async-start(bf16[4,128,1536]{2,1,0:T(8,128)(2,1)} %shard_map.226), calls=%async_computation.1 | async-start | bytes 3145728 | tf_op jit(solution)/shard_map/all_to_all | solution.py:553
  283.4 6.9 %reduce-scatter.5.cloned.1.call-done = bf16[192,3072]{1,0:T(8,128)(2,1)} async-done(((bf16[1536,3072]{1,0:T(8,128)(2,1)}), bf16[192,3072]{1,0:T(8,128)(2,1)}) %reduce-scatter.5.cloned.1.call-update) | async-done | bytes 1179664 | tf_op jit(solution)/shard_map/reduce_scatter | solution.py:540
  293.7 15.1 %shard_map.228 = (bf16[512,1664]{1,0:T(8,128)(2,1)}, bf16[144,1536]{1,0:T(8,128)(2,1)}, bf16[144,1536]{1,0:T(8,128)(2,1)}, bf16[144,1536]{1,0:T(8,128)(2,1)}, bf16[144,1536]{1,0:T(8,128)(2,1)}) custom-call(bf16[128,1536]{1,0:T(8,128)(2,1)} %bitcast.85, bf16[128,1536]{1,0:T(8,128)(2,1)} %copy-done.6, bf16[128,1536]{1,0:T(8,128)(2,1)} %copy-done.7, ...), custom_call_target="tpu_custom_call" | custom-call | flops 100000000 | bytes 100000 | tf_op jit(solution)/shard_map/pallas_call | solution.py:47
  319.2 15.9 %collective-permute-done.17.refs_1_ = bf16[144,1536]{1,0:T(8,128)(2,1)S(1)} collective-permute-done((bf16[144,1536]{1,0:T(8,128)(2,1)}, bf16[144,1536]{1,0:T(8,128)(2,1)S(1)}, u32[]{:S(2)}, u32[]{:S(2)}) %collective-permute-start.17) | collective-permute-done | bytes 442400 | tf_op jit(solution)/shard_map/ppermute | solution.py:63
  335.2 12.2 %collective-permute-done.18.refs_2_ = bf16[144,1536]{1,0:T(8,128)(2,1)S(1)} collective-permute-done((bf16[144,1536]{1,0:T(8,128)(2,1)S(1)}, bf16[144,1536]{1,0:T(8,128)(2,1)S(1)}, u32[]{:S(2)}, u32[]{:S(2)}) %collective-permute-start.18) | collective-permute-done | bytes 442400 | tf_op jit(solution)/shard_map/ppermute | solution.py:63
  348.3 8.9 %collective-permute-done.19.refs_3_ = bf16[144,1536]{1,0:T(8,128)(2,1)S(1)} collective-permute-done((bf16[144,1536]{1,0:T(8,128)(2,1)S(1)}, bf16[144,1536]{1,0:T(8,128)(2,1)S(1)}, u32[]{:S(2)}, u32[]{:S(2)}) %collective-permute-start.19) | collective-permute-done | bytes 442400 | tf_op jit(solution)/shard_map/ppermute | solution.py:63
  368.3 8.9 %collective-permute-done.21 = bf16[192,1280]{1,0:T(8,128)(2,1)S(1)} collective-permute-done((bf16[192,1280]{1,0:T(8,128)(2,1)}, bf16[192,1280]{1,0:T(8,128)(2,1)S(1)}, u32[]{:S(2)}, u32[]{:S(2)}) %collective-permute-start.21) | collective-permute-done | bytes 491552 | tf_op jit(solution)/shard_map/ppermute | solution.py:63
  377.2 10.0 %collective-permute-done.22 = bf16[192,1280]{1,0:T(8,128)(2,1)} collective-permute-done((bf16[192,1280]{1,0:T(8,128)(2,1)}, bf16[192,1280]{1,0:T(8,128)(2,1)}, u32[]{:S(2)}, u32[]{:S(2)}) %collective-permute-start.22) | collective-permute-done | bytes 491552 | tf_op jit(solution)/shard_map/ppermute | solution.py:63
  (197 shorter events, 92.4 us)
Async XLA Ops:
  7.2 51.3 %all-gather.3.cloned.1.call-start = ((), (), s32[]{:S(2)}) async-start(), calls=%async_computation.4 | async-start | bytes 7077888 | tf_op jit(solution)/shard_map/all_gather | solution.py:468
  11.2 119.8 %all-gather.5.cloned.1.call-start = ((), (), s32[]{:S(2)}) async-start(), calls=%async_computation.5 | async-start | bytes 10616832 | tf_op jit(solution)/shard_map/all_gather | solution.py:470
  12.7 16.4 %collective-permute-start = (bf16[128,1536]{1,0:T(8,128)(2,1)S(1)}, bf16[128,1536]{1,0:T(8,128)(2,1)S(1)}, u32[]{:S(2)}, u32[]{:S(2)}) collective-permute-start(bf16[128,1536]{1,0:T(8,128)(2,1)S(1)} %bitcast.87), channel_id=1, source_target_pairs={{0,1},{1,0},{2,3},{3,2},{4,5},{5,4},{6,7},{7,6},{8,9},{9,8},{10,11... | collective-permute-start | bytes 1179656 | tf_op jit(solution)/shard_map/ppermute | solution.py:63
  12.7 29.4 %collective-permute-start.1 = (bf16[128,1536]{1,0:T(8,128)(2,1)S(1)}, bf16[128,1536]{1,0:T(8,128)(2,1)S(1)}, u32[]{:S(2)}, u32[]{:S(2)}) collective-permute-start(bf16[128,1536]{1,0:T(8,128)(2,1)S(1)} %bitcast.88), channel_id=1, source_target_pairs={{0,2},{1,3},{2,0},{3,1},{4,6},{5,7},{6,4},{7,5},{8,10},{9,11},{10,... | collective-permute-start | bytes 1179656 | tf_op jit(solution)/shard_map/ppermute | solution.py:63
  15.8 34.3 %collective-permute-start.2 = (bf16[128,1536]{1,0:T(8,128)(2,1)S(1)}, bf16[128,1536]{1,0:T(8,128)(2,1)S(1)}, u32[]{:S(2)}, u32[]{:S(2)}) collective-permute-start(bf16[128,1536]{1,0:T(8,128)(2,1)S(1)} %bitcast.89), channel_id=1, source_target_pairs={{0,3},{1,2},{2,1},{3,0},{4,7},{5,6},{6,5},{7,4},{8,11},{9,10},{10,... | collective-permute-start | bytes 1179656 | tf_op jit(solution)/shard_map/ppermute | solution.py:63
  51.4 79.6 %all-to-all-start = ((bf16[4,128,1536]{2,1,0:T(8,128)(2,1)}), bf16[4,128,1536]{2,1,0:T(8,128)(2,1)S(1)}, u32[]{:S(2)}, u32[]{:S(2)}) async-start(bf16[4,128,1536]{2,1,0:T(8,128)(2,1)} %broadcast_in_dim.38), calls=%async_computation | async-start | bytes 3145728 | tf_op jit(solution)/shard_map/all_to_all | solution.py:78
  55.7 234.6 %reduce-scatter.5.cloned.1.call-start = ((), (), s32[]{:S(2)}) async-start(), calls=%async_computation.6 | async-start | bytes 10616832 | tf_op jit(solution)/shard_map/reduce_scatter | solution.py:540
  69.7 4.0 collective-permute-start.3
  83.9 20.5 %collective-permute-start.4 = (bf16[128,1536]{1,0:T(8,128)(2,1)}, bf16[128,1536]{1,0:T(8,128)(2,1)S(1)}, u32[]{:S(2)}, u32[]{:S(2)}) collective-permute-start(bf16[128,1536]{1,0:T(8,128)(2,1)} %get-tuple-element.83), channel_id=1, source_target_pairs={{0,1},{1,0},{2,3},{3,2},{4,5},{5,4},{6,7},{7,6},{8,9},{9,8},{10,11... | collective-permute-start | bytes 1179656 | tf_op jit(solution)/shard_map/ppermute | solution.py:63
  84.5 30.2 %collective-permute-start.5 = (bf16[128,1536]{1,0:T(8,128)(2,1)}, bf16[128,1536]{1,0:T(8,128)(2,1)S(1)}, u32[]{:S(2)}, u32[]{:S(2)}) collective-permute-start(bf16[128,1536]{1,0:T(8,128)(2,1)} %get-tuple-element.84), channel_id=1, source_target_pairs={{0,2},{1,3},{2,0},{3,1},{4,6},{5,7},{6,4},{7,5},{8,10},{9,11},{10,... | collective-permute-start | bytes 1179656 | tf_op jit(solution)/shard_map/ppermute | solution.py:63
  86.9 37.1 %collective-permute-start.6 = (bf16[128,1536]{1,0:T(8,128)(2,1)}, bf16[128,1536]{1,0:T(8,128)(2,1)S(1)}, u32[]{:S(2)}, u32[]{:S(2)}) collective-permute-start(bf16[128,1536]{1,0:T(8,128)(2,1)} %get-tuple-element.85), channel_id=1, source_target_pairs={{0,3},{1,2},{2,1},{3,0},{4,7},{5,6},{6,5},{7,4},{8,11},{9,10},{10,... | collective-permute-start | bytes 1179656 | tf_op jit(solution)/shard_map/ppermute | solution.py:63
  127.5 15.0 %collective-permute-start.7 = (bf16[128,1536]{1,0:T(8,128)(2,1)}, bf16[128,1536]{1,0:T(8,128)(2,1)S(1)}, u32[]{:S(2)}, u32[]{:S(2)}) collective-permute-start(bf16[128,1536]{1,0:T(8,128)(2,1)} %get-tuple-element.91.refs_0_), channel_id=1, source_target_pairs={{0,1},{1,0},{2,3},{3,2},{4,5},{5,4},{6,7},{7,6},{8,9},{9,8},{10,11... | collective-permute-start | bytes 1179656 | tf_op jit(solution)/shard_map/ppermute | solution.py:63
  127.5 28.8 %collective-permute-start.8 = (bf16[128,1536]{1,0:T(8,128)(2,1)}, bf16[128,1536]{1,0:T(8,128)(2,1)S(1)}, u32[]{:S(2)}, u32[]{:S(2)}) collective-permute-start(bf16[128,1536]{1,0:T(8,128)(2,1)} %get-tuple-element.91.refs_0_), channel_id=1, source_target_pairs={{0,2},{1,3},{2,0},{3,1},{4,6},{5,7},{6,4},{7,5},{8,10},{9,11},{10,... | collective-permute-start | bytes 1179656 | tf_op jit(solution)/shard_map/ppermute | solution.py:63
  129.5 34.8 %collective-permute-start.9 = (bf16[128,1536]{1,0:T(8,128)(2,1)}, bf16[128,1536]{1,0:T(8,128)(2,1)S(1)}, u32[]{:S(2)}, u32[]{:S(2)}) collective-permute-start(bf16[128,1536]{1,0:T(8,128)(2,1)} %get-tuple-element.91.refs_0_), channel_id=1, source_target_pairs={{0,3},{1,2},{2,1},{3,0},{4,7},{5,6},{6,5},{7,4},{8,11},{9,10},{10,... | collective-permute-start | bytes 1179656 | tf_op jit(solution)/shard_map/ppermute | solution.py:63
  178.8 15.8 %collective-permute-start.10 = (bf16[128,1536]{1,0:T(8,128)(2,1)}, bf16[128,1536]{1,0:T(8,128)(2,1)S(1)}, u32[]{:S(2)}, u32[]{:S(2)}) collective-permute-start(bf16[128,1536]{1,0:T(8,128)(2,1)} %get-tuple-element.97), channel_id=1, source_target_pairs={{0,1},{1,0},{2,3},{3,2},{4,5},{5,4},{6,7},{7,6},{8,9},{9,8},{10,11... | collective-permute-start | bytes 1179656 | tf_op jit(solution)/shard_map/ppermute | solution.py:63
  178.9 28.9 %collective-permute-start.11 = (bf16[128,1536]{1,0:T(8,128)(2,1)}, bf16[128,1536]{1,0:T(8,128)(2,1)S(1)}, u32[]{:S(2)}, u32[]{:S(2)}) collective-permute-start(bf16[128,1536]{1,0:T(8,128)(2,1)} %get-tuple-element.98), channel_id=1, source_target_pairs={{0,2},{1,3},{2,0},{3,1},{4,6},{5,7},{6,4},{7,5},{8,10},{9,11},{10,... | collective-permute-start | bytes 1179656 | tf_op jit(solution)/shard_map/ppermute | solution.py:63
  181.0 33.5 %collective-permute-start.12 = (bf16[128,1536]{1,0:T(8,128)(2,1)}, bf16[128,1536]{1,0:T(8,128)(2,1)S(1)}, u32[]{:S(2)}, u32[]{:S(2)}) collective-permute-start(bf16[128,1536]{1,0:T(8,128)(2,1)} %get-tuple-element.99), channel_id=1, source_target_pairs={{0,3},{1,2},{2,1},{3,0},{4,7},{5,6},{6,5},{7,4},{8,11},{9,10},{10,... | collective-permute-start | bytes 1179656 | tf_op jit(solution)/shard_map/ppermute | solution.py:63
  218.6 12.3 %collective-permute-start.13 = (bf16[128,1536]{1,0:T(8,128)(2,1)}, bf16[128,1536]{1,0:T(8,128)(2,1)S(1)}, u32[]{:S(2)}, u32[]{:S(2)}) collective-permute-start(bf16[128,1536]{1,0:T(8,128)(2,1)} %get-tuple-element.107.refs_0_), channel_id=1, source_target_pairs={{0,1},{1,0},{2,3},{3,2},{4,5},{5,4},{6,7},{7,6},{8,9},{9,8},{10,11... | collective-permute-start | bytes 1179656 | tf_op jit(solution)/shard_map/ppermute | solution.py:63
  218.6 28.5 %collective-permute-start.14 = (bf16[128,1536]{1,0:T(8,128)(2,1)}, bf16[128,1536]{1,0:T(8,128)(2,1)S(1)}, u32[]{:S(2)}, u32[]{:S(2)}) collective-permute-start(bf16[128,1536]{1,0:T(8,128)(2,1)} %get-tuple-element.107.refs_0_), channel_id=1, source_target_pairs={{0,2},{1,3},{2,0},{3,1},{4,6},{5,7},{6,4},{7,5},{8,10},{9,11},{10,... | collective-permute-start | bytes 1179656 | tf_op jit(solution)/shard_map/ppermute | solution.py:63
  220.9 32.2 %collective-permute-start.15 = (bf16[128,1536]{1,0:T(8,128)(2,1)}, bf16[128,1536]{1,0:T(8,128)(2,1)S(1)}, u32[]{:S(2)}, u32[]{:S(2)}) collective-permute-start(bf16[128,1536]{1,0:T(8,128)(2,1)} %get-tuple-element.107.refs_0_), channel_id=1, source_target_pairs={{0,3},{1,2},{2,1},{3,0},{4,7},{5,6},{6,5},{7,4},{8,11},{9,10},{10,... | collective-permute-start | bytes 1179656 | tf_op jit(solution)/shard_map/ppermute | solution.py:63
  269.8 23.0 %collective-permute-start.16 = (bf16[512,896]{1,0:T(8,128)(2,1)}, bf16[512,896]{1,0:T(8,128)(2,1)S(1)}, u32[]{:S(2)}, u32[]{:S(2)}) collective-permute-start(bf16[512,896]{1,0:T(8,128)(2,1)} %get-tuple-element.121), channel_id=1, source_target_pairs={{4,0},{5,1},{6,2},{7,3},{12,8},{13,9},{14,10},{15,11},{20,16},{21,... | collective-permute-start | bytes 2752520 | tf_op jit(solution)/shard_map/ppermute | solution.py:573
  276.3 82.1 %all-to-all-start.1 = ((bf16[4,128,1536]{2,1,0:T(8,128)(2,1)}), bf16[4,128,1536]{2,1,0:T(8,128)(2,1)}, u32[]{:S(2)}, u32[]{:S(2)}) async-start(bf16[4,128,1536]{2,1,0:T(8,128)(2,1)} %shard_map.226), calls=%async_computation.1 | async-start | bytes 3145728 | tf_op jit(solution)/shard_map/all_to_all | solution.py:553
  280.8 86.4 %reduce-scatter.7.cloned.1.call-start = ((), (), s32[]{:S(2)}) async-start(), calls=%async_computation.7 | async-start | bytes 2654208
  315.0 45.1 %collective-permute-start.20 = (bf16[4,192,1280]{2,1,0:T(8,128)(2,1)}, bf16[4,192,1280]{2,1,0:T(8,128)(2,1)S(1)}, u32[]{:S(2)}, u32[]{:S(2)}) collective-permute-start(bf16[4,192,1280]{2,1,0:T(8,128)(2,1)} %dynamic-slice_bitcast_fusion), channel_id=1, source_target_pairs={{0,4},{4,0},{1,5},{5,1},{2,6},{6,2},{3,7},{7,3},{8,12},{12,8},{9,1... | collective-permute-start | bytes 5898248 | tf_op jit(solution)/shard_map/ppermute | solution.py:63
  315.0 20.1 %collective-permute-start.17 = (bf16[144,1536]{1,0:T(8,128)(2,1)}, bf16[144,1536]{1,0:T(8,128)(2,1)S(1)}, u32[]{:S(2)}, u32[]{:S(2)}) collective-permute-start(bf16[144,1536]{1,0:T(8,128)(2,1)} %get-tuple-element.127), channel_id=1, source_target_pairs={{0,1},{1,0},{2,3},{3,2},{4,5},{5,4},{6,7},{7,6},{8,9},{9,8},{10,11... | collective-permute-start | bytes 1327112 | tf_op jit(solution)/shard_map/ppermute | solution.py:63
  315.6 31.9 %collective-permute-start.18 = (bf16[144,1536]{1,0:T(8,128)(2,1)S(1)}, bf16[144,1536]{1,0:T(8,128)(2,1)S(1)}, u32[]{:S(2)}, u32[]{:S(2)}) collective-permute-start(bf16[144,1536]{1,0:T(8,128)(2,1)S(1)} %copy-done.38), channel_id=1, source_target_pairs={{0,2},{1,3},{2,0},{3,1},{4,6},{5,7},{6,4},{7,5},{8,10},{9,11},{10,... | collective-permute-start | bytes 1327112 | tf_op jit(solution)/shard_map/ppermute | solution.py:63
  317.9 39.3 %collective-permute-start.19 = (bf16[144,1536]{1,0:T(8,128)(2,1)S(1)}, bf16[144,1536]{1,0:T(8,128)(2,1)S(1)}, u32[]{:S(2)}, u32[]{:S(2)}) collective-permute-start(bf16[144,1536]{1,0:T(8,128)(2,1)S(1)} %copy-done.37), channel_id=1, source_target_pairs={{0,3},{1,2},{2,1},{3,0},{4,7},{5,6},{6,5},{7,4},{8,11},{9,10},{10,... | collective-permute-start | bytes 1327112 | tf_op jit(solution)/shard_map/ppermute | solution.py:63
  362.8 14.4 %collective-permute-start.21 = (bf16[192,1280]{1,0:T(8,128)(2,1)}, bf16[192,1280]{1,0:T(8,128)(2,1)S(1)}, u32[]{:S(2)}, u32[]{:S(2)}) collective-permute-start(bf16[192,1280]{1,0:T(8,128)(2,1)} %get-tuple-element.182), channel_id=1, source_target_pairs={{0,8},{8,0},{16,24},{24,16},{1,9},{9,1},{17,25},{25,17},{2,10},{10... | collective-permute-start | bytes 1474568 | tf_op jit(solution)/shard_map/ppermute | solution.py:63
  364.1 23.1 %collective-permute-start.22 = (bf16[192,1280]{1,0:T(8,128)(2,1)}, bf16[192,1280]{1,0:T(8,128)(2,1)}, u32[]{:S(2)}, u32[]{:S(2)}) collective-permute-start(bf16[192,1280]{1,0:T(8,128)(2,1)} %get-tuple-element.181), channel_id=1, source_target_pairs={{0,16},{8,24},{16,0},{24,8},{1,17},{9,25},{17,1},{25,9},{2,18},{10... | collective-permute-start | bytes 1474568 | tf_op jit(solution)/shard_map/ppermute | solution.py:63
  364.8 22.4 %collective-permute-start.23 = (bf16[192,1280]{1,0:T(8,128)(2,1)}, bf16[192,1280]{1,0:T(8,128)(2,1)}, u32[]{:S(2)}, u32[]{:S(2)}) collective-permute-start(bf16[192,1280]{1,0:T(8,128)(2,1)} %get-tuple-element.180), channel_id=1, source_target_pairs={{0,24},{8,16},{16,8},{24,0},{1,25},{9,17},{17,9},{25,1},{2,26},{10... | collective-permute-start | bytes 1474568 | tf_op jit(solution)/shard_map/ppermute | solution.py:63
  392.1 7.0 %collective-permute-start.24 = (f32[3224]{0:T(1024)S(1)}, f32[3224]{0:T(1024)S(1)}, u32[]{:S(2)}, u32[]{:S(2)}) collective-permute-start(f32[3224]{0:T(1024)S(1)} %concatenate.28), channel_id=1, source_target_pairs={{0,4},{4,0},{1,5},{5,1},{2,6},{6,2},{3,7},{7,3},{8,12},{12,8},{9,1... | collective-permute-start | bytes 38696 | tf_op jit(solution)/shard_map/ppermute | solution.py:63
  399.1 5.3 %collective-permute-start.27 = (f32[3224]{0:T(1024)S(1)}, f32[3224]{0:T(1024)S(1)}, u32[]{:S(2)}, u32[]{:S(2)}) collective-permute-start(f32[3224]{0:T(1024)S(1)} %add.162), channel_id=1, source_target_pairs={{0,24},{8,16},{16,8},{24,0},{1,25},{9,17},{17,9},{25,1},{2,26},{10... | collective-permute-start | bytes 38696 | tf_op jit(solution)/shard_map/ppermute | solution.py:63
  (47 other events, 361.4 us)
Sparse Core Ops, SparseCore 0:
  11.3 46.6 all-gather.2
  59.9 58.8 all-gather.4
  214.7 75.5 reduce-scatter.4
  293.5 42.4 reduce-scatter.6

commit v3 on v2

--- a/solution.py
+++ b/solution.py
@@ -65,17 +65,30 @@
 
 def gather_rows(own):
     n = lax.axis_size("tp")
-    return [own] + [swap(own, "tp", k) for k in range(1, n)]
-
-
-def send_rows(parts):
-    n = lax.axis_size("tp")
-    return [parts[0]] + [swap(parts[k], "tp", k) for k in range(1, n)]
+    if n != 4:
+        return [own] + [swap(own, "tp", k) for k in range(1, n)]
+    far = swap(own, "tp", 2)
+    near = swap(own, "tp", 1)
+    return [own, near, far, swap(far, "tp", 1)]
 
 
 def gather_all(own):
     n = lax.axis_size("tp")
     return lax.all_to_all(jnp.broadcast_to(own[None], (n,) + own.shape), "tp", 0, 0, tiled=True)
+
+
+def scatter_all(blocks):
+    return lax.all_to_all(blocks, "tp", 0, 0, tiled=True)
+
+
+def send_rows(parts):
+    n = lax.axis_size("tp")
+    if n != 4:
+        return [parts[0]] + [swap(parts[k], "tp", k) for k in range(1, n)]
+    across = swap(parts[3], "tp", 1)
+    near = swap(parts[1], "tp", 1)
+    far = (parts[2].astype(f32) + across.astype(f32)).astype(bf16)
+    return [parts[0], near, swap(far, "tp", 2)]
 
 
 def after(value, *others):
@@ -99,13 +112,6 @@
 
     arrived = [swap(pair(k).astype(bf16), "shard", k) for k in range(1, shards)]
     return pair(0), arrived
-
-
-def finish_weight(state):
-    own, arrived = state
-    for g in arrived:
-        own = own + g.astype(f32)
-    return own
 
 
 def sum_over(value, axes):
@@ -355,7 +361,7 @@
     x_refs, refs = refs[:chunks], refs[chunks:]
     (w_ref, qk_ref, qraw_ref, kraw_ref, dq_ref, dk_ref, dv_ref, back_ref, dopen_ref, dcum_ref, pre_ref, rank_ref,
      rank_t_ref, gm_ref) = refs[:14]
-    mixed_ref, out_refs = refs[14], refs[15:]
+    mixed_ref, out_ref = refs[14:]
     cols = heads * size
     width = x_refs[0].shape[1]
     rows = x_refs[0].shape[0]
@@ -382,26 +388,33 @@
     df = jnp.concatenate([dlog, jnp.zeros((span, 128 - heads), f32)], axis=1) * jax.nn.sigmoid(-pre_ref[...])
     bias = jnp.sum(df, axis=0, keepdims=True)
     mixed_ref[:, 3 * cols : 3 * cols + 128] = df.astype(bf16)
-    gain = jnp.zeros((1, width), f32)
-    lows = []
+    me = lax.axis_index("tp")
+    units = []
     for c in range(chunks):
-        at = slice(c * rows, (c + 1) * rows)
-        dn = mm_nt(mixed_ref[at, :], w_ref[:, cols:])
-        out_refs[c][0:rows, :] = dn.astype(bf16)
         x = x_refs[c][...].astype(f32)
-        r = lax.rsqrt(jnp.mean(x * x, axis=1, keepdims=True) + epsilon)
-        gain = gain + jnp.sum(dn * (x * r), axis=0, keepdims=True)
+        units.append(x * lax.rsqrt(jnp.mean(x * x, axis=1, keepdims=True) + epsilon))
+    gains = []
+    for b in range(0, width, 256):
+        dn = mm_nt(mixed_ref[...], w_ref[b : b + 256, cols:])
+        gain = jnp.zeros((1, 256), f32)
+        for c in range(chunks):
+            piece = dn[c * rows : (c + 1) * rows, :]
+            out_ref[pl.ds(me ^ c, 1), 0:rows, b : b + 256] = piece.astype(bf16)[None]
+            gain = gain + jnp.sum(piece * units[c][:, b : b + 256], axis=0, keepdims=True)
+        gains.append(gain)
+    gain = jnp.concatenate(gains, axis=1)
+    bias = pltpu.roll(bias, me * heads, 1)
     lanes = jnp.concatenate([sums[0], sums[1], bias, jnp.zeros((1, width - 2 * size - 128), f32)], axis=1)
     low = jnp.concatenate([gain, lanes, gm_ref[...], jnp.zeros((13, width), f32)], axis=0).astype(bf16)
     for c in range(chunks):
-        out_refs[c][rows : rows + 16, :] = low
-
-
-def middle_kernel(chunks, x_ref, gain_ref, *refs):
+        out_ref[c, rows : rows + 16, :] = low
+
+
+def middle_kernel(x_ref, gain_ref, *refs):
     middle = x_ref[...].astype(f32)
-    for c in range(chunks):
-        middle = middle + refs[c][...].astype(f32)
-    mid_ref, nm_ref = refs[chunks:]
+    for ref in refs[:-2]:
+        middle = middle + ref[...].astype(f32)
+    mid_ref, nm_ref = refs[-2:]
     mid_ref[...] = middle
     r = lax.rsqrt(jnp.mean(middle * middle, axis=1, keepdims=True) + epsilon)
     nm_ref[...] = (middle * r * gain_ref[...]).astype(bf16)
@@ -414,11 +427,11 @@
     return r * (e - u * jnp.mean(e * u, axis=1, keepdims=True)), jnp.sum(d * u, axis=0, keepdims=True)
 
 
-def middle_back_kernel(chunks, mid_ref, cot_ref, gain_ref, *refs):
+def middle_back_kernel(mid_ref, cot_ref, gain_ref, *refs):
     d = refs[0][...].astype(f32)
-    for c in range(1, chunks):
-        d = d + refs[c][...].astype(f32)
-    dmid_ref, branch_ref, part_ref = refs[chunks:]
+    for ref in refs[1:-3]:
+        d = d + ref[...].astype(f32)
+    dmid_ref, branch_ref, part_ref = refs[-3:]
     back, part = norm_back(d, mid_ref[...], gain_ref[...])
     back = back + cot_ref[...].astype(f32)
     dmid_ref[...] = back
@@ -426,14 +439,38 @@
     part_ref[...] = part
 
 
-def input_back_kernel(chunks, x_ref, dmid_ref, gain_ref, *refs):
+def input_back_kernel(x_ref, dmid_ref, gain_ref, *refs):
     rows = x_ref.shape[0]
-    d = refs[0][...].astype(f32)
-    for c in range(1, chunks):
-        d = d + refs[c][...].astype(f32)
-    back, _ = norm_back(d[0:rows, :], x_ref[...].astype(f32), gain_ref[...])
-    refs[chunks][...] = (back + dmid_ref[...]).astype(bf16)
-    refs[chunks + 1][...] = d[rows:, :]
+    out_ref = refs[-1]
+    d = refs[0][0, 0:rows, :].astype(f32)
+    for c in range(1, refs[0].shape[0]):
+        d = d + refs[0][c, 0:rows, :].astype(f32)
+    back, _ = norm_back(d, x_ref[...].astype(f32), gain_ref[...])
+    out_ref[...] = (back + dmid_ref[...]).astype(bf16)
+
+
+def finish_ffn_kernel(in_ref, gu_ref, down_ref):
+    units = down_ref.shape[1]
+    gu_ref[:, 0, :] = in_ref[:, :units].astype(f32)
+    gu_ref[:, 1, :] = in_ref[:, units : 2 * units].astype(f32)
+    down_ref[...] = in_ref[:, 2 * units :].astype(f32)
+
+
+def finish_gates_kernel(in_ref, out_ref, gate_ref):
+    cols = out_ref.shape[1]
+    out_ref[...] = in_ref[:, :cols].astype(f32)
+    gate_ref[...] = in_ref[:, cols:].astype(f32)
+
+
+def finish_qkv_kernel(own_ref, *refs):
+    qkv_ref, forget_ref = refs[-2:]
+    cols = qkv_ref.shape[2]
+    total = own_ref[...]
+    for ref in refs[:-2]:
+        total = total + ref[...].astype(f32)
+    for i in range(3):
+        qkv_ref[:, i, :] = total[:, i * cols : (i + 1) * cols]
+    forget_ref[...] = total[:, 3 * cols : 3 * cols + forget_ref.shape[1]]
 
 
 def body(tokens, cotangent, lengths, w_qkv, w_forget, forget_bias, w_ogate, w_out, w_gu, w_down, gain_attn, gain_mlp,
@@ -503,20 +540,20 @@
         qa, ka, va, left, opener, rank, rank_t, w_out_full,
         blocks={7: out_block},
     )
+    middle, nm_own = call(
+        middle_kernel,
+        [sds((rows, width), f32), sds((rows, width), bf16)],
+        x_own, gain_m, *send_rows(after(branch, cot)),
+    )
     tile = min(512, units)
     steps = units // tile
     d_hidden, cot = call(
         functools.partial(hidden_back_kernel, n),
         [sds((span, units), f32), sds((span, width), bf16)],
-        after(cot, branch), rest,
+        after(cot, nm_own), rest,
         grid=(steps,),
         in_specs=[whole((n, rows, width)), pl.BlockSpec((width, tile), lambda j: (0, j + 2 * steps))],
         out_specs=[pl.BlockSpec((span, tile), lambda j: (0, j)), whole((span, width))],
-    )
-    middle, nm_own = call(
-        functools.partial(middle_kernel, n),
-        [sds((rows, width), f32), sds((rows, width), bf16)],
-        x_own, gain_m, *send_rows(branch),
     )
     nm_parts = after(gather_rows(nm_own), d_hidden)
     nm, hidden, d_units, *p_parts = call(
@@ -537,23 +574,20 @@
     )
     p_got = send_rows(p_parts)
     part_ffn = jnp.concatenate([mm_tn(nm, d_units).astype(bf16), mm_tn(cot, hidden).astype(bf16)], axis=1)
-    grad_ffn = lax.psum_scatter(after(part_ffn, *p_got), both, scatter_dimension=0, tiled=True)
+    grad_ffn = lax.psum_scatter(after(part_ffn, p_got[1]), both, scatter_dimension=0, tiled=True)
     d_middle, db_own, gain_m_part = call(
-        functools.partial(middle_back_kernel, n),
+        middle_back_kernel,
         [sds((rows, width), f32), sds((rows, width), bf16), sds((1, width), f32)],
         middle, cot_own, gain_m, *after(p_got, part_ffn),
     )
     db_parts = gather_rows(db_own)
-    (down,) = call(
+    (down_rows,) = call(
         functools.partial(down_kernel, n),
         [sds((n, rows, width), bf16)],
         after(hidden, db_own), rest,
         blocks={1: (width, units)}, places={1: (0, 2)},
     )
-    down = lax.all_to_all(after(down, db_parts), "tp", 0, 0, tiled=True)
-    down_sum = jnp.sum(down.astype(f32), axis=0)
-    output = (valid * (middle + down_sum)).astype(bf16)
-
+    down = scatter_all(after(down_rows, db_parts))
     d_branch, dq, dk, dv, back, d_open, d_cum = call(
         functools.partial(attend_back_kernel, heads, size, n),
         [
@@ -565,39 +599,38 @@
             sds((span, cols), bf16),
             sds((span, 128), f32),
         ],
-        *db_parts, qa, ka, va, kl, vl, cum, lse, opener, attended, rank, rank_t, w_out_full,
+        *after(db_parts, down_rows), qa, ka, va, kl, vl, cum, lse, opener, attended, rank, rank_t, w_out_full,
         blocks={n + 11: out_block}, weight=100,
     )
     part_gates = jnp.concatenate([mm_tn(d_branch, gated), mm_tn(normed, d_open)], axis=1).astype(bf16)
-    grad_gates = lax.psum_scatter(after(part_gates, grad_ffn), both, scatter_dimension=0, tiled=True)
     back = lax.ppermute(back, "ctx", [(1, 0)])
-    mixed, *dn = call(
+    mixed, dn = call(
         functools.partial(project_back_kernel, heads, size, n),
-        [sds((span, wide), bf16)] + [sds((rows + 16, width), bf16)] * n,
+        [sds((span, wide), bf16), sds((n, rows + 16, width), bf16)],
         *x_parts, first, qk_wide, qraw, kraw, dq, dk, dv, back, d_open, d_cum, pre, rank, rank_t, gain_m_part,
     )
+    down_sum = jnp.sum(after(down, mixed).astype(f32), axis=0)
+    output = (valid * (middle + down_sum)).astype(bf16)
     deep = 3 * cols + 128
-    dn = send_rows(dn)
+    grad_gates = lax.psum_scatter(after(part_gates, mixed, grad_ffn), both, scatter_dimension=0, tiled=True)
     state_qkv = scatter_weight(mm_tn(normed, mixed[:, :deep]).astype(bf16))
-    input_grad, own_sums = call(
-        functools.partial(input_back_kernel, n),
-        [sds((rows, width), bf16), sds((16, width), f32)],
-        x_own, d_middle, gain_a, *after(dn, grad_gates, output, state_qkv[1]),
-    )
-    grad_ffn, grad_gates = grad_ffn.astype(f32), grad_gates.astype(f32)
-    grad_gu, grad_down = grad_ffn[:, : 2 * units].reshape(slab, 2, units), grad_ffn[:, 2 * units :]
-    grad_out, grad_ogate = grad_gates[:, :cols], grad_gates[:, cols:]
-    grad_first = finish_weight(state_qkv)
-    grad_qkv = grad_first[:, : 3 * cols].reshape(slab, 3, cols)
-    grad_forget = grad_first[:, 3 * cols : 3 * cols + heads]
-
-    me_bits = [(me ^ k) * heads for k in range(n)]
-    bias_sum = jnp.zeros((n * heads,), f32)
-    for k in range(n):
-        bias_sum = lax.dynamic_update_slice_in_dim(
-            bias_sum, dn[k][rows + 1, 2 * size : 2 * size + heads].astype(f32), me_bits[k], 0
-        )
-    small = jnp.concatenate([own_sums[0], own_sums[1, : 2 * size], bias_sum, own_sums[2]])
+    dn = scatter_all(after(dn, output, grad_ffn))
+    grad_gu, grad_down = call(
+        finish_ffn_kernel, [sds((slab, 2, units), f32), sds((slab, units), f32)], grad_ffn
+    )
+    dn_late, grad_gu, grad_down, _ = lax.optimization_barrier((dn, grad_gu, grad_down, state_qkv[1]))
+    (input_grad,) = call(
+        input_back_kernel, [sds((rows, width), bf16)], x_own, d_middle, gain_a, dn_late
+    )
+    grad_out, grad_ogate = call(finish_gates_kernel, [sds((slab, cols), f32)] * 2, grad_gates)
+    grad_qkv, grad_forget = call(
+        finish_qkv_kernel,
+        [sds((slab, 3, cols), f32), sds((slab, heads), f32)],
+        state_qkv[0], *state_qkv[1],
+    )
+
+    sums = jnp.sum(dn[:, rows:].astype(f32), axis=0)
+    small = jnp.concatenate([sums[0], sums[1, : 2 * size + n * heads], sums[2]])
     small = sum_over(small, ("ctx", "shard"))
     edges = [0, width, width + 2 * size, width + 2 * size + n * heads]
     return (

time: 420 us -> 364 us (0.87)
  the two profiles are of different devices: /device:TPU:8 before, /device:TPU:0 now
where the time goes in v3:
time: 364 us; the launch traced here: 358 us
  waiting for transfers between devices  149 us (41%)
  Pallas kernels  89.3 us (25%)
  starting transfers between devices  50.4 us (14%)
  local copies, waits for them, and re-layouts  23.6 us (6%)
  matrix products  16.9 us (5%)
  between operations  15.1 us (4%)
  other arithmetic  13.6 us (4%)
    ppermute x23, waiting for transfers between devices, swap(): return lax.ppermute(value, axis, [(j, j ^ bit) for j in range(n)])  112 us
    pallas_call x13, Pallas kernels, call(): pl.pallas_call(kernel, out_shape=outs, scratch_shapes=list(scratch), comp...  89.3 us
    ppermute x23, starting transfers between devices, swap(): return lax.ppermute(value, axis, [(j, j ^ bit) for j in range(n)])  31.2 us
    all_to_all x2, waiting for transfers between devices, scatter_all(): return lax.all_to_all(blocks, 'tp', 0, 0, tiled=True)  26.7 us
    dot_general x5, matrix products, mm_tn(): lax.dot_general(left, right, (((0,), (0,)), ((), ())), preferred_element_...  16.9 us
    unnamed x84, local copies, waits for them, and re-layouts  11 us
    all_to_all x2, starting transfers between devices, scatter_all(): return lax.all_to_all(blocks, 'tp', 0, 0, tiled=True)  9.59 us
  transfers between devices with their start and end apart: 32, of which 17 were waited for; matrix products, arithmetic and copies ran while one was open for 12% of the time, Pallas kernels for 21%

profile of v3, /device:TPU:0, one launch (start us, length us, event | category | flops | bytes accessed | tf_op | source)
XLA Modules:
  0.0 357.6 jit_solution(5215707768655812737)
XLA Ops:
  12.6 4.1 %collective-permute-start.1 = (bf16[128,1536]{1,0:T(8,128)(2,1)S(1)}, bf16[128,1536]{1,0:T(8,128)(2,1)S(1)}, u32[]{:S(2)}, u32[]{:S(2)}) collective-permute-start(bf16[128,1536]{1,0:T(8,128)(2,1)S(1)} %bitcast.57), channel_id=1, source_target_pairs={{0,2},{1,3},{2,0},{3,1},{4,6},{5,7},{6,4},{7,5},{8,10},{9,11},{10,... | collective-permute-start | bytes 1179656 | tf_op jit(solution)/shard_map/ppermute | solution.py:63
  19.0 15.4 %collective-permute-done.1.refs_2_ = bf16[128,1536]{1,0:T(8,128)(2,1)S(1)} collective-permute-done((bf16[128,1536]{1,0:T(8,128)(2,1)S(1)}, bf16[128,1536]{1,0:T(8,128)(2,1)S(1)}, u32[]{:S(2)}, u32[]{:S(2)}) %collective-permute-start.1) | collective-permute-done | bytes 393248 | tf_op jit(solution)/shard_map/ppermute | solution.py:63
  35.2 9.5 %collective-permute-done.2.refs_3_ = bf16[128,1536]{1,0:T(8,128)(2,1)S(1)} collective-permute-done((bf16[128,1536]{1,0:T(8,128)(2,1)S(1)}, bf16[128,1536]{1,0:T(8,128)(2,1)S(1)}, u32[]{:S(2)}, u32[]{:S(2)}) %collective-permute-start.2) | collective-permute-done | bytes 393248 | tf_op jit(solution)/shard_map/ppermute | solution.py:63
  46.0 5.5 %all-to-all-start = ((bf16[4,128,1536]{2,1,0:T(8,128)(2,1)}), bf16[4,128,1536]{2,1,0:T(8,128)(2,1)S(1)}, u32[]{:S(2)}, u32[]{:S(2)}) async-start(bf16[4,128,1536]{2,1,0:T(8,128)(2,1)} %broadcast_in_dim.38), calls=%async_computation | async-start | bytes 3145728 | tf_op jit(solution)/shard_map/all_to_all | solution.py:77
  54.2 5.3 %all-gather.3.cloned.1.call-done.refs_4_.wout_ref.refs_15_ = bf16[1536,2048]{1,0:T(8,128)(2,1)} async-done(((bf16[192,2048]{1,0:T(8,128)(2,1)}), bf16[1536,2048]{1,0:T(8,128)(2,1)}) %all-gather.3.cloned.1.call-update) | async-done | bytes 6291472 | tf_op jit(solution)/shard_map/all_gather | solution.py:505
  59.6 11.2 %shard_map.220 = (bf16[512,1536]{1,0:T(8,128)(2,1)}, bf16[512,768]{1,0:T(8,128)(2,1)}, bf16[512,768]{1,0:T(8,128)(2,1)}, bf16[512,768]{1,0:T(8,128)(2,1)}, bf16[...) custom-call(bf16[128,1536]{1,0:T(8,128)(2,1)} %bitcast.53, ...), custom_call_target="tpu_custom_call" | custom-call | flops 100000000 | bytes 100000 | tf_op jit(solution)/shard_map/pallas_call | solution.py:47
  76.2 9.3 %shard_map.221 = (bf16[512,384]{1,0:T(8,128)(2,1)}, f32[512,384]{1,0:T(8,128)}, f32[512,128]{1,0:T(8,128)}, bf16[512,768]{1,0:T(8,128)(2,1)}, bf16[512,768]{1,0:...) custom-call(bf16[512,768]{1,0:T(8,128)(2,1)} %get-tuple-element.86.q, ...), custom_call_target="tpu_custom_call" | custom-call | flops 100000000 | bytes 100000 | tf_op jit(solution)/shard_map/pallas_call | solution.py:47
  89.9 10.2 %collective-permute-done.5 = bf16[128,1536]{1,0:T(8,128)(2,1)S(1)} collective-permute-done((bf16[128,1536]{1,0:T(8,128)(2,1)}, bf16[128,1536]{1,0:T(8,128)(2,1)S(1)}, u32[]{:S(2)}, u32[]{:S(2)}) %collective-permute-start.5) | collective-permute-done | bytes 393248 | tf_op jit(solution)/shard_map/ppermute | solution.py:63
  101.9 10.6 %collective-permute-done.4.refs_1_ = bf16[128,1536]{1,0:T(8,128)(2,1)S(1)} collective-permute-done((bf16[128,1536]{1,0:T(8,128)(2,1)}, bf16[128,1536]{1,0:T(8,128)(2,1)S(1)}, u32[]{:S(2)}, u32[]{:S(2)}) %collective-permute-start.4) | collective-permute-done | bytes 393248 | tf_op jit(solution)/shard_map/ppermute | solution.py:63
  112.6 5.8 %collective-permute-done.6.refs_2_ = bf16[128,1536]{1,0:T(8,128)(2,1)S(1)} collective-permute-done((bf16[128,1536]{1,0:T(8,128)(2,1)S(1)}, bf16[128,1536]{1,0:T(8,128)(2,1)S(1)}, u32[]{:S(2)}, u32[]{:S(2)}) %collective-permute-start.6) | collective-permute-done | bytes 393248 | tf_op jit(solution)/shard_map/ppermute | solution.py:63
  121.8 3.5 collective-permute-start.7
  125.3 11.1 %collective-permute-done.8.refs_2_ = bf16[128,1536]{1,0:T(8,128)(2,1)S(1)} collective-permute-done((bf16[128,1536]{1,0:T(8,128)(2,1)}, bf16[128,1536]{1,0:T(8,128)(2,1)S(1)}, u32[]{:S(2)}, u32[]{:S(2)}) %collective-permute-start.8) | collective-permute-done | bytes 393248 | tf_op jit(solution)/shard_map/ppermute | solution.py:63
  137.2 5.4 %shard_map.223 = (f32[512,1024]{1,0:T(8,128)}, bf16[512,1536]{1,0:T(8,128)(2,1)}) custom-call(bf16[4,128,1536]{2,1,0:T(8,128)(2,1)} %copy-done.2, bf16[1536,3072]{1,0:T(8,128)(2,1)} %all-gather.5.cloned.1.call-done.wd_ref.refs_5_.refs_6_), custom_call_target="tpu_custom_call" | custom-call | flops 100000000 | bytes 100000 | tf_op jit(solution)/shard_map/pallas_call | solution.py:47
  146.0 13.6 %shard_map.224 = (bf16[512,1536]{1,0:T(8,128)(2,1)}, bf16[512,1024]{1,0:T(8,128)(2,1)}, bf16[512,2048]{1,0:T(8,128)(2,1)}, bf16[128,1536]{1,0:T(8,128)(2,1)}, bf...) custom-call(bf16[128,1536]{1,0:T(8,128)(2,1)} %get-tuple-element.104.refs_0_, ...), custom_call_target="tpu_custom_call" | custom-call | flops 100000000 | bytes 100000 | tf_op jit(solution)/shard_map/pallas_call | solution.py:47
  161.5 3.7 %convolution_convert_fusion.2 = bf16[1536,1024]{1,0:T(8,128)(2,1)S(1)} fusion(bf16[512,1536]{1,0:T(8,128)(2,1)} %get-tuple-element.115, bf16[512,1024]{1,0:T(8,128)(2,1)} %get-tuple-element.120.hid_ref), kind=kOutput, calls=%fused_computation.3 | convolution fusion | flops 1612185600 | bytes 5767168 | tf_op jit(solution)/shard_map/dot_general | solution.py:27
  165.2 3.7 %convolution_convert_fusion.1 = bf16[1536,2048]{1,0:T(8,128)(2,1)S(1)} fusion(bf16[512,1536]{1,0:T(8,128)(2,1)S(1)} %copy-done.32, bf16[512,2048]{1,0:T(8,128)(2,1)S(1)} %copy-done.31), kind=kOutput, calls=%fused_computation.2 | convolution fusion | flops 3224371200 | bytes 9961472 | tf_op jit(solution)/shard_map/dot_general | solution.py:27
  168.9 4.6 %pad_maximum_fusion = bf16[1536,3072]{1,0:T(8,128)(2,1)} fusion(bf16[1536,1024]{1,0:T(8,128)(2,1)S(1)} %convolution_convert_fusion.2, bf16[1536,2048]{1,0:T(8,128)(2,1)S(1)} %convolution_convert_fusion.1), kind=kLoop, calls=%fused_computation | loop fusion | flops 18874368 | bytes 18874368 | tf_op jit(solution)/shard_map/concatenate | solution.py:576
  174.9 8.4 %collective-permute-done.11 = bf16[128,1536]{1,0:T(8,128)(2,1)S(1)} collective-permute-done((bf16[128,1536]{1,0:T(8,128)(2,1)S(1)}, bf16[128,1536]{1,0:T(8,128)(2,1)S(1)}, u32[]{:S(2)}, u32[]{:S(2)}) %collective-permute-start.11) | collective-permute-done | bytes 393248 | tf_op jit(solution)/shard_map/ppermute | solution.py:63
  183.3 4.7 %collective-permute-start.12 = (bf16[128,1536]{1,0:T(8,128)(2,1)S(1)}, bf16[128,1536]{1,0:T(8,128)(2,1)S(1)}, u32[]{:S(2)}, u32[]{:S(2)}) collective-permute-start(bf16[128,1536]{1,0:T(8,128)(2,1)S(1)} %add_convert_fusion), channel_id=1, source_target_pairs={{0,2},{1,3},{2,0},{3,1},{4,6},{5,7},{6,4},{7,5},{8,10},{9,11},{10,... | collective-permute-start | bytes 1179656 | tf_op jit(solution)/shard_map/ppermute | solution.py:63
  188.0 13.4 %collective-permute-done.12.refs_2_ = bf16[128,1536]{1,0:T(8,128)(2,1)S(1)} collective-permute-done((bf16[128,1536]{1,0:T(8,128)(2,1)S(1)}, bf16[128,1536]{1,0:T(8,128)(2,1)S(1)}, u32[]{:S(2)}, u32[]{:S(2)}) %collective-permute-start.12) | collective-permute-done | bytes 393248 | tf_op jit(solution)/shard_map/ppermute | solution.py:63
  205.5 3.5 collective-permute-start.13
  209.0 15.4 %collective-permute-done.14.refs_2_ = bf16[128,1536]{1,0:T(8,128)(2,1)S(1)} collective-permute-done((bf16[128,1536]{1,0:T(8,128)(2,1)}, bf16[128,1536]{1,0:T(8,128)(2,1)S(1)}, u32[]{:S(2)}, u32[]{:S(2)}) %collective-permute-start.14) | collective-permute-done | bytes 393248 | tf_op jit(solution)/shard_map/ppermute | solution.py:63
  224.4 5.5 %shard_map.226 = bf16[4,128,1536]{2,1,0:T(8,128)(2,1)} custom-call(bf16[512,1024]{1,0:T(8,128)(2,1)} %get-tuple-element.120.hid_ref, bf16[1536,3072]{1,0:T(8,128)(2,1)} %all-gather.5.cloned.1.call-done.wd_ref.refs_5_.refs_6_), custom_call_target="tpu_custom_call" | custom-call | flops 100000000 | bytes 100000 | tf_op jit(solution)/shard_map/pallas_call | solution.py:47
  229.9 3.9 %collective-permute-done.15.refs_3_ = bf16[128,1536]{1,0:T(8,128)(2,1)S(1)} collective-permute-done((bf16[128,1536]{1,0:T(8,128)(2,1)S(1)}, bf16[128,1536]{1,0:T(8,128)(2,1)S(1)}, u32[]{:S(2)}, u32[]{:S(2)}) %collective-permute-start.15) | collective-permute-done | bytes 393248 | tf_op jit(solution)/shard_map/ppermute | solution.py:63
  233.8 4.5 %all-to-all-start.1 = ((bf16[4,128,1536]{2,1,0:T(8,128)(2,1)}), bf16[4,128,1536]{2,1,0:T(8,128)(2,1)S(1)}, u32[]{:S(2)}, u32[]{:S(2)}) async-start(bf16[4,128,1536]{2,1,0:T(8,128)(2,1)} %shard_map.226), calls=%async_computation.1 | async-start | bytes 3145728 | tf_op jit(solution)/shard_map/all_to_all | solution.py:81
  238.3 15.7 %shard_map.227 = (bf16[512,1536]{1,0:T(8,128)(2,1)}, f32[512,384]{1,0:T(8,128)}, f32[512,384]{1,0:T(8,128)}, f32[512,384]{1,0:T(8,128)}, bf16[512,896]{1,0:T(8,1...) custom-call(bf16[128,1536]{1,0:T(8,128)(2,1)} %get-tuple-element.124.refs_0_, bf16[128,1536]{1,0:T(8,128)(2,1)} %copy-done.35, ...), custom_call_target="tpu_custom_call" | custom-call | flops 99999997952 | bytes 100000000 | tf_op jit(solution)/shard_map/pallas_call | solution.py:47
  261.8 11.7 %shard_map.228 = (bf16[512,1664]{1,0:T(8,128)(2,1)}, bf16[4,144,1536]{2,1,0:T(8,128)(2,1)}) custom-call(bf16[128,1536]{1,0:T(8,128)(2,1)} %bitcast.55, bf16[128,1536]{1,0:T(8,128)(2,1)} %copy-done.6, bf16[128,1536]{1,0:T(8,128)(2,1)} %copy-done.5, bf16[128,1536]{1,0:T(8,128)(2,1)} %copy-done.7, ...), custom_call_target="tpu_custom_call" | custom-call | flops 100000000 | bytes 100000 | tf_op jit(solution)/shard_map/pallas_call | solution.py:47
  273.5 5.9 %convolution_convert_fusion = bf16[1536,1280]{1,0:T(8,128)(2,1)} fusion(bf16[512,1536]{1,0:T(8,128)(2,1)} %get-tuple-element.149, bf16[512,1664]{1,0:T(8,128)(2,1)} %get-tuple-element.141), kind=kOutput, calls=%fused_computation.1 | convolution fusion | flops 2015232000 | bytes 6815744 | tf_op jit(solution)/shard_map/dot_general | solution.py:27
  281.4 5.1 %all-to-all-start.2 = ((bf16[4,144,1536]{2,1,0:T(8,128)(2,1)}), bf16[4,144,1536]{2,1,0:T(8,128)(2,1)S(1)}, u32[]{:S(2)}, u32[]{:S(2)}) async-start(bf16[4,144,1536]{2,1,0:T(8,128)(2,1)} %get-tuple-element.146), calls=%async_computation.3 | async-start | bytes 3538944 | tf_op jit(solution)/shard_map/all_to_all | solution.py:81
  290.9 3.9 %collective-permute-done.17 = bf16[4,192,1280]{2,1,0:T(8,128)(2,1)} collective-permute-done((bf16[4,192,1280]{2,1,0:T(8,128)(2,1)}, bf16[4,192,1280]{2,1,0:T(8,128)(2,1)}, u32[]{:S(2)}, u32[]{:S(2)}) %collective-permute-start.17) | collective-permute-done | bytes 1966112 | tf_op jit(solution)/shard_map/ppermute | solution.py:63
  294.8 3.8 %convert_add_fusion = (f32[192,1280]{1,0:T(8,128)}, bf16[192,1280]{1,0:T(8,128)(2,1)}, bf16[192,1280]{1,0:T(8,128)(2,1)}, bf16[192,1280]{1,0:T(8,128)(2,1)}) fusion(bf16[4,192,1280]{2,1,0:T(8,128)(2,1)} %collective-permute-done.17, s32[]{:T(128)S(6)} %select_n.47, bf16[4,2,192,1280]{3,2,1,0:T(8,128)(2,1)} %bitcast.60, s32[]{:T(128)S(6)} %select_n.48, ...), kind=kLoop, calls=%fused_computation.11 | loop fusion | flops 3686400 | bytes 6389796 | tf_op jit(solution)/shard_map/add | solution.py:111
  302.3 26.7 %all-to-all-done.2.refs_0_ = bf16[4,144,1536]{2,1,0:T(8,128)(2,1)S(1)} async-done(((bf16[4,144,1536]{2,1,0:T(8,128)(2,1)}), bf16[4,144,1536]{2,1,0:T(8,128)(2,1)S(1)}, u32[]{:S(2)}, u32[]{:S(2)}) %all-to-all-start.2) | async-done | bytes 1769504 | tf_op jit(solution)/shard_map/all_to_all | solution.py:81
  (173 shorter events, 77.8 us)
Async XLA Ops:
  7.2 52.4 %all-gather.3.cloned.1.call-start = ((), (), s32[]{:S(2)}) async-start(), calls=%async_computation.5 | async-start | bytes 7077888 | tf_op jit(solution)/shard_map/all_gather | solution.py:505
  11.2 126.0 %all-gather.5.cloned.1.call-start = ((), (), s32[]{:S(2)}) async-start(), calls=%async_computation.6 | async-start | bytes 10616832 | tf_op jit(solution)/shard_map/all_gather | solution.py:507
  12.6 21.7 %collective-permute-start.1 = (bf16[128,1536]{1,0:T(8,128)(2,1)S(1)}, bf16[128,1536]{1,0:T(8,128)(2,1)S(1)}, u32[]{:S(2)}, u32[]{:S(2)}) collective-permute-start(bf16[128,1536]{1,0:T(8,128)(2,1)S(1)} %bitcast.57), channel_id=1, source_target_pairs={{0,2},{1,3},{2,0},{3,1},{4,6},{5,7},{6,4},{7,5},{8,10},{9,11},{10,... | collective-permute-start | bytes 1179656 | tf_op jit(solution)/shard_map/ppermute | solution.py:63
  16.8 18.4 %collective-permute-start = (bf16[128,1536]{1,0:T(8,128)(2,1)S(1)}, bf16[128,1536]{1,0:T(8,128)(2,1)S(1)}, u32[]{:S(2)}, u32[]{:S(2)}) collective-permute-start(bf16[128,1536]{1,0:T(8,128)(2,1)S(1)} %bitcast.58), channel_id=1, source_target_pairs={{0,1},{1,0},{2,3},{3,2},{4,5},{5,4},{6,7},{7,6},{8,9},{9,8},{10,11... | collective-permute-start | bytes 1179656 | tf_op jit(solution)/shard_map/ppermute | solution.py:63
  34.4 10.2 %collective-permute-start.2 = (bf16[128,1536]{1,0:T(8,128)(2,1)S(1)}, bf16[128,1536]{1,0:T(8,128)(2,1)S(1)}, u32[]{:S(2)}, u32[]{:S(2)}) collective-permute-start(bf16[128,1536]{1,0:T(8,128)(2,1)S(1)} %collective-permute-done.1.refs_2_), channel_id=1, source_target_pairs={{0,1},{1,0},{2,3},{3,2},{4,5},{5,4},{6,7},{7,6},{8,9},{9,8},{10,11... | collective-permute-start | bytes 1179656 | tf_op jit(solution)/shard_map/ppermute | solution.py:63
  46.0 41.9 %all-to-all-start = ((bf16[4,128,1536]{2,1,0:T(8,128)(2,1)}), bf16[4,128,1536]{2,1,0:T(8,128)(2,1)S(1)}, u32[]{:S(2)}, u32[]{:S(2)}) async-start(bf16[4,128,1536]{2,1,0:T(8,128)(2,1)} %broadcast_in_dim.38), calls=%async_computation | async-start | bytes 3145728 | tf_op jit(solution)/shard_map/all_to_all | solution.py:77
  51.5 229.9 %reduce-scatter.3.cloned.1.call-start = ((), (), s32[]{:S(2)}) async-start(), calls=%async_computation.7 | async-start | bytes 10616832 | tf_op jit(solution)/shard_map/reduce_scatter | solution.py:577
  70.7 4.5 %collective-permute-start.3 = (bf16[512,896]{1,0:T(8,128)(2,1)}, bf16[512,896]{1,0:T(8,128)(2,1)S(1)}, u32[]{:S(2)}, u32[]{:S(2)}) collective-permute-start(bf16[512,896]{1,0:T(8,128)(2,1)} %get-tuple-element.89), channel_id=1, source_target_pairs={{0,4},{1,5},{2,6},{3,7},{8,12},{9,13},{10,14},{11,15},{16,20},{17,... | collective-permute-start | bytes 2752520 | tf_op jit(solution)/shard_map/ppermute | solution.py:534
  87.9 12.3 %collective-permute-start.5 = (bf16[128,1536]{1,0:T(8,128)(2,1)}, bf16[128,1536]{1,0:T(8,128)(2,1)S(1)}, u32[]{:S(2)}, u32[]{:S(2)}) collective-permute-start(bf16[128,1536]{1,0:T(8,128)(2,1)} %get-tuple-element.99), channel_id=1, source_target_pairs={{0,1},{1,0},{2,3},{3,2},{4,5},{5,4},{6,7},{7,6},{8,9},{9,8},{10,11... | collective-permute-start | bytes 1179656 | tf_op jit(solution)/shard_map/ppermute | solution.py:63
  87.9 24.7 %collective-permute-start.4 = (bf16[128,1536]{1,0:T(8,128)(2,1)}, bf16[128,1536]{1,0:T(8,128)(2,1)S(1)}, u32[]{:S(2)}, u32[]{:S(2)}) collective-permute-start(bf16[128,1536]{1,0:T(8,128)(2,1)} %get-tuple-element.97), channel_id=1, source_target_pairs={{0,1},{1,0},{2,3},{3,2},{4,5},{5,4},{6,7},{7,6},{8,9},{9,8},{10,11... | collective-permute-start | bytes 1179656 | tf_op jit(solution)/shard_map/ppermute | solution.py:63
  101.2 17.2 %collective-permute-start.6 = (bf16[128,1536]{1,0:T(8,128)(2,1)S(1)}, bf16[128,1536]{1,0:T(8,128)(2,1)S(1)}, u32[]{:S(2)}, u32[]{:S(2)}) collective-permute-start(bf16[128,1536]{1,0:T(8,128)(2,1)S(1)} %add_convert_fusion.1), channel_id=1, source_target_pairs={{0,2},{1,3},{2,0},{3,1},{4,6},{5,7},{6,4},{7,5},{8,10},{9,11},{10,... | collective-permute-start | bytes 1179656 | tf_op jit(solution)/shard_map/ppermute | solution.py:63
  121.8 14.6 %collective-permute-start.8 = (bf16[128,1536]{1,0:T(8,128)(2,1)}, bf16[128,1536]{1,0:T(8,128)(2,1)S(1)}, u32[]{:S(2)}, u32[]{:S(2)}) collective-permute-start(bf16[128,1536]{1,0:T(8,128)(2,1)} %get-tuple-element.104.refs_0_), channel_id=1, source_target_pairs={{0,2},{1,3},{2,0},{3,1},{4,6},{5,7},{6,4},{7,5},{8,10},{9,11},{10,... | collective-permute-start | bytes 1179656 | tf_op jit(solution)/shard_map/ppermute | solution.py:63
  121.8 20.8 %collective-permute-start.7 = (bf16[128,1536]{1,0:T(8,128)(2,1)}, bf16[128,1536]{1,0:T(8,128)(2,1)S(1)}, u32[]{:S(2)}, u32[]{:S(2)}) collective-permute-start(bf16[128,1536]{1,0:T(8,128)(2,1)} %get-tuple-element.104.refs_0_), channel_id=1, source_target_pairs={{0,1},{1,0},{2,3},{3,2},{4,5},{5,4},{6,7},{7,6},{8,9},{9,8},{10,11... | collective-permute-start | bytes 1179656 | tf_op jit(solution)/shard_map/ppermute | solution.py:63
  136.4 8.9 %collective-permute-start.9 = (bf16[128,1536]{1,0:T(8,128)(2,1)S(1)}, bf16[128,1536]{1,0:T(8,128)(2,1)S(1)}, u32[]{:S(2)}, u32[]{:S(2)}) collective-permute-start(bf16[128,1536]{1,0:T(8,128)(2,1)S(1)} %collective-permute-done.8.refs_2_), channel_id=1, source_target_pairs={{0,1},{1,0},{2,3},{3,2},{4,5},{5,4},{6,7},{7,6},{8,9},{9,8},{10,11... | collective-permute-start | bytes 1179656 | tf_op jit(solution)/shard_map/ppermute | solution.py:63
  159.7 13.8 %collective-permute-start.10 = (bf16[128,1536]{1,0:T(8,128)(2,1)}, bf16[128,1536]{1,0:T(8,128)(2,1)S(1)}, u32[]{:S(2)}, u32[]{:S(2)}) collective-permute-start(bf16[128,1536]{1,0:T(8,128)(2,1)} %get-tuple-element.110), channel_id=1, source_target_pairs={{0,1},{1,0},{2,3},{3,2},{4,5},{5,4},{6,7},{7,6},{8,9},{9,8},{10,11... | collective-permute-start | bytes 1179656 | tf_op jit(solution)/shard_map/ppermute | solution.py:63
  174.6 8.7 %collective-permute-start.11 = (bf16[128,1536]{1,0:T(8,128)(2,1)S(1)}, bf16[128,1536]{1,0:T(8,128)(2,1)S(1)}, u32[]{:S(2)}, u32[]{:S(2)}) collective-permute-start(bf16[128,1536]{1,0:T(8,128)(2,1)S(1)} %copy-done.36), channel_id=1, source_target_pairs={{0,1},{1,0},{2,3},{3,2},{4,5},{5,4},{6,7},{7,6},{8,9},{9,8},{10,11... | collective-permute-start | bytes 1179656 | tf_op jit(solution)/shard_map/ppermute | solution.py:63
  183.3 18.1 %collective-permute-start.12 = (bf16[128,1536]{1,0:T(8,128)(2,1)S(1)}, bf16[128,1536]{1,0:T(8,128)(2,1)S(1)}, u32[]{:S(2)}, u32[]{:S(2)}) collective-permute-start(bf16[128,1536]{1,0:T(8,128)(2,1)S(1)} %add_convert_fusion), channel_id=1, source_target_pairs={{0,2},{1,3},{2,0},{3,1},{4,6},{5,7},{6,4},{7,5},{8,10},{9,11},{10,... | collective-permute-start | bytes 1179656 | tf_op jit(solution)/shard_map/ppermute | solution.py:63
  205.4 19.0 %collective-permute-start.14 = (bf16[128,1536]{1,0:T(8,128)(2,1)}, bf16[128,1536]{1,0:T(8,128)(2,1)S(1)}, u32[]{:S(2)}, u32[]{:S(2)}) collective-permute-start(bf16[128,1536]{1,0:T(8,128)(2,1)} %get-tuple-element.124.refs_0_), channel_id=1, source_target_pairs={{0,2},{1,3},{2,0},{3,1},{4,6},{5,7},{6,4},{7,5},{8,10},{9,11},{10,... | collective-permute-start | bytes 1179656 | tf_op jit(solution)/shard_map/ppermute | solution.py:63
  205.5 24.4 %collective-permute-start.13 = (bf16[128,1536]{1,0:T(8,128)(2,1)}, bf16[128,1536]{1,0:T(8,128)(2,1)S(1)}, u32[]{:S(2)}, u32[]{:S(2)}) collective-permute-start(bf16[128,1536]{1,0:T(8,128)(2,1)} %get-tuple-element.124.refs_0_), channel_id=1, source_target_pairs={{0,1},{1,0},{2,3},{3,2},{4,5},{5,4},{6,7},{7,6},{8,9},{9,8},{10,11... | collective-permute-start | bytes 1179656 | tf_op jit(solution)/shard_map/ppermute | solution.py:63
  224.4 9.4 %collective-permute-start.15 = (bf16[128,1536]{1,0:T(8,128)(2,1)S(1)}, bf16[128,1536]{1,0:T(8,128)(2,1)S(1)}, u32[]{:S(2)}, u32[]{:S(2)}) collective-permute-start(bf16[128,1536]{1,0:T(8,128)(2,1)S(1)} %collective-permute-done.14.refs_2_), channel_id=1, source_target_pairs={{0,1},{1,0},{2,3},{3,2},{4,5},{5,4},{6,7},{7,6},{8,9},{9,8},{10,11... | collective-permute-start | bytes 1179656 | tf_op jit(solution)/shard_map/ppermute | solution.py:63
  233.8 45.6 %all-to-all-start.1 = ((bf16[4,128,1536]{2,1,0:T(8,128)(2,1)}), bf16[4,128,1536]{2,1,0:T(8,128)(2,1)S(1)}, u32[]{:S(2)}, u32[]{:S(2)}) async-start(bf16[4,128,1536]{2,1,0:T(8,128)(2,1)} %shard_map.226), calls=%async_computation.1 | async-start | bytes 3145728 | tf_op jit(solution)/shard_map/all_to_all | solution.py:81
  254.1 6.8 %collective-permute-start.16 = (bf16[512,896]{1,0:T(8,128)(2,1)}, bf16[512,896]{1,0:T(8,128)(2,1)S(1)}, u32[]{:S(2)}, u32[]{:S(2)}) collective-permute-start(bf16[512,896]{1,0:T(8,128)(2,1)} %get-tuple-element.136), channel_id=1, source_target_pairs={{4,0},{5,1},{6,2},{7,3},{12,8},{13,9},{14,10},{15,11},{20,16},{21,... | collective-permute-start | bytes 2752520 | tf_op jit(solution)/shard_map/ppermute | solution.py:606
  281.4 47.6 %all-to-all-start.2 = ((bf16[4,144,1536]{2,1,0:T(8,128)(2,1)}), bf16[4,144,1536]{2,1,0:T(8,128)(2,1)S(1)}, u32[]{:S(2)}, u32[]{:S(2)}) async-start(bf16[4,144,1536]{2,1,0:T(8,128)(2,1)} %get-tuple-element.146), calls=%async_computation.3 | async-start | bytes 3538944 | tf_op jit(solution)/shard_map/all_to_all | solution.py:81
  286.5 62.6 %reduce-scatter.5.cloned.1.call-start = ((), (), s32[]{:S(2)}) async-start(), calls=%async_computation.8 | async-start | bytes 2654208 | tf_op jit(solution)/shard_map/reduce_scatter | solution.py:615
  290.0 4.8 %collective-permute-start.17 = (bf16[4,192,1280]{2,1,0:T(8,128)(2,1)}, bf16[4,192,1280]{2,1,0:T(8,128)(2,1)}, u32[]{:S(2)}, u32[]{:S(2)}) collective-permute-start(bf16[4,192,1280]{2,1,0:T(8,128)(2,1)} %dynamic-slice_bitcast_fusion), channel_id=1, source_target_pairs={{0,4},{4,0},{1,5},{5,1},{2,6},{6,2},{3,7},{7,3},{8,12},{12,8},{9,1... | collective-permute-start | bytes 5898248 | tf_op jit(solution)/shard_map/ppermute | solution.py:63
  298.6 30.6 %collective-permute-start.18 = (bf16[192,1280]{1,0:T(8,128)(2,1)}, bf16[192,1280]{1,0:T(8,128)(2,1)S(1)}, u32[]{:S(2)}, u32[]{:S(2)}) collective-permute-start(bf16[192,1280]{1,0:T(8,128)(2,1)} %get-tuple-element.189), channel_id=1, source_target_pairs={{0,8},{8,0},{16,24},{24,16},{1,9},{9,1},{17,25},{25,17},{2,10},{10... | collective-permute-start | bytes 1474568 | tf_op jit(solution)/shard_map/ppermute | solution.py:63
  299.7 29.5 %collective-permute-start.19 = (bf16[192,1280]{1,0:T(8,128)(2,1)}, bf16[192,1280]{1,0:T(8,128)(2,1)S(1)}, u32[]{:S(2)}, u32[]{:S(2)}) collective-permute-start(bf16[192,1280]{1,0:T(8,128)(2,1)} %get-tuple-element.188), channel_id=1, source_target_pairs={{0,16},{8,24},{16,0},{24,8},{1,17},{9,25},{17,1},{25,9},{2,18},{10... | collective-permute-start | bytes 1474568 | tf_op jit(solution)/shard_map/ppermute | solution.py:63
  302.3 28.3 %collective-permute-start.20 = (bf16[192,1280]{1,0:T(8,128)(2,1)}, bf16[192,1280]{1,0:T(8,128)(2,1)S(1)}, u32[]{:S(2)}, u32[]{:S(2)}) collective-permute-start(bf16[192,1280]{1,0:T(8,128)(2,1)} %get-tuple-element.187), channel_id=1, source_target_pairs={{0,24},{8,16},{16,8},{24,0},{1,25},{9,17},{17,9},{25,1},{2,26},{10... | collective-permute-start | bytes 1474568 | tf_op jit(solution)/shard_map/ppermute | solution.py:63
  329.2 8.2 %collective-permute-start.21 = (f32[3224]{0:T(1024)S(1)}, f32[3224]{0:T(1024)S(1)}, u32[]{:S(2)}, u32[]{:S(2)}) collective-permute-start(f32[3224]{0:T(1024)S(1)} %concatenate.27), channel_id=1, source_target_pairs={{0,4},{4,0},{1,5},{5,1},{2,6},{6,2},{3,7},{7,3},{8,12},{12,8},{9,1... | collective-permute-start | bytes 38696 | tf_op jit(solution)/shard_map/ppermute | solution.py:63
  337.4 9.8 %collective-permute-start.24 = (f32[3224]{0:T(1024)S(1)}, f32[3224]{0:T(1024)S(1)}, u32[]{:S(2)}, u32[]{:S(2)}) collective-permute-start(f32[3224]{0:T(1024)S(1)} %add.145), channel_id=1, source_target_pairs={{0,24},{8,16},{16,8},{24,0},{1,25},{9,17},{17,9},{25,1},{2,26},{10... | collective-permute-start | bytes 38696 | tf_op jit(solution)/shard_map/ppermute | solution.py:63
  339.6 7.6 %collective-permute-start.23 = (f32[3224]{0:T(1024)S(1)}, f32[3224]{0:T(1024)S(1)}, u32[]{:S(2)}, u32[]{:S(2)}) collective-permute-start(f32[3224]{0:T(1024)S(1)} %add.145), channel_id=1, source_target_pairs={{0,16},{8,24},{16,0},{24,8},{1,17},{9,25},{17,1},{25,9},{2,18},{10... | collective-permute-start | bytes 38696 | tf_op jit(solution)/shard_map/ppermute | solution.py:63
  340.5 6.6 %collective-permute-start.22 = (f32[3224]{0:T(1024)S(1)}, f32[3224]{0:T(1024)S(1)}, u32[]{:S(2)}, u32[]{:S(2)}) collective-permute-start(f32[3224]{0:T(1024)S(1)} %add.145), channel_id=1, source_target_pairs={{0,8},{8,0},{16,24},{24,16},{1,9},{9,1},{17,25},{25,17},{2,10},{10... | collective-permute-start | bytes 38696 | tf_op jit(solution)/shard_map/ppermute | solution.py:63
  (40 other events, 270.6 us)
Sparse Core Ops, SparseCore 0:
  11.3 48.2 all-gather.2
  61.5 58.8 all-gather.4
  173.6 76.4 reduce-scatter.2
  290.3 54.3 reduce-scatter.4

commit v4 on v3

--- a/solution.py
+++ b/solution.py
@@ -81,37 +81,18 @@
     return lax.all_to_all(blocks, "tp", 0, 0, tiled=True)
 
 
-def send_rows(parts):
+def send_rows(parts, *late):
     n = lax.axis_size("tp")
     if n != 4:
         return [parts[0]] + [swap(parts[k], "tp", k) for k in range(1, n)]
     across = swap(parts[3], "tp", 1)
-    near = swap(parts[1], "tp", 1)
+    near = swap(after(parts[1], *late) if late else parts[1], "tp", 1)
     far = (parts[2].astype(f32) + across.astype(f32)).astype(bf16)
     return [parts[0], near, swap(far, "tp", 2)]
 
 
 def after(value, *others):
     return lax.optimization_barrier((value, others))[0]
-
-
-def pick(value, index, axis=0):
-    return lax.dynamic_index_in_dim(value, index, axis, keepdims=False)
-
-
-def scatter_weight(part):
-    shards, halves = lax.axis_size("shard"), lax.axis_size("ctx")
-    me, half = lax.axis_index("shard"), lax.axis_index("ctx")
-    width, cols = part.shape
-    blocks = part.reshape(shards, halves, width // (shards * halves), cols)
-    got = swap(pick(blocks, 1 - half, 1), "ctx", 1)
-    keep = pick(blocks, half, 1)
-
-    def pair(k):
-        return pick(keep, me ^ k).astype(f32) + pick(got, me ^ k).astype(f32)
-
-    arrived = [swap(pair(k).astype(bf16), "shard", k) for k in range(1, shards)]
-    return pair(0), arrived
 
 
 def sum_over(value, axes):
@@ -241,7 +222,7 @@
         branch_refs[c][...] = branch[c * step : (c + 1) * step, :]
 
 
-def hidden_back_kernel(chunks, cot_ref, wd_ref, dh_ref, order_ref):
+def hidden_back_kernel(chunks, cot_ref, normed_ref, wd_ref, dh_ref, order_ref, flip_ref):
     me = lax.axis_index("tp")
     rows = cot_ref.shape[1]
 
@@ -249,6 +230,7 @@
     def _():
         for c in range(chunks):
             order_ref[c * rows : (c + 1) * rows, :] = cot_ref[pl.ds(me ^ c, 1)][0]
+        flip_ref[...] = jnp.transpose(normed_ref[...])
 
     dh_ref[...] = mm(order_ref[...], wd_ref[...])
 
@@ -361,7 +343,7 @@
     x_refs, refs = refs[:chunks], refs[chunks:]
     (w_ref, qk_ref, qraw_ref, kraw_ref, dq_ref, dk_ref, dv_ref, back_ref, dopen_ref, dcum_ref, pre_ref, rank_ref,
      rank_t_ref, gm_ref) = refs[:14]
-    mixed_ref, out_ref = refs[14:]
+    mixed_ref, out_refs = refs[14], refs[15:]
     cols = heads * size
     width = x_refs[0].shape[1]
     rows = x_refs[0].shape[0]
@@ -399,7 +381,7 @@
         gain = jnp.zeros((1, 256), f32)
         for c in range(chunks):
             piece = dn[c * rows : (c + 1) * rows, :]
-            out_ref[pl.ds(me ^ c, 1), 0:rows, b : b + 256] = piece.astype(bf16)[None]
+            out_refs[c][0:rows, b : b + 256] = piece.astype(bf16)
             gain = gain + jnp.sum(piece * units[c][:, b : b + 256], axis=0, keepdims=True)
         gains.append(gain)
     gain = jnp.concatenate(gains, axis=1)
@@ -407,7 +389,7 @@
     lanes = jnp.concatenate([sums[0], sums[1], bias, jnp.zeros((1, width - 2 * size - 128), f32)], axis=1)
     low = jnp.concatenate([gain, lanes, gm_ref[...], jnp.zeros((13, width), f32)], axis=0).astype(bf16)
     for c in range(chunks):
-        out_ref[c, rows : rows + 16, :] = low
+        out_refs[c][rows : rows + 16, :] = low
 
 
 def middle_kernel(x_ref, gain_ref, *refs):
@@ -439,21 +421,23 @@
     part_ref[...] = part
 
 
-def input_back_kernel(x_ref, dmid_ref, gain_ref, *refs):
-    rows = x_ref.shape[0]
-    out_ref = refs[-1]
-    d = refs[0][0, 0:rows, :].astype(f32)
-    for c in range(1, refs[0].shape[0]):
-        d = d + refs[0][c, 0:rows, :].astype(f32)
-    back, _ = norm_back(d, x_ref[...].astype(f32), gain_ref[...])
-    out_ref[...] = (back + dmid_ref[...]).astype(bf16)
-
-
-def finish_ffn_kernel(in_ref, gu_ref, down_ref):
-    units = down_ref.shape[1]
-    gu_ref[:, 0, :] = in_ref[:, :units].astype(f32)
-    gu_ref[:, 1, :] = in_ref[:, units : 2 * units].astype(f32)
-    down_ref[...] = in_ref[:, 2 * units :].astype(f32)
+def weight_send_kernel(flip_ref, d_ref, out_ref):
+    deep = out_ref.shape[2]
+    other = 1 - lax.axis_index("ctx")
+    for s in range(out_ref.shape[0]):
+        out_ref[s] = mm(flip_ref[pl.ds(2 * s + other, 1)][0], d_ref[:, :deep]).astype(bf16)
+
+
+def weight_keep_kernel(flip_ref, d_ref, got_ref, own_ref, *pair_refs):
+    deep = got_ref.shape[2]
+    me, half = lax.axis_index("shard"), lax.axis_index("ctx")
+    for k in range(got_ref.shape[0]):
+        total = mm(flip_ref[pl.ds(2 * (me ^ k) + half, 1)][0], d_ref[:, :deep])
+        total = total + got_ref[pl.ds(me ^ k, 1)][0].astype(f32)
+        if k == 0:
+            own_ref[...] = total
+        else:
+            pair_refs[k - 1][...] = total.astype(bf16)
 
 
 def finish_gates_kernel(in_ref, out_ref, gate_ref):
@@ -462,15 +446,27 @@
     gate_ref[...] = in_ref[:, cols:].astype(f32)
 
 
-def finish_qkv_kernel(own_ref, *refs):
-    qkv_ref, forget_ref = refs[-2:]
+def finish_kernel(terms, x_ref, dmid_ref, gain_ref, ffn_ref, own_ref, *refs):
+    dn_refs, refs = refs[:terms], refs[terms:]
+    arrived, refs = refs[:-5], refs[-5:]
+    in_ref, gu_ref, down_ref, qkv_ref, forget_ref = refs
+    rows = x_ref.shape[0]
+    d = dn_refs[0][0:rows, :].astype(f32)
+    for ref in dn_refs[1:]:
+        d = d + ref[0:rows, :].astype(f32)
+    back, _ = norm_back(d, x_ref[...].astype(f32), gain_ref[...])
+    in_ref[...] = (back + dmid_ref[...]).astype(bf16)
+    units = down_ref.shape[1]
+    gu_ref[:, 0, :] = ffn_ref[:, :units].astype(f32)
+    gu_ref[:, 1, :] = ffn_ref[:, units : 2 * units].astype(f32)
+    down_ref[...] = ffn_ref[:, 2 * units :].astype(f32)
     cols = qkv_ref.shape[2]
     total = own_ref[...]
-    for ref in refs[:-2]:
+    for ref in arrived:
         total = total + ref[...].astype(f32)
     for i in range(3):
-        qkv_ref[:, i, :] = total[:, i * cols : (i + 1) * cols]
-    forget_ref[...] = total[:, 3 * cols : 3 * cols + forget_ref.shape[1]]
+        qkv_ref[i] = total[:, i * cols : (i + 1) * cols]
+    forget_ref[...] = jnp.transpose(total[:, 3 * cols :])[: forget_ref.shape[0], :]
 
 
 def body(tokens, cotangent, lengths, w_qkv, w_forget, forget_bias, w_ogate, w_out, w_gu, w_down, gain_attn, gain_mlp,
@@ -500,7 +496,7 @@
     rank, rank_t = order[:, None], order[None, :]
 
     first = jnp.concatenate(
-        [w_out, w_qkv.reshape(slab, 3 * cols), w_forget, jnp.zeros((slab, 128 - heads), bf16), w_ogate], axis=1
+        [w_out, w_qkv[:, 0], w_qkv[:, 1], w_qkv[:, 2], w_forget, jnp.zeros((slab, 128 - heads), bf16), w_ogate], axis=1
     )
     first = lax.all_gather(first, both, axis=0, tiled=True)
     rest = jnp.concatenate([w_gu.reshape(slab, 2 * units), w_down], axis=1)
@@ -547,13 +543,13 @@
     )
     tile = min(512, units)
     steps = units // tile
-    d_hidden, cot = call(
+    d_hidden, cot, flip = call(
         functools.partial(hidden_back_kernel, n),
-        [sds((span, units), f32), sds((span, width), bf16)],
-        after(cot, nm_own), rest,
+        [sds((span, units), f32), sds((span, width), bf16), sds((width, span), bf16)],
+        after(cot, nm_own), normed, rest,
         grid=(steps,),
-        in_specs=[whole((n, rows, width)), pl.BlockSpec((width, tile), lambda j: (0, j + 2 * steps))],
-        out_specs=[pl.BlockSpec((span, tile), lambda j: (0, j)), whole((span, width))],
+        in_specs=[whole((n, rows, width)), whole((span, width)), pl.BlockSpec((width, tile), lambda j: (0, j + 2 * steps))],
+        out_specs=[pl.BlockSpec((span, tile), lambda j: (0, j)), whole((span, width)), whole((width, span))],
     )
     nm_parts = after(gather_rows(nm_own), d_hidden)
     nm, hidden, d_units, *p_parts = call(
@@ -572,8 +568,9 @@
         + [whole((rows, width))] * n,
         scratch=[pltpu.VMEM((width, 2 * units), bf16)],
     )
-    p_got = send_rows(p_parts)
-    part_ffn = jnp.concatenate([mm_tn(nm, d_units).astype(bf16), mm_tn(cot, hidden).astype(bf16)], axis=1)
+    part_down = mm_tn(cot, hidden).astype(bf16)
+    p_got = send_rows(p_parts, part_down)
+    part_ffn = jnp.concatenate([mm_tn(nm, d_units).astype(bf16), part_down], axis=1)
     grad_ffn = lax.psum_scatter(after(part_ffn, p_got[1]), both, scatter_dimension=0, tiled=True)
     d_middle, db_own, gain_m_part = call(
         middle_back_kernel,
@@ -604,32 +601,40 @@
     )
     part_gates = jnp.concatenate([mm_tn(d_branch, gated), mm_tn(normed, d_open)], axis=1).astype(bf16)
     back = lax.ppermute(back, "ctx", [(1, 0)])
-    mixed, dn = call(
+    mixed, *dn = call(
         functools.partial(project_back_kernel, heads, size, n),
-        [sds((span, wide), bf16), sds((n, rows + 16, width), bf16)],
+        [sds((span, wide), bf16)] + [sds((rows + 16, width), bf16)] * n,
         *x_parts, first, qk_wide, qraw, kraw, dq, dk, dv, back, d_open, d_cum, pre, rank, rank_t, gain_m_part,
     )
     down_sum = jnp.sum(after(down, mixed).astype(f32), axis=0)
     output = (valid * (middle + down_sum)).astype(bf16)
     deep = 3 * cols + 128
-    grad_gates = lax.psum_scatter(after(part_gates, mixed, grad_ffn), both, scatter_dimension=0, tiled=True)
-    state_qkv = scatter_weight(mm_tn(normed, mixed[:, :deep]).astype(bf16))
-    dn = scatter_all(after(dn, output, grad_ffn))
-    grad_gu, grad_down = call(
-        finish_ffn_kernel, [sds((slab, 2, units), f32), sds((slab, units), f32)], grad_ffn
-    )
-    dn_late, grad_gu, grad_down, _ = lax.optimization_barrier((dn, grad_gu, grad_down, state_qkv[1]))
-    (input_grad,) = call(
-        input_back_kernel, [sds((rows, width), bf16)], x_own, d_middle, gain_a, dn_late
-    )
-    grad_out, grad_ogate = call(finish_gates_kernel, [sds((slab, cols), f32)] * 2, grad_gates)
-    grad_qkv, grad_forget = call(
-        finish_qkv_kernel,
-        [sds((slab, 3, cols), f32), sds((slab, heads), f32)],
-        state_qkv[0], *state_qkv[1],
-    )
-
-    sums = jnp.sum(dn[:, rows:].astype(f32), axis=0)
+    grad_gates = lax.psum_scatter(after(part_gates, grad_ffn), both, scatter_dimension=0, tiled=True)
+    shards = lax.axis_size("shard")
+    flip = flip.reshape(2 * shards, slab, span)
+    (sent,) = call(weight_send_kernel, [sds((shards, slab, deep), bf16)], flip, mixed)
+    grad_own, *pairs = call(
+        weight_keep_kernel,
+        [sds((slab, deep), f32)] + [sds((slab, deep), bf16)] * (shards - 1),
+        flip, mixed, swap(sent, "ctx", 1),
+    )
+    state_qkv = grad_own, [swap(p, "shard", k + 1) for k, p in enumerate(pairs)]
+    dn = send_rows(after(dn, output))
+    grad_out, grad_ogate = call(finish_gates_kernel, [sds((slab, cols), f32)] * 2, grad_gates, weight=100)
+    input_grad, grad_gu, grad_down, grad_qkv, grad_forget = call(
+        functools.partial(finish_kernel, len(dn)),
+        [
+            sds((rows, width), bf16),
+            sds((slab, 2, units), f32),
+            sds((slab, units), f32),
+            sds((3, slab, cols), f32),
+            sds((heads, slab), f32),
+        ],
+        x_own, d_middle, gain_a, grad_ffn, state_qkv[0], *dn, *state_qkv[1],
+    )
+    grad_qkv, grad_forget = jnp.swapaxes(grad_qkv, 0, 1), jnp.swapaxes(grad_forget, 0, 1)
+
+    sums = sum(g[rows:].astype(f32) for g in dn)
     small = jnp.concatenate([sums[0], sums[1, : 2 * size + n * heads], sums[2]])
     small = sum_over(small, ("ctx", "shard"))
     edges = [0, width, width + 2 * size, width + 2 * size + n * heads]

time: 364 us -> 355 us (0.975)
  Pallas kernels: 89.3 us -> 96.2 us
  matrix products: 16.9 us -> 10 us
  local copies, waits for them, and re-layouts: 23.6 us -> 17 us
    all_to_all x2 -> x1, waiting for transfers between devices: 26.7 us -> 0.01 us  [scatter_all(): return lax.all_to_all(blocks, 'tp', 0, 0, tiled=True)]
    ppermute x23 -> x26, waiting for transfers between devices: 112 us -> 138 us  [swap(): return lax.ppermute(value, axis, [(j, j ^ bit) for j in range(n)])]
    ppermute x23 -> x26, starting transfers between devices: 31.2 us -> 38.4 us  [swap(): return lax.ppermute(value, axis, [(j, j ^ bit) for j in range(n)])]
    pallas_call x13, Pallas kernels: 89.3 us -> 96.2 us  [call(): pl.pallas_call(kernel, out_shape=outs, scratch_shapes=list(scratch), comp...]
    dot_general x5 -> x4, matrix products: 16.9 us -> 10 us  [mm_tn(): lax.dot_general(left, right, (((0,), (0,)), ((), ())), preferred_element_...]
    all_to_all x2 -> x1, starting transfers between devices: 9.59 us -> 4 us  [scatter_all(): return lax.all_to_all(blocks, 'tp', 0, 0, tiled=True)]
    unnamed x84 -> x90, local copies, waits for them, and re-layouts: 11 us -> 7.38 us
  transfers between devices with their start and end apart: 32 -> 34, of which waited for: 17 -> 20; matrix products, arithmetic and copies ran while one was open for 12% -> 7% of each run, Pallas kernels for 21% -> 23%
where the time goes in v4:
time: 355 us; the launch traced here: 349 us
  waiting for transfers between devices  148 us (42%)
  Pallas kernels  96.2 us (27%)
  starting transfers between devices  52.3 us (15%)
  local copies, waits for them, and re-layouts  17 us (5%)
  between operations  15.1 us (4%)
  other arithmetic  10.6 us (3%)
  matrix products  10 us (3%)
    ppermute x26, waiting for transfers between devices, swap(): return lax.ppermute(value, axis, [(j, j ^ bit) for j in range(n)])  138 us
    pallas_call x13, Pallas kernels, call(): pl.pallas_call(kernel, out_shape=outs, scratch_shapes=list(scratch), comp...  96.2 us
    ppermute x26, starting transfers between devices, swap(): return lax.ppermute(value, axis, [(j, j ^ bit) for j in range(n)])  38.4 us
    dot_general x4, matrix products, mm_tn(): lax.dot_general(left, right, (((0,), (0,)), ((), ())), preferred_element_...  10 us
    unnamed x90, local copies, waits for them, and re-layouts  7.38 us
  transfers between devices with their start and end apart: 34, of which 20 were waited for; matrix products, arithmetic and copies ran while one was open for 7% of the time, Pallas kernels for 23%

profile of v4, /device:TPU:0, one launch (start us, length us, event | category | flops | bytes accessed | tf_op | source)
XLA Modules:
  0.0 349.0 jit_solution(11441216907436145144)
XLA Ops:
  12.7 4.1 %collective-permute-start.1 = (bf16[128,1536]{1,0:T(8,128)(2,1)S(1)}, bf16[128,1536]{1,0:T(8,128)(2,1)S(1)}, u32[]{:S(2)}, u32[]{:S(2)}) collective-permute-start(bf16[128,1536]{1,0:T(8,128)(2,1)S(1)} %bitcast.36), channel_id=1, source_target_pairs={{0,2},{1,3},{2,0},{3,1},{4,6},{5,7},{6,4},{7,5},{8,10},{9,11},{10,... | collective-permute-start | bytes 1179656 | tf_op jit(solution)/shard_map/ppermute | solution.py:63
  19.0 15.4 %collective-permute-done.1.refs_2_ = bf16[128,1536]{1,0:T(8,128)(2,1)S(1)} collective-permute-done((bf16[128,1536]{1,0:T(8,128)(2,1)S(1)}, bf16[128,1536]{1,0:T(8,128)(2,1)S(1)}, u32[]{:S(2)}, u32[]{:S(2)}) %collective-permute-start.1) | collective-permute-done | bytes 393248 | tf_op jit(solution)/shard_map/ppermute | solution.py:63
  35.2 9.5 %collective-permute-done.2.refs_3_ = bf16[128,1536]{1,0:T(8,128)(2,1)S(1)} collective-permute-done((bf16[128,1536]{1,0:T(8,128)(2,1)S(1)}, bf16[128,1536]{1,0:T(8,128)(2,1)S(1)}, u32[]{:S(2)}, u32[]{:S(2)}) %collective-permute-start.2) | collective-permute-done | bytes 393248 | tf_op jit(solution)/shard_map/ppermute | solution.py:63
  46.0 5.5 %all-to-all-start = ((bf16[4,128,1536]{2,1,0:T(8,128)(2,1)}), bf16[4,128,1536]{2,1,0:T(8,128)(2,1)S(1)}, u32[]{:S(2)}, u32[]{:S(2)}) async-start(bf16[4,128,1536]{2,1,0:T(8,128)(2,1)} %broadcast_in_dim.38), calls=%async_computation | async-start | bytes 3145728 | tf_op jit(solution)/shard_map/all_to_all | solution.py:77
  54.3 5.4 %all-gather.3.cloned.1.call-done.refs_4_.wout_ref.refs_15_ = bf16[1536,2048]{1,0:T(8,128)(2,1)} async-done(((bf16[192,2048]{1,0:T(8,128)(2,1)}), bf16[1536,2048]{1,0:T(8,128)(2,1)}) %all-gather.3.cloned.1.call-update) | async-done | bytes 6291472 | tf_op jit(solution)/shard_map/all_gather | solution.py:501
  59.6 11.2 %shard_map.220 = (bf16[512,1536]{1,0:T(8,128)(2,1)}, bf16[512,768]{1,0:T(8,128)(2,1)}, bf16[512,768]{1,0:T(8,128)(2,1)}, bf16[512,768]{1,0:T(8,128)(2,1)}, bf16[...) custom-call(bf16[128,1536]{1,0:T(8,128)(2,1)} %bitcast.32, ...), custom_call_target="tpu_custom_call" | custom-call | flops 100000000 | bytes 100000 | tf_op jit(solution)/shard_map/pallas_call | solution.py:47
  76.2 9.3 %shard_map.221 = (bf16[512,384]{1,0:T(8,128)(2,1)}, f32[512,384]{1,0:T(8,128)}, f32[512,128]{1,0:T(8,128)}, bf16[512,768]{1,0:T(8,128)(2,1)}, bf16[512,768]{1,0:...) custom-call(bf16[512,768]{1,0:T(8,128)(2,1)} %get-tuple-element.96.q, ...), custom_call_target="tpu_custom_call" | custom-call | flops 100000000 | bytes 100000 | tf_op jit(solution)/shard_map/pallas_call | solution.py:47
  89.9 10.2 %collective-permute-done.5 = bf16[128,1536]{1,0:T(8,128)(2,1)S(1)} collective-permute-done((bf16[128,1536]{1,0:T(8,128)(2,1)}, bf16[128,1536]{1,0:T(8,128)(2,1)S(1)}, u32[]{:S(2)}, u32[]{:S(2)}) %collective-permute-start.5) | collective-permute-done | bytes 393248 | tf_op jit(solution)/shard_map/ppermute | solution.py:63
  102.0 10.6 %collective-permute-done.4.refs_1_ = bf16[128,1536]{1,0:T(8,128)(2,1)S(1)} collective-permute-done((bf16[128,1536]{1,0:T(8,128)(2,1)}, bf16[128,1536]{1,0:T(8,128)(2,1)S(1)}, u32[]{:S(2)}, u32[]{:S(2)}) %collective-permute-start.4) | collective-permute-done | bytes 393248 | tf_op jit(solution)/shard_map/ppermute | solution.py:63
  112.6 5.9 %collective-permute-done.6.refs_2_ = bf16[128,1536]{1,0:T(8,128)(2,1)S(1)} collective-permute-done((bf16[128,1536]{1,0:T(8,128)(2,1)S(1)}, bf16[128,1536]{1,0:T(8,128)(2,1)S(1)}, u32[]{:S(2)}, u32[]{:S(2)}) %collective-permute-start.6) | collective-permute-done | bytes 393248 | tf_op jit(solution)/shard_map/ppermute | solution.py:63
  121.8 3.5 collective-permute-start.7
  125.3 11.2 %collective-permute-done.8.refs_2_ = bf16[128,1536]{1,0:T(8,128)(2,1)S(1)} collective-permute-done((bf16[128,1536]{1,0:T(8,128)(2,1)}, bf16[128,1536]{1,0:T(8,128)(2,1)S(1)}, u32[]{:S(2)}, u32[]{:S(2)}) %collective-permute-start.8) | collective-permute-done | bytes 393248 | tf_op jit(solution)/shard_map/ppermute | solution.py:63
  137.2 6.4 %shard_map.223 = (f32[512,1024]{1,0:T(8,128)}, bf16[512,1536]{1,0:T(8,128)(2,1)}, bf16[1536,512]{1,0:T(8,128)(2,1)}) custom-call(bf16[4,128,1536]{2,1,0:T(8,128)(2,1)} %copy-done.1, bf16[512,1536]{1,0:T(8,128)(2,1)} %get-tuple-element.113.normed_ref, bf16[1536,3072]{1,0:T(8,128)(2,1)} %all-gather.5.cloned.1.call-done.wd_ref.refs_5_.refs_6_), custom_call_target="tpu_custom_call" | custom-call | flops 100000000 | bytes 100000 | tf_op jit(solution)/shard_map/pallas_call | solution.py:47
  146.0 14.1 %shard_map.224 = (bf16[512,1536]{1,0:T(8,128)(2,1)}, bf16[512,1024]{1,0:T(8,128)(2,1)}, bf16[512,2048]{1,0:T(8,128)(2,1)}, bf16[128,1536]{1,0:T(8,128)(2,1)}, bf...) custom-call(bf16[128,1536]{1,0:T(8,128)(2,1)} %get-tuple-element.115.refs_0_, ...), custom_call_target="tpu_custom_call" | custom-call | flops 100000000 | bytes 100000 | tf_op jit(solution)/shard_map/pallas_call | solution.py:47
  165.2 3.7 %convolution_convert_fusion = bf16[1536,2048]{1,0:T(8,128)(2,1)S(1)} fusion(bf16[512,1536]{1,0:T(8,128)(2,1)S(1)} %copy-done.34, bf16[512,2048]{1,0:T(8,128)(2,1)S(1)} %copy-done.32), kind=kOutput, calls=%fused_computation.1 | convolution fusion | flops 3224371200 | bytes 9961472 | tf_op jit(solution)/shard_map/dot_general | solution.py:27
  168.9 4.5 %pad_maximum_fusion = bf16[1536,3072]{1,0:T(8,128)(2,1)} fusion(bf16[1536,1024]{1,0:T(8,128)(2,1)S(1)} %convolution_convert_fusion.1, bf16[1536,2048]{1,0:T(8,128)(2,1)S(1)} %convolution_convert_fusion), kind=kLoop, calls=%fused_computation | loop fusion | flops 18874368 | bytes 18874368 | tf_op jit(solution)/shard_map/concatenate | solution.py:573
  174.9 8.3 %collective-permute-done.11 = bf16[128,1536]{1,0:T(8,128)(2,1)S(1)} collective-permute-done((bf16[128,1536]{1,0:T(8,128)(2,1)S(1)}, bf16[128,1536]{1,0:T(8,128)(2,1)S(1)}, u32[]{:S(2)}, u32[]{:S(2)}) %collective-permute-start.11) | collective-permute-done | bytes 393248 | tf_op jit(solution)/shard_map/ppermute | solution.py:63
  183.4 4.6 %collective-permute-start.12 = (bf16[128,1536]{1,0:T(8,128)(2,1)S(1)}, bf16[128,1536]{1,0:T(8,128)(2,1)S(1)}, u32[]{:S(2)}, u32[]{:S(2)}) collective-permute-start(bf16[128,1536]{1,0:T(8,128)(2,1)S(1)} %add_convert_fusion.1), channel_id=1, source_target_pairs={{0,2},{1,3},{2,0},{3,1},{4,6},{5,7},{6,4},{7,5},{8,10},{9,11},{10,... | collective-permute-start | bytes 1179656 | tf_op jit(solution)/shard_map/ppermute | solution.py:63
  188.0 13.2 %collective-permute-done.12.refs_2_ = bf16[128,1536]{1,0:T(8,128)(2,1)S(1)} collective-permute-done((bf16[128,1536]{1,0:T(8,128)(2,1)S(1)}, bf16[128,1536]{1,0:T(8,128)(2,1)S(1)}, u32[]{:S(2)}, u32[]{:S(2)}) %collective-permute-start.12) | collective-permute-done | bytes 393248 | tf_op jit(solution)/shard_map/ppermute | solution.py:63
  208.8 15.4 %collective-permute-done.14.refs_2_ = bf16[128,1536]{1,0:T(8,128)(2,1)S(1)} collective-permute-done((bf16[128,1536]{1,0:T(8,128)(2,1)}, bf16[128,1536]{1,0:T(8,128)(2,1)S(1)}, u32[]{:S(2)}, u32[]{:S(2)}) %collective-permute-start.14) | collective-permute-done | bytes 393248 | tf_op jit(solution)/shard_map/ppermute | solution.py:63
  224.2 5.5 %shard_map.226 = bf16[4,128,1536]{2,1,0:T(8,128)(2,1)} custom-call(bf16[512,1024]{1,0:T(8,128)(2,1)} %get-tuple-element.132.hid_ref, bf16[1536,3072]{1,0:T(8,128)(2,1)} %all-gather.5.cloned.1.call-done.wd_ref.refs_5_.refs_6_), custom_call_target="tpu_custom_call" | custom-call | flops 100000000 | bytes 100000 | tf_op jit(solution)/shard_map/pallas_call | solution.py:47
  233.7 4.0 %all-to-all-start.1 = ((bf16[4,128,1536]{2,1,0:T(8,128)(2,1)}), bf16[4,128,1536]{2,1,0:T(8,128)(2,1)S(1)}, u32[]{:S(2)}, u32[]{:S(2)}) async-start(bf16[4,128,1536]{2,1,0:T(8,128)(2,1)} %shard_map.226), calls=%async_computation.1 | async-start | bytes 3145728 | tf_op jit(solution)/shard_map/all_to_all | solution.py:81
  238.2 15.8 %shard_map.227 = (bf16[512,1536]{1,0:T(8,128)(2,1)}, f32[512,384]{1,0:T(8,128)}, f32[512,384]{1,0:T(8,128)}, f32[512,384]{1,0:T(8,128)}, bf16[512,896]{1,0:T(8,1...) custom-call(bf16[128,1536]{1,0:T(8,128)(2,1)} %get-tuple-element.136.refs_0_, bf16[128,1536]{1,0:T(8,128)(2,1)} %copy-done.39, ...), custom_call_target="tpu_custom_call" | custom-call | flops 99999997952 | bytes 100000000 | tf_op jit(solution)/shard_map/pallas_call | solution.py:47
  260.3 11.9 %shard_map.228 = (bf16[512,1664]{1,0:T(8,128)(2,1)}, bf16[144,1536]{1,0:T(8,128)(2,1)}, bf16[144,1536]{1,0:T(8,128)(2,1)}, bf16[144,1536]{1,0:T(8,128)(2,1)}, bf16[144,1536]{1,0:T(8,128)(2,1)}) custom-call(bf16[128,1536]{1,0:T(8,128)(2,1)} %bitcast.34, bf16[128,1536]{1,0:T(8,128)(2,1)} %copy-done.5, bf16[128,1536]{1,0:T(8,128)(2,1)} %copy-done.4, ...), custom_call_target="tpu_custom_call" | custom-call | flops 100000000 | bytes 100000 | tf_op jit(solution)/shard_map/pallas_call | solution.py:47
  272.2 4.6 %shard_map.229 = bf16[4,192,1280]{2,1,0:T(8,128)(2,1)} custom-call(bf16[8,192,512]{2,1,0:T(8,128)(2,1)} %bitcast.38, bf16[512,1664]{1,0:T(8,128)(2,1)} %get-tuple-element.153.d_ref), custom_call_target="tpu_custom_call" | custom-call | flops 100000000 | bytes 100000 | tf_op jit(solution)/shard_map/pallas_call | solution.py:47
  282.1 10.7 %collective-permute-done.19 = bf16[144,1536]{1,0:T(8,128)(2,1)S(1)} collective-permute-done((bf16[144,1536]{1,0:T(8,128)(2,1)S(1)}, bf16[144,1536]{1,0:T(8,128)(2,1)S(1)}, u32[]{:S(2)}, u32[]{:S(2)}) %collective-permute-start.19) | collective-permute-done | bytes 442400 | tf_op jit(solution)/shard_map/ppermute | solution.py:63
  296.2 4.5 %shard_map.230 = (f32[192,1280]{1,0:T(8,128)}, bf16[192,1280]{1,0:T(8,128)(2,1)}, bf16[192,1280]{1,0:T(8,128)(2,1)}, bf16[192,1280]{1,0:T(8,128)(2,1)}) custom-call(bf16[8,192,512]{2,1,0:T(8,128)(2,1)} %bitcast.39, bf16[512,1664]{1,0:T(8,128)(2,1)} %get-tuple-element.153.d_ref, bf16[4,192,1280]{2,1,0:T(8,128)(2,1)} %collective-permute-done.17.got_ref), custom_call_target="tpu_custom_call" | custom-call | flops 100000000 | bytes 100000 | tf_op jit(solution)/shard_map/pallas_call | solution.py:47
  304.8 5.3 %collective-permute-done.18.refs_1_ = bf16[144,1536]{1,0:T(8,128)(2,1)S(1)} collective-permute-done((bf16[144,1536]{1,0:T(8,128)(2,1)S(1)}, bf16[144,1536]{1,0:T(8,128)(2,1)S(1)}, u32[]{:S(2)}, u32[]{:S(2)}) %collective-permute-start.18) | collective-permute-done | bytes 442400 | tf_op jit(solution)/shard_map/ppermute | solution.py:63
  310.1 6.2 %collective-permute-done.20.refs_2_ = bf16[144,1536]{1,0:T(8,128)(2,1)S(1)} collective-permute-done((bf16[144,1536]{1,0:T(8,128)(2,1)S(1)}, bf16[144,1536]{1,0:T(8,128)(2,1)S(1)}, u32[]{:S(2)}, u32[]{:S(2)}) %collective-permute-start.20) | collective-permute-done | bytes 442400 | tf_op jit(solution)/shard_map/ppermute | solution.py:63
  318.4 3.4 collective-permute-start.27
  321.8 6.7 %collective-permute-done.27 = f32[3224]{0:T(1024)S(1)} collective-permute-done((f32[3224]{0:T(1024)S(1)}, f32[3224]{0:T(1024)S(1)}, u32[]{:S(2)}, u32[]{:S(2)}) %collective-permute-start.27) | collective-permute-done | bytes 12928 | tf_op jit(solution)/shard_map/ppermute | solution.py:63
  335.2 5.3 %shard_map.231 = (bf16[128,1536]{1,0:T(8,128)(2,1)}, f32[192,2,1024]{2,1,0:T(2,128)}, f32[192,1024]{1,0:T(8,128)}, f32[3,192,384]{2,1,0:T(8,128)}, f32[6,192]{1,0:T(8,128)}) custom-call(bf16[128,1536]{1,0:T(8,128)(2,1)} %bitcast.35, f32[128,1536]{1,0:T(8,128)} %get-tuple-element.155.dmid_ref, f32[1,1536]{1,0:T(1,128)} %broadcast_in_dim.34.refs_5_.gain_ref, ...), custom_call_target="tpu_custom_call" | custom-call | flops 100000000 | bytes 100000 | tf_op jit(solution)/shard_map/pallas_call | solution.py:47
  (181 shorter events, 78.1 us)
Async XLA Ops:
  7.2 52.4 %all-gather.3.cloned.1.call-start = ((), (), s32[]{:S(2)}) async-start(), calls=%async_computation.4 | async-start | bytes 7077888 | tf_op jit(solution)/shard_map/all_gather | solution.py:501
  11.2 125.9 %all-gather.5.cloned.1.call-start = ((), (), s32[]{:S(2)}) async-start(), calls=%async_computation.5 | async-start | bytes 10616832 | tf_op jit(solution)/shard_map/all_gather | solution.py:503
  12.7 21.7 %collective-permute-start.1 = (bf16[128,1536]{1,0:T(8,128)(2,1)S(1)}, bf16[128,1536]{1,0:T(8,128)(2,1)S(1)}, u32[]{:S(2)}, u32[]{:S(2)}) collective-permute-start(bf16[128,1536]{1,0:T(8,128)(2,1)S(1)} %bitcast.36), channel_id=1, source_target_pairs={{0,2},{1,3},{2,0},{3,1},{4,6},{5,7},{6,4},{7,5},{8,10},{9,11},{10,... | collective-permute-start | bytes 1179656 | tf_op jit(solution)/shard_map/ppermute | solution.py:63
  16.8 18.4 %collective-permute-start = (bf16[128,1536]{1,0:T(8,128)(2,1)S(1)}, bf16[128,1536]{1,0:T(8,128)(2,1)S(1)}, u32[]{:S(2)}, u32[]{:S(2)}) collective-permute-start(bf16[128,1536]{1,0:T(8,128)(2,1)S(1)} %bitcast.37), channel_id=1, source_target_pairs={{0,1},{1,0},{2,3},{3,2},{4,5},{5,4},{6,7},{7,6},{8,9},{9,8},{10,11... | collective-permute-start | bytes 1179656 | tf_op jit(solution)/shard_map/ppermute | solution.py:63
  34.4 10.2 %collective-permute-start.2 = (bf16[128,1536]{1,0:T(8,128)(2,1)S(1)}, bf16[128,1536]{1,0:T(8,128)(2,1)S(1)}, u32[]{:S(2)}, u32[]{:S(2)}) collective-permute-start(bf16[128,1536]{1,0:T(8,128)(2,1)S(1)} %collective-permute-done.1.refs_2_), channel_id=1, source_target_pairs={{0,1},{1,0},{2,3},{3,2},{4,5},{5,4},{6,7},{7,6},{8,9},{9,8},{10,11... | collective-permute-start | bytes 1179656 | tf_op jit(solution)/shard_map/ppermute | solution.py:63
  46.0 41.9 %all-to-all-start = ((bf16[4,128,1536]{2,1,0:T(8,128)(2,1)}), bf16[4,128,1536]{2,1,0:T(8,128)(2,1)S(1)}, u32[]{:S(2)}, u32[]{:S(2)}) async-start(bf16[4,128,1536]{2,1,0:T(8,128)(2,1)} %broadcast_in_dim.38), calls=%async_computation | async-start | bytes 3145728 | tf_op jit(solution)/shard_map/all_to_all | solution.py:77
  51.5 208.8 %reduce-scatter.3.cloned.1.call-start = ((), (), s32[]{:S(2)}) async-start(), calls=%async_computation.6 | async-start | bytes 10616832 | tf_op jit(solution)/shard_map/reduce_scatter | solution.py:574
  70.8 4.5 %collective-permute-start.3 = (bf16[512,896]{1,0:T(8,128)(2,1)}, bf16[512,896]{1,0:T(8,128)(2,1)S(1)}, u32[]{:S(2)}, u32[]{:S(2)}) collective-permute-start(bf16[512,896]{1,0:T(8,128)(2,1)} %get-tuple-element.99), channel_id=1, source_target_pairs={{0,4},{1,5},{2,6},{3,7},{8,12},{9,13},{10,14},{11,15},{16,20},{17,... | collective-permute-start | bytes 2752520 | tf_op jit(solution)/shard_map/ppermute | solution.py:530
  87.9 12.3 %collective-permute-start.5 = (bf16[128,1536]{1,0:T(8,128)(2,1)}, bf16[128,1536]{1,0:T(8,128)(2,1)S(1)}, u32[]{:S(2)}, u32[]{:S(2)}) collective-permute-start(bf16[128,1536]{1,0:T(8,128)(2,1)} %get-tuple-element.109), channel_id=1, source_target_pairs={{0,1},{1,0},{2,3},{3,2},{4,5},{5,4},{6,7},{7,6},{8,9},{9,8},{10,11... | collective-permute-start | bytes 1179656 | tf_op jit(solution)/shard_map/ppermute | solution.py:63
  87.9 24.7 %collective-permute-start.4 = (bf16[128,1536]{1,0:T(8,128)(2,1)}, bf16[128,1536]{1,0:T(8,128)(2,1)S(1)}, u32[]{:S(2)}, u32[]{:S(2)}) collective-permute-start(bf16[128,1536]{1,0:T(8,128)(2,1)} %get-tuple-element.107), channel_id=1, source_target_pairs={{0,1},{1,0},{2,3},{3,2},{4,5},{5,4},{6,7},{7,6},{8,9},{9,8},{10,11... | collective-permute-start | bytes 1179656 | tf_op jit(solution)/shard_map/ppermute | solution.py:63
  101.3 17.2 %collective-permute-start.6 = (bf16[128,1536]{1,0:T(8,128)(2,1)S(1)}, bf16[128,1536]{1,0:T(8,128)(2,1)S(1)}, u32[]{:S(2)}, u32[]{:S(2)}) collective-permute-start(bf16[128,1536]{1,0:T(8,128)(2,1)S(1)} %add_convert_fusion.2), channel_id=1, source_target_pairs={{0,2},{1,3},{2,0},{3,1},{4,6},{5,7},{6,4},{7,5},{8,10},{9,11},{10,... | collective-permute-start | bytes 1179656 | tf_op jit(solution)/shard_map/ppermute | solution.py:63
  121.8 14.6 %collective-permute-start.8 = (bf16[128,1536]{1,0:T(8,128)(2,1)}, bf16[128,1536]{1,0:T(8,128)(2,1)S(1)}, u32[]{:S(2)}, u32[]{:S(2)}) collective-permute-start(bf16[128,1536]{1,0:T(8,128)(2,1)} %get-tuple-element.115.refs_0_), channel_id=1, source_target_pairs={{0,2},{1,3},{2,0},{3,1},{4,6},{5,7},{6,4},{7,5},{8,10},{9,11},{10,... | collective-permute-start | bytes 1179656 | tf_op jit(solution)/shard_map/ppermute | solution.py:63
  121.8 21.8 %collective-permute-start.7 = (bf16[128,1536]{1,0:T(8,128)(2,1)}, bf16[128,1536]{1,0:T(8,128)(2,1)S(1)}, u32[]{:S(2)}, u32[]{:S(2)}) collective-permute-start(bf16[128,1536]{1,0:T(8,128)(2,1)} %get-tuple-element.115.refs_0_), channel_id=1, source_target_pairs={{0,1},{1,0},{2,3},{3,2},{4,5},{5,4},{6,7},{7,6},{8,9},{9,8},{10,11... | collective-permute-start | bytes 1179656 | tf_op jit(solution)/shard_map/ppermute | solution.py:63
  136.4 8.9 %collective-permute-start.9 = (bf16[128,1536]{1,0:T(8,128)(2,1)S(1)}, bf16[128,1536]{1,0:T(8,128)(2,1)S(1)}, u32[]{:S(2)}, u32[]{:S(2)}) collective-permute-start(bf16[128,1536]{1,0:T(8,128)(2,1)S(1)} %collective-permute-done.8.refs_2_), channel_id=1, source_target_pairs={{0,1},{1,0},{2,3},{3,2},{4,5},{5,4},{6,7},{7,6},{8,9},{9,8},{10,11... | collective-permute-start | bytes 1179656 | tf_op jit(solution)/shard_map/ppermute | solution.py:63
  163.4 10.1 %collective-permute-start.10 = (bf16[128,1536]{1,0:T(8,128)(2,1)S(1)}, bf16[128,1536]{1,0:T(8,128)(2,1)S(1)}, u32[]{:S(2)}, u32[]{:S(2)}) collective-permute-start(bf16[128,1536]{1,0:T(8,128)(2,1)S(1)} %copy-done.41), channel_id=1, source_target_pairs={{0,1},{1,0},{2,3},{3,2},{4,5},{5,4},{6,7},{7,6},{8,9},{9,8},{10,11... | collective-permute-start | bytes 1179656 | tf_op jit(solution)/shard_map/ppermute | solution.py:63
  174.6 8.7 %collective-permute-start.11 = (bf16[128,1536]{1,0:T(8,128)(2,1)S(1)}, bf16[128,1536]{1,0:T(8,128)(2,1)S(1)}, u32[]{:S(2)}, u32[]{:S(2)}) collective-permute-start(bf16[128,1536]{1,0:T(8,128)(2,1)S(1)} %copy-done.40), channel_id=1, source_target_pairs={{0,1},{1,0},{2,3},{3,2},{4,5},{5,4},{6,7},{7,6},{8,9},{9,8},{10,11... | collective-permute-start | bytes 1179656 | tf_op jit(solution)/shard_map/ppermute | solution.py:63
  183.4 17.9 %collective-permute-start.12 = (bf16[128,1536]{1,0:T(8,128)(2,1)S(1)}, bf16[128,1536]{1,0:T(8,128)(2,1)S(1)}, u32[]{:S(2)}, u32[]{:S(2)}) collective-permute-start(bf16[128,1536]{1,0:T(8,128)(2,1)S(1)} %add_convert_fusion.1), channel_id=1, source_target_pairs={{0,2},{1,3},{2,0},{3,1},{4,6},{5,7},{6,4},{7,5},{8,10},{9,11},{10,... | collective-permute-start | bytes 1179656 | tf_op jit(solution)/shard_map/ppermute | solution.py:63
  205.2 19.0 %collective-permute-start.14 = (bf16[128,1536]{1,0:T(8,128)(2,1)}, bf16[128,1536]{1,0:T(8,128)(2,1)S(1)}, u32[]{:S(2)}, u32[]{:S(2)}) collective-permute-start(bf16[128,1536]{1,0:T(8,128)(2,1)} %get-tuple-element.136.refs_0_), channel_id=1, source_target_pairs={{0,2},{1,3},{2,0},{3,1},{4,6},{5,7},{6,4},{7,5},{8,10},{9,11},{10,... | collective-permute-start | bytes 1179656 | tf_op jit(solution)/shard_map/ppermute | solution.py:63
  205.4 24.2 %collective-permute-start.13 = (bf16[128,1536]{1,0:T(8,128)(2,1)}, bf16[128,1536]{1,0:T(8,128)(2,1)S(1)}, u32[]{:S(2)}, u32[]{:S(2)}) collective-permute-start(bf16[128,1536]{1,0:T(8,128)(2,1)} %get-tuple-element.136.refs_0_), channel_id=1, source_target_pairs={{0,1},{1,0},{2,3},{3,2},{4,5},{5,4},{6,7},{7,6},{8,9},{9,8},{10,11... | collective-permute-start | bytes 1179656 | tf_op jit(solution)/shard_map/ppermute | solution.py:63
  224.2 9.5 %collective-permute-start.15 = (bf16[128,1536]{1,0:T(8,128)(2,1)S(1)}, bf16[128,1536]{1,0:T(8,128)(2,1)}, u32[]{:S(2)}, u32[]{:S(2)}) collective-permute-start(bf16[128,1536]{1,0:T(8,128)(2,1)S(1)} %collective-permute-done.14.refs_2_), channel_id=1, source_target_pairs={{0,1},{1,0},{2,3},{3,2},{4,5},{5,4},{6,7},{7,6},{8,9},{9,8},{10,11... | collective-permute-start | bytes 1179656 | tf_op jit(solution)/shard_map/ppermute | solution.py:63
  233.7 45.2 %all-to-all-start.1 = ((bf16[4,128,1536]{2,1,0:T(8,128)(2,1)}), bf16[4,128,1536]{2,1,0:T(8,128)(2,1)S(1)}, u32[]{:S(2)}, u32[]{:S(2)}) async-start(bf16[4,128,1536]{2,1,0:T(8,128)(2,1)} %shard_map.226), calls=%async_computation.1 | async-start | bytes 3145728 | tf_op jit(solution)/shard_map/all_to_all | solution.py:81
  237.7 102.8 %reduce-scatter.5.cloned.1.call-start = ((), (), s32[]{:S(2)}) async-start(), calls=%async_computation.7 | async-start | bytes 2654208 | tf_op jit(solution)/shard_map/reduce_scatter | solution.py:612
  254.0 6.3 %collective-permute-start.16 = (bf16[512,896]{1,0:T(8,128)(2,1)}, bf16[512,896]{1,0:T(8,128)(2,1)}, u32[]{:S(2)}, u32[]{:S(2)}) collective-permute-start(bf16[512,896]{1,0:T(8,128)(2,1)} %get-tuple-element.148), channel_id=1, source_target_pairs={{4,0},{5,1},{6,2},{7,3},{12,8},{13,9},{14,10},{15,11},{20,16},{21,... | collective-permute-start | bytes 2752520 | tf_op jit(solution)/shard_map/ppermute | solution.py:603
  276.8 19.4 %collective-permute-start.17 = (bf16[4,192,1280]{2,1,0:T(8,128)(2,1)}, bf16[4,192,1280]{2,1,0:T(8,128)(2,1)}, u32[]{:S(2)}, u32[]{:S(2)}) collective-permute-start(bf16[4,192,1280]{2,1,0:T(8,128)(2,1)} %shard_map.229), channel_id=1, source_target_pairs={{0,4},{4,0},{1,5},{5,1},{2,6},{6,2},{3,7},{7,3},{8,12},{12,8},{9,1... | collective-permute-start | bytes 5898248 | tf_op jit(solution)/shard_map/ppermute | solution.py:63
  280.0 12.8 %collective-permute-start.19 = (bf16[144,1536]{1,0:T(8,128)(2,1)S(1)}, bf16[144,1536]{1,0:T(8,128)(2,1)S(1)}, u32[]{:S(2)}, u32[]{:S(2)}) collective-permute-start(bf16[144,1536]{1,0:T(8,128)(2,1)S(1)} %copy-done.36), channel_id=1, source_target_pairs={{0,1},{1,0},{2,3},{3,2},{4,5},{5,4},{6,7},{7,6},{8,9},{9,8},{10,11... | collective-permute-start | bytes 1327112 | tf_op jit(solution)/shard_map/ppermute | solution.py:63
  282.1 28.0 %collective-permute-start.18 = (bf16[144,1536]{1,0:T(8,128)(2,1)S(1)}, bf16[144,1536]{1,0:T(8,128)(2,1)S(1)}, u32[]{:S(2)}, u32[]{:S(2)}) collective-permute-start(bf16[144,1536]{1,0:T(8,128)(2,1)S(1)} %copy-done.35), channel_id=1, source_target_pairs={{0,1},{1,0},{2,3},{3,2},{4,5},{5,4},{6,7},{7,6},{8,9},{9,8},{10,11... | collective-permute-start | bytes 1327112 | tf_op jit(solution)/shard_map/ppermute | solution.py:63
  292.9 23.3 %collective-permute-start.20 = (bf16[144,1536]{1,0:T(8,128)(2,1)S(1)}, bf16[144,1536]{1,0:T(8,128)(2,1)S(1)}, u32[]{:S(2)}, u32[]{:S(2)}) collective-permute-start(bf16[144,1536]{1,0:T(8,128)(2,1)S(1)} %add_convert_fusion), channel_id=1, source_target_pairs={{0,2},{1,3},{2,0},{3,1},{4,6},{5,7},{6,4},{7,5},{8,10},{9,11},{10,... | collective-permute-start | bytes 1327112 | tf_op jit(solution)/shard_map/ppermute | solution.py:63
  300.7 33.3 %collective-permute-start.21 = (bf16[192,1280]{1,0:T(8,128)(2,1)}, bf16[192,1280]{1,0:T(8,128)(2,1)S(1)}, u32[]{:S(2)}, u32[]{:S(2)}) collective-permute-start(bf16[192,1280]{1,0:T(8,128)(2,1)} %get-tuple-element.167), channel_id=1, source_target_pairs={{0,8},{8,0},{16,24},{24,16},{1,9},{9,1},{17,25},{25,17},{2,10},{10... | collective-permute-start | bytes 1474568 | tf_op jit(solution)/shard_map/ppermute | solution.py:63
  302.1 31.9 %collective-permute-start.22 = (bf16[192,1280]{1,0:T(8,128)(2,1)}, bf16[192,1280]{1,0:T(8,128)(2,1)S(1)}, u32[]{:S(2)}, u32[]{:S(2)}) collective-permute-start(bf16[192,1280]{1,0:T(8,128)(2,1)} %get-tuple-element.168), channel_id=1, source_target_pairs={{0,16},{8,24},{16,0},{24,8},{1,17},{9,25},{17,1},{25,9},{2,18},{10... | collective-permute-start | bytes 1474568 | tf_op jit(solution)/shard_map/ppermute | solution.py:63
  304.8 29.3 %collective-permute-start.23 = (bf16[192,1280]{1,0:T(8,128)(2,1)}, bf16[192,1280]{1,0:T(8,128)(2,1)S(1)}, u32[]{:S(2)}, u32[]{:S(2)}) collective-permute-start(bf16[192,1280]{1,0:T(8,128)(2,1)} %get-tuple-element.169), channel_id=1, source_target_pairs={{0,24},{8,16},{16,8},{24,0},{1,25},{9,17},{17,9},{25,1},{2,26},{10... | collective-permute-start | bytes 1474568 | tf_op jit(solution)/shard_map/ppermute | solution.py:63
  318.4 10.1 %collective-permute-start.27 = (f32[3224]{0:T(1024)S(1)}, f32[3224]{0:T(1024)S(1)}, u32[]{:S(2)}, u32[]{:S(2)}) collective-permute-start(f32[3224]{0:T(1024)S(1)} %add.94), channel_id=1, source_target_pairs={{0,24},{8,16},{16,8},{24,0},{1,25},{9,17},{17,9},{25,1},{2,26},{10... | collective-permute-start | bytes 38696 | tf_op jit(solution)/shard_map/ppermute | solution.py:63
  321.8 7.2 %collective-permute-start.26 = (f32[3224]{0:T(1024)S(1)}, f32[3224]{0:T(1024)S(1)}, u32[]{:S(2)}, u32[]{:S(2)}) collective-permute-start(f32[3224]{0:T(1024)S(1)} %add.94), channel_id=1, source_target_pairs={{0,16},{8,24},{16,0},{24,8},{1,17},{9,25},{17,1},{25,9},{2,18},{10... | collective-permute-start | bytes 38696 | tf_op jit(solution)/shard_map/ppermute | solution.py:63
  (46 other events, 354.7 us)
Sparse Core Ops, SparseCore 0:
  11.4 48.2 all-gather.2
  61.5 58.8 all-gather.4
  173.6 76.5 reduce-scatter.2
  260.4 49.3 reduce-scatter.4

commit v5 on v4

--- a/solution.py
+++ b/solution.py
@@ -135,18 +135,20 @@
     return total[:, :heads] + total[:, heads : 2 * heads] + total[:, 2 * heads : 3 * heads]
 
 
-def project_kernel(heads, size, chunks, *refs):
-    x_refs, refs = refs[:chunks], refs[chunks:]
-    w_ref, gain_ref, qk_ref, bias_ref, rank_ref, rank_t_ref = refs[:6]
-    (normed_ref, qa_ref, ka_ref, va_ref, send_ref, qraw_ref, kraw_ref, open_ref, pre_ref, cum_ref) = refs[6:]
-    rows = x_refs[0].shape[0]
-    span = rows * chunks
+def norm_kernel(gain_ref, *refs):
+    normed_ref = refs[-1]
+    rows = refs[0].shape[0]
+    for c, x_ref in enumerate(refs[:-1]):
+        x = x_ref[...].astype(f32)
+        r = lax.rsqrt(jnp.mean(x * x, axis=1, keepdims=True) + epsilon)
+        normed_ref[c * rows : (c + 1) * rows, :] = (x * r * gain_ref[...]).astype(bf16)
+
+
+def project_kernel(heads, size, *refs):
+    normed_ref, w_ref, qk_ref, bias_ref, rank_ref, rank_t_ref = refs[:6]
+    (qa_ref, ka_ref, va_ref, send_ref, qraw_ref, kraw_ref, open_ref, pre_ref, cum_ref) = refs[6:]
+    span = normed_ref.shape[0]
     cols = heads * size
-    gain = gain_ref[...]
-    for c in range(chunks):
-        x = x_refs[c][...].astype(f32)
-        r = lax.rsqrt(jnp.mean(x * x, axis=1, keepdims=True) + epsilon)
-        normed_ref[c * rows : (c + 1) * rows, :] = (x * r * gain).astype(bf16)
     normed = normed_ref[...]
     pre = mm(normed, w_ref[:, 4 * cols : 4 * cols + 128]) + bias_ref[...]
     pre_ref[...] = pre
@@ -339,15 +341,14 @@
     back_ref[:, 2 * cols :] = spread(sent, rows)
 
 
-def project_back_kernel(heads, size, chunks, *refs):
-    x_refs, refs = refs[:chunks], refs[chunks:]
-    (w_ref, qk_ref, qraw_ref, kraw_ref, dq_ref, dk_ref, dv_ref, back_ref, dopen_ref, dcum_ref, pre_ref, rank_ref,
-     rank_t_ref, gm_ref) = refs[:14]
-    mixed_ref, out_refs = refs[14], refs[15:]
+def project_back_kernel(heads, size, *refs):
+    (normed_ref, gain_ref, w_ref, qk_ref, qraw_ref, kraw_ref, dq_ref, dk_ref, dv_ref, back_ref, dopen_ref, dcum_ref, pre_ref, rank_ref,
+     rank_t_ref, gm_ref) = refs[:16]
+    mixed_ref, out_refs = refs[16], refs[17:]
     cols = heads * size
-    width = x_refs[0].shape[1]
-    rows = x_refs[0].shape[0]
-    span = rows * chunks
+    span, width = normed_ref.shape
+    chunks = len(out_refs)
+    rows = span // chunks
     sums = []
     for which, raw_ref in ((0, qraw_ref), (1, kraw_ref)):
         d = dq_ref[...] if which == 0 else dk_ref[...] + back_ref[:, :cols].astype(f32)
@@ -371,20 +372,14 @@
     bias = jnp.sum(df, axis=0, keepdims=True)
     mixed_ref[:, 3 * cols : 3 * cols + 128] = df.astype(bf16)
     me = lax.axis_index("tp")
-    units = []
-    for c in range(chunks):
-        x = x_refs[c][...].astype(f32)
-        units.append(x * lax.rsqrt(jnp.mean(x * x, axis=1, keepdims=True) + epsilon))
     gains = []
     for b in range(0, width, 256):
         dn = mm_nt(mixed_ref[...], w_ref[b : b + 256, cols:])
-        gain = jnp.zeros((1, 256), f32)
         for c in range(chunks):
-            piece = dn[c * rows : (c + 1) * rows, :]
-            out_refs[c][0:rows, b : b + 256] = piece.astype(bf16)
-            gain = gain + jnp.sum(piece * units[c][:, b : b + 256], axis=0, keepdims=True)
+            out_refs[c][0:rows, b : b + 256] = dn[c * rows : (c + 1) * rows, :].astype(bf16)
+        gain = jnp.sum(dn * normed_ref[:, b : b + 256].astype(f32), axis=0, keepdims=True)
         gains.append(gain)
-    gain = jnp.concatenate(gains, axis=1)
+    gain = jnp.concatenate(gains, axis=1) / gain_ref[...]
     bias = pltpu.roll(bias, me * heads, 1)
     lanes = jnp.concatenate([sums[0], sums[1], bias, jnp.zeros((1, width - 2 * size - 128), f32)], axis=1)
     low = jnp.concatenate([gain, lanes, gm_ref[...], jnp.zeros((13, width), f32)], axis=0).astype(bf16)
@@ -511,10 +506,10 @@
     gain_a, gain_m = gain_attn[None, :], gain_mlp[None, :]
     qk_wide = jnp.tile(qk_gain, (1, heads))
 
-    normed, qa, ka, va, sent, qraw, kraw, opener, pre, cum = call(
-        functools.partial(project_kernel, heads, size, n),
+    (normed,) = call(norm_kernel, [sds((span, width), bf16)], gain_a, *x_parts)
+    qa, ka, va, sent, qraw, kraw, opener, pre, cum = call(
+        functools.partial(project_kernel, heads, size),
         [
-            sds((span, width), bf16),
             sds((span, heads * 128), bf16),
             sds((span, heads * 128), bf16),
             sds((span, heads * 128), bf16),
@@ -525,7 +520,7 @@
             sds((span, 128), f32),
             sds((span, 128), f32),
         ],
-        *x_parts, first, gain_a, qk_wide, bias, rank, rank_t,
+        normed, first, qk_wide, bias, rank, rank_t,
     )
     left = lax.ppermute(sent, "ctx", [(0, 1)])
     gated, attended, lse, kl, vl, *branch = call(
@@ -602,9 +597,9 @@
     part_gates = jnp.concatenate([mm_tn(d_branch, gated), mm_tn(normed, d_open)], axis=1).astype(bf16)
     back = lax.ppermute(back, "ctx", [(1, 0)])
     mixed, *dn = call(
-        functools.partial(project_back_kernel, heads, size, n),
+        functools.partial(project_back_kernel, heads, size),
         [sds((span, wide), bf16)] + [sds((rows + 16, width), bf16)] * n,
-        *x_parts, first, qk_wide, qraw, kraw, dq, dk, dv, back, d_open, d_cum, pre, rank, rank_t, gain_m_part,
+        normed, gain_a, first, qk_wide, qraw, kraw, dq, dk, dv, back, d_open, d_cum, pre, rank, rank_t, gain_m_part,
     )
     down_sum = jnp.sum(after(down, mixed).astype(f32), axis=0)
     output = (valid * (middle + down_sum)).astype(bf16)

time: 355 us -> 354 us (level)
    pallas_call x13 -> x14, Pallas kernels: 96.2 us -> 98.9 us  [call(): pl.pallas_call(kernel, out_shape=outs, scratch_shapes=list(scratch), comp...]
  transfers between devices with their start and end apart: 34 -> 34, of which waited for: 20 -> 20; matrix products, arithmetic and copies ran while one was open for 7% -> 7% of each run, Pallas kernels for 23% -> 24%
where the time goes in v5:
time: 354 us; the launch traced here: 348 us
  waiting for transfers between devices  145 us (41%)
  Pallas kernels  98.9 us (28%)
  starting transfers between devices  51.2 us (14%)
  local copies, waits for them, and re-layouts  17 us (5%)
  between operations  15.4 us (4%)
  other arithmetic  10.6 us (3%)
  matrix products  10 us (3%)
    ppermute x26, waiting for transfers between devices, swap(): return lax.ppermute(value, axis, [(j, j ^ bit) for j in range(n)])  138 us
    pallas_call x14, Pallas kernels, call(): pl.pallas_call(kernel, out_shape=outs, scratch_shapes=list(scratch), comp...  98.9 us
    ppermute x26, starting transfers between devices, swap(): return lax.ppermute(value, axis, [(j, j ^ bit) for j in range(n)])  37.2 us
    dot_general x4, matrix products, mm_tn(): lax.dot_general(left, right, (((0,), (0,)), ((), ())), preferred_element_...  10 us
    unnamed x90, local copies, waits for them, and re-layouts  7.38 us
  transfers between devices with their start and end apart: 34, of which 20 were waited for; matrix products, arithmetic and copies ran while one was open for 7% of the time, Pallas kernels for 24%

profile of v5, /device:TPU:0, one launch (start us, length us, event | category | flops | bytes accessed | tf_op | source)
XLA Modules:
  0.0 348.2 jit_solution(4157096921856935836)
XLA Ops:
  12.7 4.1 %collective-permute-start.1 = (bf16[128,1536]{1,0:T(8,128)(2,1)S(1)}, bf16[128,1536]{1,0:T(8,128)(2,1)S(1)}, u32[]{:S(2)}, u32[]{:S(2)}) collective-permute-start(bf16[128,1536]{1,0:T(8,128)(2,1)S(1)} %bitcast.37), channel_id=1, source_target_pairs={{0,2},{1,3},{2,0},{3,1},{4,6},{5,7},{6,4},{7,5},{8,10},{9,11},{10,... | collective-permute-start | bytes 1179656 | tf_op jit(solution)/shard_map/ppermute | solution.py:63
  19.0 15.4 %collective-permute-done.1.refs_2_ = bf16[128,1536]{1,0:T(8,128)(2,1)S(1)} collective-permute-done((bf16[128,1536]{1,0:T(8,128)(2,1)S(1)}, bf16[128,1536]{1,0:T(8,128)(2,1)S(1)}, u32[]{:S(2)}, u32[]{:S(2)}) %collective-permute-start.1) | collective-permute-done | bytes 393248 | tf_op jit(solution)/shard_map/ppermute | solution.py:63
  35.2 9.5 %collective-permute-done.2.refs_3_ = bf16[128,1536]{1,0:T(8,128)(2,1)S(1)} collective-permute-done((bf16[128,1536]{1,0:T(8,128)(2,1)S(1)}, bf16[128,1536]{1,0:T(8,128)(2,1)S(1)}, u32[]{:S(2)}, u32[]{:S(2)}) %collective-permute-start.2) | collective-permute-done | bytes 393248 | tf_op jit(solution)/shard_map/ppermute | solution.py:63
  46.0 5.5 %all-to-all-start = ((bf16[4,128,1536]{2,1,0:T(8,128)(2,1)}), bf16[4,128,1536]{2,1,0:T(8,128)(2,1)S(1)}, u32[]{:S(2)}, u32[]{:S(2)}) async-start(bf16[4,128,1536]{2,1,0:T(8,128)(2,1)} %broadcast_in_dim.38), calls=%async_computation | async-start | bytes 3145728 | tf_op jit(solution)/shard_map/all_to_all | solution.py:77
  59.6 10.8 %shard_map.221 = (bf16[512,768]{1,0:T(8,128)(2,1)}, bf16[512,768]{1,0:T(8,128)(2,1)}, bf16[512,768]{1,0:T(8,128)(2,1)}, bf16[512,896]{1,0:T(8,128)(2,1)}, f32[51...) custom-call(bf16[512,1536]{1,0:T(8,128)(2,1)} %shard_map.220.refs_0_.nor, ...), custom_call_target="tpu_custom_call" | custom-call | flops 100000000 | bytes 100000 | tf_op jit(solution)/shard_map/pallas_call | solution.py:47
  75.9 9.3 %shard_map.222 = (bf16[512,384]{1,0:T(8,128)(2,1)}, f32[512,384]{1,0:T(8,128)}, f32[512,128]{1,0:T(8,128)}, bf16[512,768]{1,0:T(8,128)(2,1)}, bf16[512,768]{1,0:...) custom-call(bf16[512,768]{1,0:T(8,128)(2,1)} %get-tuple-element.95.q, ...), custom_call_target="tpu_custom_call" | custom-call | flops 100000000 | bytes 100000 | tf_op jit(solution)/shard_map/pallas_call | solution.py:47
  89.9 10.2 %collective-permute-done.5 = bf16[128,1536]{1,0:T(8,128)(2,1)S(1)} collective-permute-done((bf16[128,1536]{1,0:T(8,128)(2,1)}, bf16[128,1536]{1,0:T(8,128)(2,1)S(1)}, u32[]{:S(2)}, u32[]{:S(2)}) %collective-permute-start.5) | collective-permute-done | bytes 393248 | tf_op jit(solution)/shard_map/ppermute | solution.py:63
  101.9 10.3 %collective-permute-done.4.refs_1_ = bf16[128,1536]{1,0:T(8,128)(2,1)S(1)} collective-permute-done((bf16[128,1536]{1,0:T(8,128)(2,1)}, bf16[128,1536]{1,0:T(8,128)(2,1)S(1)}, u32[]{:S(2)}, u32[]{:S(2)}) %collective-permute-start.4) | collective-permute-done | bytes 393248 | tf_op jit(solution)/shard_map/ppermute | solution.py:63
  112.2 6.2 %collective-permute-done.6.refs_2_ = bf16[128,1536]{1,0:T(8,128)(2,1)S(1)} collective-permute-done((bf16[128,1536]{1,0:T(8,128)(2,1)S(1)}, bf16[128,1536]{1,0:T(8,128)(2,1)S(1)}, u32[]{:S(2)}, u32[]{:S(2)}) %collective-permute-start.6) | collective-permute-done | bytes 393248 | tf_op jit(solution)/shard_map/ppermute | solution.py:63
  124.4 11.6 %collective-permute-done.8.refs_2_ = bf16[128,1536]{1,0:T(8,128)(2,1)S(1)} collective-permute-done((bf16[128,1536]{1,0:T(8,128)(2,1)}, bf16[128,1536]{1,0:T(8,128)(2,1)S(1)}, u32[]{:S(2)}, u32[]{:S(2)}) %collective-permute-start.8) | collective-permute-done | bytes 393248 | tf_op jit(solution)/shard_map/ppermute | solution.py:63
  136.4 6.3 %shard_map.224 = (f32[512,1024]{1,0:T(8,128)}, bf16[512,1536]{1,0:T(8,128)(2,1)}, bf16[1536,512]{1,0:T(8,128)(2,1)}) custom-call(bf16[4,128,1536]{2,1,0:T(8,128)(2,1)} %copy-done.1, bf16[512,1536]{1,0:T(8,128)(2,1)} %shard_map.220.refs_0_.normed_ref, bf16[1536,3072]{1,0:T(8,128)(2,1)} %all-gather.5.cloned.1.call-done.wd_ref.refs_5_.refs_6_), custom_call_target="tpu_custom_call" | custom-call | flops 100000000 | bytes 100000 | tf_op jit(solution)/shard_map/pallas_call | solution.py:47
  145.2 14.1 %shard_map.225 = (bf16[512,1536]{1,0:T(8,128)(2,1)}, bf16[512,1024]{1,0:T(8,128)(2,1)}, bf16[512,2048]{1,0:T(8,128)(2,1)}, bf16[128,1536]{1,0:T(8,128)(2,1)}, bf...) custom-call(bf16[128,1536]{1,0:T(8,128)(2,1)} %get-tuple-element.113.refs_0_, ...), custom_call_target="tpu_custom_call" | custom-call | flops 100000000 | bytes 100000 | tf_op jit(solution)/shard_map/pallas_call | solution.py:47
  164.4 3.7 %convolution_convert_fusion = bf16[1536,2048]{1,0:T(8,128)(2,1)S(1)} fusion(bf16[512,1536]{1,0:T(8,128)(2,1)S(1)} %copy-done.34, bf16[512,2048]{1,0:T(8,128)(2,1)S(1)} %copy-done.32), kind=kOutput, calls=%fused_computation.1 | convolution fusion | flops 3224371200 | bytes 9961472 | tf_op jit(solution)/shard_map/dot_general | solution.py:27
  168.1 4.5 %pad_maximum_fusion = bf16[1536,3072]{1,0:T(8,128)(2,1)} fusion(bf16[1536,1024]{1,0:T(8,128)(2,1)S(1)} %convolution_convert_fusion.1, bf16[1536,2048]{1,0:T(8,128)(2,1)S(1)} %convolution_convert_fusion), kind=kLoop, calls=%fused_computation | loop fusion | flops 18874368 | bytes 18874368 | tf_op jit(solution)/shard_map/concatenate | solution.py:568
  174.0 8.3 %collective-permute-done.11 = bf16[128,1536]{1,0:T(8,128)(2,1)S(1)} collective-permute-done((bf16[128,1536]{1,0:T(8,128)(2,1)S(1)}, bf16[128,1536]{1,0:T(8,128)(2,1)S(1)}, u32[]{:S(2)}, u32[]{:S(2)}) %collective-permute-start.11) | collective-permute-done | bytes 393248 | tf_op jit(solution)/shard_map/ppermute | solution.py:63
  185.7 13.9 %collective-permute-done.12.refs_2_ = bf16[128,1536]{1,0:T(8,128)(2,1)S(1)} collective-permute-done((bf16[128,1536]{1,0:T(8,128)(2,1)S(1)}, bf16[128,1536]{1,0:T(8,128)(2,1)S(1)}, u32[]{:S(2)}, u32[]{:S(2)}) %collective-permute-start.12) | collective-permute-done | bytes 393248 | tf_op jit(solution)/shard_map/ppermute | solution.py:63
  203.5 3.6 %collective-permute-start.13 = (bf16[128,1536]{1,0:T(8,128)(2,1)}, bf16[128,1536]{1,0:T(8,128)(2,1)S(1)}, u32[]{:S(2)}, u32[]{:S(2)}) collective-permute-start(bf16[128,1536]{1,0:T(8,128)(2,1)} %get-tuple-element.134.refs_0_), channel_id=1, source_target_pairs={{0,1},{1,0},{2,3},{3,2},{4,5},{5,4},{6,7},{7,6},{8,9},{9,8},{10,11... | collective-permute-start | bytes 1179656 | tf_op jit(solution)/shard_map/ppermute | solution.py:63
  207.1 15.6 %collective-permute-done.14.refs_2_ = bf16[128,1536]{1,0:T(8,128)(2,1)S(1)} collective-permute-done((bf16[128,1536]{1,0:T(8,128)(2,1)}, bf16[128,1536]{1,0:T(8,128)(2,1)S(1)}, u32[]{:S(2)}, u32[]{:S(2)}) %collective-permute-start.14) | collective-permute-done | bytes 393248 | tf_op jit(solution)/shard_map/ppermute | solution.py:63
  222.7 5.5 %shard_map.227 = bf16[4,128,1536]{2,1,0:T(8,128)(2,1)} custom-call(bf16[512,1024]{1,0:T(8,128)(2,1)} %get-tuple-element.130.hid_ref, bf16[1536,3072]{1,0:T(8,128)(2,1)} %all-gather.5.cloned.1.call-done.wd_ref.refs_5_.refs_6_), custom_call_target="tpu_custom_call" | custom-call | flops 100000000 | bytes 100000 | tf_op jit(solution)/shard_map/pallas_call | solution.py:47
  228.9 3.3 collective-permute-done.15.refs_3_
  232.2 4.1 %all-to-all-start.1 = ((bf16[4,128,1536]{2,1,0:T(8,128)(2,1)}), bf16[4,128,1536]{2,1,0:T(8,128)(2,1)S(1)}, u32[]{:S(2)}, u32[]{:S(2)}) async-start(bf16[4,128,1536]{2,1,0:T(8,128)(2,1)} %shard_map.227), calls=%async_computation.1 | async-start | bytes 3145728 | tf_op jit(solution)/shard_map/all_to_all | solution.py:81
  236.4 15.8 %shard_map.228 = (bf16[512,1536]{1,0:T(8,128)(2,1)}, f32[512,384]{1,0:T(8,128)}, f32[512,384]{1,0:T(8,128)}, f32[512,384]{1,0:T(8,128)}, bf16[512,896]{1,0:T(8,1...) custom-call(bf16[128,1536]{1,0:T(8,128)(2,1)} %get-tuple-element.134.refs_0_, bf16[128,1536]{1,0:T(8,128)(2,1)} %copy-done.39, ...), custom_call_target="tpu_custom_call" | custom-call | flops 99999997952 | bytes 100000000 | tf_op jit(solution)/shard_map/pallas_call | solution.py:47
  258.6 11.9 %shard_map.229 = (bf16[512,1664]{1,0:T(8,128)(2,1)}, bf16[144,1536]{1,0:T(8,128)(2,1)}, bf16[144,1536]{1,0:T(8,128)(2,1)}, bf16[144,1536]{1,0:T(8,128)(2,1)}, bf16[144,1536]{1,0:T(8,128)(2,1)}) custom-call(bf16[512,1536]{1,0:T(8,128)(2,1)} %shard_map.220.refs_0_.normed_ref, f32[1,1536]{1,0:T(1,128)} %broadcast_in_dim.33.gain_ref.refs_1_, ...), custom_call_target="tpu_custom_call" | custom-call | flops 100000000 | bytes 100000 | tf_op jit(solution)/shard_map/pallas_call | solution.py:47
  270.5 4.6 %shard_map.230 = bf16[4,192,1280]{2,1,0:T(8,128)(2,1)} custom-call(bf16[8,192,512]{2,1,0:T(8,128)(2,1)} %bitcast.32, bf16[512,1664]{1,0:T(8,128)(2,1)} %get-tuple-element.151.d_ref), custom_call_target="tpu_custom_call" | custom-call | flops 100000000 | bytes 100000 | tf_op jit(solution)/shard_map/pallas_call | solution.py:47
  280.4 10.7 %collective-permute-done.19 = bf16[144,1536]{1,0:T(8,128)(2,1)S(1)} collective-permute-done((bf16[144,1536]{1,0:T(8,128)(2,1)S(1)}, bf16[144,1536]{1,0:T(8,128)(2,1)S(1)}, u32[]{:S(2)}, u32[]{:S(2)}) %collective-permute-start.19) | collective-permute-done | bytes 442400 | tf_op jit(solution)/shard_map/ppermute | solution.py:63
  291.3 3.2 collective-permute-start.20
  294.5 4.5 %shard_map.231 = (f32[192,1280]{1,0:T(8,128)}, bf16[192,1280]{1,0:T(8,128)(2,1)}, bf16[192,1280]{1,0:T(8,128)(2,1)}, bf16[192,1280]{1,0:T(8,128)(2,1)}) custom-call(bf16[8,192,512]{2,1,0:T(8,128)(2,1)} %bitcast.33, bf16[512,1664]{1,0:T(8,128)(2,1)} %get-tuple-element.151.d_ref, bf16[4,192,1280]{2,1,0:T(8,128)(2,1)} %collective-permute-done.17.got_ref), custom_call_target="tpu_custom_call" | custom-call | flops 100000000 | bytes 100000 | tf_op jit(solution)/shard_map/pallas_call | solution.py:47
  304.0 4.4 %collective-permute-done.18.refs_1_ = bf16[144,1536]{1,0:T(8,128)(2,1)S(1)} collective-permute-done((bf16[144,1536]{1,0:T(8,128)(2,1)S(1)}, bf16[144,1536]{1,0:T(8,128)(2,1)S(1)}, u32[]{:S(2)}, u32[]{:S(2)}) %collective-permute-start.18) | collective-permute-done | bytes 442400 | tf_op jit(solution)/shard_map/ppermute | solution.py:63
  308.3 6.2 %collective-permute-done.20.refs_2_ = bf16[144,1536]{1,0:T(8,128)(2,1)S(1)} collective-permute-done((bf16[144,1536]{1,0:T(8,128)(2,1)S(1)}, bf16[144,1536]{1,0:T(8,128)(2,1)S(1)}, u32[]{:S(2)}, u32[]{:S(2)}) %collective-permute-start.20) | collective-permute-done | bytes 442400 | tf_op jit(solution)/shard_map/ppermute | solution.py:63
  316.7 4.0 %collective-permute-start.27 = (f32[3224]{0:T(1024)S(1)}, f32[3224]{0:T(1024)S(1)}, u32[]{:S(2)}, u32[]{:S(2)}) collective-permute-start(f32[3224]{0:T(1024)S(1)} %add.94), channel_id=1, source_target_pairs={{0,24},{8,16},{16,8},{24,0},{1,25},{9,17},{17,9},{25,1},{2,26},{10... | collective-permute-start | bytes 38696 | tf_op jit(solution)/shard_map/ppermute | solution.py:63
  320.7 6.7 %collective-permute-done.27 = f32[3224]{0:T(1024)S(1)} collective-permute-done((f32[3224]{0:T(1024)S(1)}, f32[3224]{0:T(1024)S(1)}, u32[]{:S(2)}, u32[]{:S(2)}) %collective-permute-start.27) | collective-permute-done | bytes 12928 | tf_op jit(solution)/shard_map/ppermute | solution.py:63
  334.2 5.3 %shard_map.232 = (bf16[128,1536]{1,0:T(8,128)(2,1)}, f32[192,2,1024]{2,1,0:T(2,128)}, f32[192,1024]{1,0:T(8,128)}, f32[3,192,384]{2,1,0:T(8,128)}, f32[6,192]{1,0:T(8,128)}) custom-call(bf16[128,1536]{1,0:T(8,128)(2,1)} %bitcast.36, f32[128,1536]{1,0:T(8,128)} %get-tuple-element.153.dmid_ref, f32[1,1536]{1,0:T(1,128)} %broadcast_in_dim.33.gain_ref.refs_1_, ...), custom_call_target="tpu_custom_call" | custom-call | flops 100000000 | bytes 100000 | tf_op jit(solution)/shard_map/pallas_call | solution.py:47
  (182 shorter events, 79.8 us)
Async XLA Ops:
  7.2 52.4 %all-gather.3.cloned.1.call-start = ((), (), s32[]{:S(2)}) async-start(), calls=%async_computation.4 | async-start | bytes 7077888 | tf_op jit(solution)/shard_map/all_gather | solution.py:496
  11.2 125.1 %all-gather.5.cloned.1.call-start = ((), (), s32[]{:S(2)}) async-start(), calls=%async_computation.5 | async-start | bytes 10616832 | tf_op jit(solution)/shard_map/all_gather | solution.py:498
  12.7 21.7 %collective-permute-start.1 = (bf16[128,1536]{1,0:T(8,128)(2,1)S(1)}, bf16[128,1536]{1,0:T(8,128)(2,1)S(1)}, u32[]{:S(2)}, u32[]{:S(2)}) collective-permute-start(bf16[128,1536]{1,0:T(8,128)(2,1)S(1)} %bitcast.37), channel_id=1, source_target_pairs={{0,2},{1,3},{2,0},{3,1},{4,6},{5,7},{6,4},{7,5},{8,10},{9,11},{10,... | collective-permute-start | bytes 1179656 | tf_op jit(solution)/shard_map/ppermute | solution.py:63
  16.8 18.4 %collective-permute-start = (bf16[128,1536]{1,0:T(8,128)(2,1)S(1)}, bf16[128,1536]{1,0:T(8,128)(2,1)S(1)}, u32[]{:S(2)}, u32[]{:S(2)}) collective-permute-start(bf16[128,1536]{1,0:T(8,128)(2,1)S(1)} %bitcast.38), channel_id=1, source_target_pairs={{0,1},{1,0},{2,3},{3,2},{4,5},{5,4},{6,7},{7,6},{8,9},{9,8},{10,11... | collective-permute-start | bytes 1179656 | tf_op jit(solution)/shard_map/ppermute | solution.py:63
  34.4 10.2 %collective-permute-start.2 = (bf16[128,1536]{1,0:T(8,128)(2,1)S(1)}, bf16[128,1536]{1,0:T(8,128)(2,1)S(1)}, u32[]{:S(2)}, u32[]{:S(2)}) collective-permute-start(bf16[128,1536]{1,0:T(8,128)(2,1)S(1)} %collective-permute-done.1.refs_2_), channel_id=1, source_target_pairs={{0,1},{1,0},{2,3},{3,2},{4,5},{5,4},{6,7},{7,6},{8,9},{9,8},{10,11... | collective-permute-start | bytes 1179656 | tf_op jit(solution)/shard_map/ppermute | solution.py:63
  46.0 41.9 %all-to-all-start = ((bf16[4,128,1536]{2,1,0:T(8,128)(2,1)}), bf16[4,128,1536]{2,1,0:T(8,128)(2,1)S(1)}, u32[]{:S(2)}, u32[]{:S(2)}) async-start(bf16[4,128,1536]{2,1,0:T(8,128)(2,1)} %broadcast_in_dim.38), calls=%async_computation | async-start | bytes 3145728 | tf_op jit(solution)/shard_map/all_to_all | solution.py:77
  51.5 207.1 %reduce-scatter.3.cloned.1.call-start = ((), (), s32[]{:S(2)}) async-start(), calls=%async_computation.6 | async-start | bytes 10616832 | tf_op jit(solution)/shard_map/reduce_scatter | solution.py:569
  70.4 4.5 %collective-permute-start.3 = (bf16[512,896]{1,0:T(8,128)(2,1)}, bf16[512,896]{1,0:T(8,128)(2,1)S(1)}, u32[]{:S(2)}, u32[]{:S(2)}) collective-permute-start(bf16[512,896]{1,0:T(8,128)(2,1)} %get-tuple-element.98), channel_id=1, source_target_pairs={{0,4},{1,5},{2,6},{3,7},{8,12},{9,13},{10,14},{11,15},{16,20},{17,... | collective-permute-start | bytes 2752520 | tf_op jit(solution)/shard_map/ppermute | solution.py:525
  87.9 12.3 %collective-permute-start.5 = (bf16[128,1536]{1,0:T(8,128)(2,1)}, bf16[128,1536]{1,0:T(8,128)(2,1)S(1)}, u32[]{:S(2)}, u32[]{:S(2)}) collective-permute-start(bf16[128,1536]{1,0:T(8,128)(2,1)} %get-tuple-element.108), channel_id=1, source_target_pairs={{0,1},{1,0},{2,3},{3,2},{4,5},{5,4},{6,7},{7,6},{8,9},{9,8},{10,11... | collective-permute-start | bytes 1179656 | tf_op jit(solution)/shard_map/ppermute | solution.py:63
  87.9 24.3 %collective-permute-start.4 = (bf16[128,1536]{1,0:T(8,128)(2,1)}, bf16[128,1536]{1,0:T(8,128)(2,1)S(1)}, u32[]{:S(2)}, u32[]{:S(2)}) collective-permute-start(bf16[128,1536]{1,0:T(8,128)(2,1)} %get-tuple-element.106), channel_id=1, source_target_pairs={{0,1},{1,0},{2,3},{3,2},{4,5},{5,4},{6,7},{7,6},{8,9},{9,8},{10,11... | collective-permute-start | bytes 1179656 | tf_op jit(solution)/shard_map/ppermute | solution.py:63
  101.3 17.2 %collective-permute-start.6 = (bf16[128,1536]{1,0:T(8,128)(2,1)S(1)}, bf16[128,1536]{1,0:T(8,128)(2,1)S(1)}, u32[]{:S(2)}, u32[]{:S(2)}) collective-permute-start(bf16[128,1536]{1,0:T(8,128)(2,1)S(1)} %add_convert_fusion.2), channel_id=1, source_target_pairs={{0,2},{1,3},{2,0},{3,1},{4,6},{5,7},{6,4},{7,5},{8,10},{9,11},{10,... | collective-permute-start | bytes 1179656 | tf_op jit(solution)/shard_map/ppermute | solution.py:63
  121.8 14.2 %collective-permute-start.8 = (bf16[128,1536]{1,0:T(8,128)(2,1)}, bf16[128,1536]{1,0:T(8,128)(2,1)S(1)}, u32[]{:S(2)}, u32[]{:S(2)}) collective-permute-start(bf16[128,1536]{1,0:T(8,128)(2,1)} %get-tuple-element.113.refs_0_), channel_id=1, source_target_pairs={{0,2},{1,3},{2,0},{3,1},{4,6},{5,7},{6,4},{7,5},{8,10},{9,11},{10,... | collective-permute-start | bytes 1179656 | tf_op jit(solution)/shard_map/ppermute | solution.py:63
  121.8 20.9 %collective-permute-start.7 = (bf16[128,1536]{1,0:T(8,128)(2,1)}, bf16[128,1536]{1,0:T(8,128)(2,1)S(1)}, u32[]{:S(2)}, u32[]{:S(2)}) collective-permute-start(bf16[128,1536]{1,0:T(8,128)(2,1)} %get-tuple-element.113.refs_0_), channel_id=1, source_target_pairs={{0,1},{1,0},{2,3},{3,2},{4,5},{5,4},{6,7},{7,6},{8,9},{9,8},{10,11... | collective-permute-start | bytes 1179656 | tf_op jit(solution)/shard_map/ppermute | solution.py:63
  136.0 8.4 %collective-permute-start.9 = (bf16[128,1536]{1,0:T(8,128)(2,1)S(1)}, bf16[128,1536]{1,0:T(8,128)(2,1)S(1)}, u32[]{:S(2)}, u32[]{:S(2)}) collective-permute-start(bf16[128,1536]{1,0:T(8,128)(2,1)S(1)} %collective-permute-done.8.refs_2_), channel_id=1, source_target_pairs={{0,1},{1,0},{2,3},{3,2},{4,5},{5,4},{6,7},{7,6},{8,9},{9,8},{10,11... | collective-permute-start | bytes 1179656 | tf_op jit(solution)/shard_map/ppermute | solution.py:63
  162.5 10.1 %collective-permute-start.10 = (bf16[128,1536]{1,0:T(8,128)(2,1)S(1)}, bf16[128,1536]{1,0:T(8,128)(2,1)S(1)}, u32[]{:S(2)}, u32[]{:S(2)}) collective-permute-start(bf16[128,1536]{1,0:T(8,128)(2,1)S(1)} %copy-done.41), channel_id=1, source_target_pairs={{0,1},{1,0},{2,3},{3,2},{4,5},{5,4},{6,7},{7,6},{8,9},{9,8},{10,11... | collective-permute-start | bytes 1179656 | tf_op jit(solution)/shard_map/ppermute | solution.py:63
  173.8 8.6 %collective-permute-start.11 = (bf16[128,1536]{1,0:T(8,128)(2,1)S(1)}, bf16[128,1536]{1,0:T(8,128)(2,1)S(1)}, u32[]{:S(2)}, u32[]{:S(2)}) collective-permute-start(bf16[128,1536]{1,0:T(8,128)(2,1)S(1)} %copy-done.40), channel_id=1, source_target_pairs={{0,1},{1,0},{2,3},{3,2},{4,5},{5,4},{6,7},{7,6},{8,9},{9,8},{10,11... | collective-permute-start | bytes 1179656 | tf_op jit(solution)/shard_map/ppermute | solution.py:63
  182.5 17.1 %collective-permute-start.12 = (bf16[128,1536]{1,0:T(8,128)(2,1)S(1)}, bf16[128,1536]{1,0:T(8,128)(2,1)S(1)}, u32[]{:S(2)}, u32[]{:S(2)}) collective-permute-start(bf16[128,1536]{1,0:T(8,128)(2,1)S(1)} %add_convert_fusion.1), channel_id=1, source_target_pairs={{0,2},{1,3},{2,0},{3,1},{4,6},{5,7},{6,4},{7,5},{8,10},{9,11},{10,... | collective-permute-start | bytes 1179656 | tf_op jit(solution)/shard_map/ppermute | solution.py:63
  203.5 19.2 %collective-permute-start.14 = (bf16[128,1536]{1,0:T(8,128)(2,1)}, bf16[128,1536]{1,0:T(8,128)(2,1)S(1)}, u32[]{:S(2)}, u32[]{:S(2)}) collective-permute-start(bf16[128,1536]{1,0:T(8,128)(2,1)} %get-tuple-element.134.refs_0_), channel_id=1, source_target_pairs={{0,2},{1,3},{2,0},{3,1},{4,6},{5,7},{6,4},{7,5},{8,10},{9,11},{10,... | collective-permute-start | bytes 1179656 | tf_op jit(solution)/shard_map/ppermute | solution.py:63
  203.5 24.6 %collective-permute-start.13 = (bf16[128,1536]{1,0:T(8,128)(2,1)}, bf16[128,1536]{1,0:T(8,128)(2,1)S(1)}, u32[]{:S(2)}, u32[]{:S(2)}) collective-permute-start(bf16[128,1536]{1,0:T(8,128)(2,1)} %get-tuple-element.134.refs_0_), channel_id=1, source_target_pairs={{0,1},{1,0},{2,3},{3,2},{4,5},{5,4},{6,7},{7,6},{8,9},{9,8},{10,11... | collective-permute-start | bytes 1179656 | tf_op jit(solution)/shard_map/ppermute | solution.py:63
  222.7 9.5 %collective-permute-start.15 = (bf16[128,1536]{1,0:T(8,128)(2,1)S(1)}, bf16[128,1536]{1,0:T(8,128)(2,1)}, u32[]{:S(2)}, u32[]{:S(2)}) collective-permute-start(bf16[128,1536]{1,0:T(8,128)(2,1)S(1)} %collective-permute-done.14.refs_2_), channel_id=1, source_target_pairs={{0,1},{1,0},{2,3},{3,2},{4,5},{5,4},{6,7},{7,6},{8,9},{9,8},{10,11... | collective-permute-start | bytes 1179656 | tf_op jit(solution)/shard_map/ppermute | solution.py:63
  232.2 45.1 %all-to-all-start.1 = ((bf16[4,128,1536]{2,1,0:T(8,128)(2,1)}), bf16[4,128,1536]{2,1,0:T(8,128)(2,1)S(1)}, u32[]{:S(2)}, u32[]{:S(2)}) async-start(bf16[4,128,1536]{2,1,0:T(8,128)(2,1)} %shard_map.227), calls=%async_computation.1 | async-start | bytes 3145728 | tf_op jit(solution)/shard_map/all_to_all | solution.py:81
  236.2 103.2 %reduce-scatter.5.cloned.1.call-start = ((), (), s32[]{:S(2)}) async-start(), calls=%async_computation.7 | async-start | bytes 2654208 | tf_op jit(solution)/shard_map/reduce_scatter | solution.py:607
  252.3 6.4 %collective-permute-start.16 = (bf16[512,896]{1,0:T(8,128)(2,1)}, bf16[512,896]{1,0:T(8,128)(2,1)}, u32[]{:S(2)}, u32[]{:S(2)}) collective-permute-start(bf16[512,896]{1,0:T(8,128)(2,1)} %get-tuple-element.146), channel_id=1, source_target_pairs={{4,0},{5,1},{6,2},{7,3},{12,8},{13,9},{14,10},{15,11},{20,16},{21,... | collective-permute-start | bytes 2752520 | tf_op jit(solution)/shard_map/ppermute | solution.py:598
  275.1 19.3 %collective-permute-start.17 = (bf16[4,192,1280]{2,1,0:T(8,128)(2,1)}, bf16[4,192,1280]{2,1,0:T(8,128)(2,1)}, u32[]{:S(2)}, u32[]{:S(2)}) collective-permute-start(bf16[4,192,1280]{2,1,0:T(8,128)(2,1)} %shard_map.230), channel_id=1, source_target_pairs={{0,4},{4,0},{1,5},{5,1},{2,6},{6,2},{3,7},{7,3},{8,12},{12,8},{9,1... | collective-permute-start | bytes 5898248 | tf_op jit(solution)/shard_map/ppermute | solution.py:63
  278.3 12.8 %collective-permute-start.19 = (bf16[144,1536]{1,0:T(8,128)(2,1)S(1)}, bf16[144,1536]{1,0:T(8,128)(2,1)S(1)}, u32[]{:S(2)}, u32[]{:S(2)}) collective-permute-start(bf16[144,1536]{1,0:T(8,128)(2,1)S(1)} %copy-done.36), channel_id=1, source_target_pairs={{0,1},{1,0},{2,3},{3,2},{4,5},{5,4},{6,7},{7,6},{8,9},{9,8},{10,11... | collective-permute-start | bytes 1327112 | tf_op jit(solution)/shard_map/ppermute | solution.py:63
  280.4 27.9 %collective-permute-start.18 = (bf16[144,1536]{1,0:T(8,128)(2,1)S(1)}, bf16[144,1536]{1,0:T(8,128)(2,1)S(1)}, u32[]{:S(2)}, u32[]{:S(2)}) collective-permute-start(bf16[144,1536]{1,0:T(8,128)(2,1)S(1)} %copy-done.35), channel_id=1, source_target_pairs={{0,1},{1,0},{2,3},{3,2},{4,5},{5,4},{6,7},{7,6},{8,9},{9,8},{10,11... | collective-permute-start | bytes 1327112 | tf_op jit(solution)/shard_map/ppermute | solution.py:63
  291.3 23.3 %collective-permute-start.20 = (bf16[144,1536]{1,0:T(8,128)(2,1)S(1)}, bf16[144,1536]{1,0:T(8,128)(2,1)S(1)}, u32[]{:S(2)}, u32[]{:S(2)}) collective-permute-start(bf16[144,1536]{1,0:T(8,128)(2,1)S(1)} %add_convert_fusion), channel_id=1, source_target_pairs={{0,2},{1,3},{2,0},{3,1},{4,6},{5,7},{6,4},{7,5},{8,10},{9,11},{10,... | collective-permute-start | bytes 1327112 | tf_op jit(solution)/shard_map/ppermute | solution.py:63
  299.0 34.0 %collective-permute-start.21 = (bf16[192,1280]{1,0:T(8,128)(2,1)}, bf16[192,1280]{1,0:T(8,128)(2,1)S(1)}, u32[]{:S(2)}, u32[]{:S(2)}) collective-permute-start(bf16[192,1280]{1,0:T(8,128)(2,1)} %get-tuple-element.165), channel_id=1, source_target_pairs={{0,8},{8,0},{16,24},{24,16},{1,9},{9,1},{17,25},{25,17},{2,10},{10... | collective-permute-start | bytes 1474568 | tf_op jit(solution)/shard_map/ppermute | solution.py:63
  300.7 32.3 %collective-permute-start.22 = (bf16[192,1280]{1,0:T(8,128)(2,1)}, bf16[192,1280]{1,0:T(8,128)(2,1)S(1)}, u32[]{:S(2)}, u32[]{:S(2)}) collective-permute-start(bf16[192,1280]{1,0:T(8,128)(2,1)} %get-tuple-element.166), channel_id=1, source_target_pairs={{0,16},{8,24},{16,0},{24,8},{1,17},{9,25},{17,1},{25,9},{2,18},{10... | collective-permute-start | bytes 1474568 | tf_op jit(solution)/shard_map/ppermute | solution.py:63
  303.7 29.3 %collective-permute-start.23 = (bf16[192,1280]{1,0:T(8,128)(2,1)}, bf16[192,1280]{1,0:T(8,128)(2,1)S(1)}, u32[]{:S(2)}, u32[]{:S(2)}) collective-permute-start(bf16[192,1280]{1,0:T(8,128)(2,1)} %get-tuple-element.167), channel_id=1, source_target_pairs={{0,24},{8,16},{16,8},{24,0},{1,25},{9,17},{17,9},{25,1},{2,26},{10... | collective-permute-start | bytes 1474568 | tf_op jit(solution)/shard_map/ppermute | solution.py:63
  316.7 10.8 %collective-permute-start.27 = (f32[3224]{0:T(1024)S(1)}, f32[3224]{0:T(1024)S(1)}, u32[]{:S(2)}, u32[]{:S(2)}) collective-permute-start(f32[3224]{0:T(1024)S(1)} %add.94), channel_id=1, source_target_pairs={{0,24},{8,16},{16,8},{24,0},{1,25},{9,17},{17,9},{25,1},{2,26},{10... | collective-permute-start | bytes 38696 | tf_op jit(solution)/shard_map/ppermute | solution.py:63
  320.7 7.3 %collective-permute-start.26 = (f32[3224]{0:T(1024)S(1)}, f32[3224]{0:T(1024)S(1)}, u32[]{:S(2)}, u32[]{:S(2)}) collective-permute-start(f32[3224]{0:T(1024)S(1)} %add.94), channel_id=1, source_target_pairs={{0,16},{8,24},{16,0},{24,8},{1,17},{9,25},{17,1},{25,9},{2,18},{10... | collective-permute-start | bytes 38696 | tf_op jit(solution)/shard_map/ppermute | solution.py:63
  (46 other events, 355.7 us)
Sparse Core Ops, SparseCore 0:
  11.4 48.2 all-gather.2
  61.5 58.8 all-gather.4
  172.8 76.1 reduce-scatter.2
  258.8 50.3 reduce-scatter.4
